TPU v7x, 32 devices: a whole 2x2x4 slice. The times are simulated.
32 devices in a mesh: tm: 8 (over z, x), det: 4 (over y, core).
Axes of the slice: x: 2, y: 2, z: 4, core: 2. Of those that a mesh axis runs over, the one named last changes fastest.
Arguments:
- timestream: float32 [8, 128, 256], P('tm', 'det'), may hold values from -101 to 101
- tile_index: int32 [8, 128, 256], P('tm', 'det'), may hold values from 0 to 31, as said below
- pixel_index: int32 [8, 128, 256], P('tm', 'det'), may hold values from 0 to 32639
- angle_bin: int32 [8, 128, 256], P('tm', 'det'), may hold values from 0 to 1023
- owner_map: int32 [32], replicated, may hold values from 0 to 31, each once
Outputs:
- sky_map: float32 [3, 1044480], P(None, ('tm', 'det'))
- residual: float32 [8, 128, 256], P('tm', 'det')
Inputs may be any that keep to these rules, and one draw needn't show every extreme that they name: `tile_index`: among the samples of one device, no tile occurs more than 512 times.
All inputs are finite; a program needn't handle non-finite values.
Results may differ from a plain program's by a relative error of at most 0.00013.
Values sent between devices are 32-bit elements; how exact they have to be, the bound alone decides.
No kernel may reach another device: no remote copies, remote signals or barrier semaphores. Data moves between devices by JAX's collectives and lax.ppermute only.
A program may use at most 320 MiB of HBM per device.

v0:
```python
import jax
import jax.numpy as jnp
from jax import lax
from jax.sharding import PartitionSpec as P

MODES = 16
NBINS = 1024
TILE_PIX = 32640


RIDGE = 1.0


def solve_stokes(sums):
    a11 = sums[0] + RIDGE
    a12 = sums[1]
    a13 = sums[2]
    a22 = sums[3] + RIDGE
    a23 = sums[4]
    a33 = sums[5] + RIDGE
    c11 = a22 * a33 - a23 * a23
    c12 = a13 * a23 - a12 * a33
    c13 = a12 * a23 - a13 * a22
    c22 = a11 * a33 - a13 * a13
    c23 = a12 * a13 - a11 * a23
    c33 = a11 * a22 - a12 * a12
    inverse = 1.0 / (a11 * c11 + a12 * c12 + a13 * c13)
    stokes_i = (c11 * sums[6] + c12 * sums[7] + c13 * sums[8]) * inverse
    stokes_q = (c12 * sums[6] + c22 * sums[7] + c23 * sums[8]) * inverse
    stokes_u = (c13 * sums[6] + c23 * sums[7] + c33 * sums[8]) * inverse
    return (stokes_i, stokes_q, stokes_u)


def shards(timestream, tile_index, pixel_index, angle_bin, owner_map):
    blocks, det_local, sample_local = timestream.shape
    highest = lax.Precision.HIGHEST
    samples_in = timestream[0]
    members = det_local * lax.axis_size("det") // MODES
    group_partial = jnp.sum(samples_in.reshape(det_local // MODES, MODES, sample_local), axis=0)
    templates = lax.psum(group_partial, "det") / members
    mode_gram = jnp.dot(templates, templates.T, precision=highest)
    mode_proj = jnp.dot(samples_in, templates.T, precision=highest)
    mode_gram, mode_proj = lax.psum((mode_gram, mode_proj), "tm")
    factor = jnp.linalg.cholesky(mode_gram + RIDGE * jnp.eye(MODES, dtype=jnp.float32))
    mode_coef = jax.scipy.linalg.cho_solve((factor, True), mode_proj.T)
    cleaned = (samples_in - jnp.dot(mode_coef.T, templates, precision=highest)).reshape(-1)
    tm_count = lax.axis_size("tm")
    det_count = lax.axis_size("det")
    owners_all = tm_count * det_count
    flat_count = det_local * sample_local
    capacity = flat_count // (owners_all // 2)
    owner_of = jnp.take(owner_map, tile_index.reshape(-1))
    order = jnp.argsort(owner_of, stable=True)
    sorted_owner = owner_of[order]
    firsts = jnp.searchsorted(sorted_owner, jnp.arange(owners_all, dtype=jnp.int32))
    ranks = jnp.arange(flat_count, dtype=jnp.int32) - firsts[sorted_owner]
    slots = jnp.zeros((flat_count,), jnp.int32).at[order].set(sorted_owner * capacity + ranks)
    pol_angle = jnp.pi * angle_bin.reshape(-1).astype(jnp.float32) / NBINS
    cosine = jnp.cos(2.0 * pol_angle)
    sine = jnp.sin(2.0 * pol_angle)
    payload = jnp.stack([cleaned, cosine, sine])
    out_floats = jnp.zeros((3, owners_all * capacity), jnp.float32).at[:, slots].set(payload)
    out_floats = jnp.transpose(out_floats.reshape(3, owners_all, capacity), (1, 0, 2))
    out_pixels = (
        jnp.full((owners_all * capacity,), -1, jnp.int32).at[slots].set(pixel_index.reshape(-1))
    )
    float_in, pixel_got = (
        lax.all_to_all(out_floats, ("tm", "det"), split_axis=0, concat_axis=0, tiled=True),
        lax.all_to_all(
            out_pixels.reshape(owners_all, capacity),
            ("tm", "det"),
            split_axis=0,
            concat_axis=0,
            tiled=True,
        ),
    )
    float_in = jnp.transpose(float_in, (1, 0, 2)).reshape(3, -1)
    pixel_got = pixel_got.reshape(-1)
    live = pixel_got >= 0
    weight_one = live.astype(jnp.float32)
    pixel_in = jnp.maximum(pixel_got, 0).astype(jnp.int32)
    value_in = float_in[0] * weight_one
    cos_in = float_in[1] * weight_one
    sin_in = float_in[2] * weight_one
    contrib = jnp.stack(
        [
            weight_one,
            cos_in,
            sin_in,
            cos_in * cos_in,
            cos_in * sin_in,
            sin_in * sin_in,
            value_in,
            cos_in * value_in,
            sin_in * value_in,
        ]
    )
    sums = jnp.zeros((9, TILE_PIX), jnp.float32).at[:, pixel_in].add(contrib)
    stokes_i, stokes_q, stokes_u = solve_stokes(sums)
    predicted = (
        weight_one * stokes_i[pixel_in] + cos_in * stokes_q[pixel_in] + sin_in * stokes_u[pixel_in]
    )
    returned = lax.all_to_all(
        predicted.reshape(owners_all, capacity),
        ("tm", "det"),
        split_axis=0,
        concat_axis=0,
        tiled=True,
    ).reshape(-1)
    model_signal = returned[slots]
    residual = (cleaned - model_signal).reshape(blocks, det_local, sample_local)
    return (jnp.stack([stokes_i, stokes_q, stokes_u]), residual)


def solution(mesh):
    placed = (
        P("tm", "det", None),
        P("tm", "det", None),
        P("tm", "det", None),
        P("tm", "det", None),
        P(),
    )
    return jax.shard_map(
        shards,
        mesh=mesh,
        in_specs=placed,
        out_specs=(P(None, ("tm", "det")), P("tm", "det", None)),
        check_vma=False,
    )
```

profile of v0, /device:TPU:0, one launch (start us, length us, event | category | flops | bytes accessed | tf_op | source)
XLA Modules:
  0.0 955.4 jit_solution(4141736998711301936)
XLA Ops:
  0.6 1.8 fusion.43
  2.5 2.1 fusion.42
  4.6 0.8 copy.72
  5.4 0.8 copy.73
  6.2 4.5 compare_select_fusion.8
  10.6 2.5 compare_reduce_fusion.49
  13.1 15.8 %select_select_fusion = s32[8192]{0:T(1024)S(1)} fusion(pred[8192]{0:T(1024)(128)(4,1)S(1)} %get-tuple-element.146, pred[8192]{0:T(1024)(128)(4,1)S(1)} %get-tuple-element.145, pred[8192]{0:T(1024)(128)(4,1)S(1)} %get-tuple-element.144, pred[8192]{0:T(1024)(128)(4,1)S(1)} %get-tuple-element.143, pred[8192]{0:T(1024)(128)(4,1)S(1)} %get-tuple-element.142, ...), kind=kLoop, calls=%fused_computation.128 | loop fusion | flops 262144 | bytes 303204 | tf_op jit(solution)/shard_map/jit(_take)/select_n | solution.py:52
  28.9 6.8 sort.17
  35.8 45.5 %gather_fusion.1 = s32[8192]{0:T(1024)S(1)} fusion(s32[8192]{0:T(1024)S(1)} %select_select_fusion, s32[8192]{0:T(1024)S(1)} %get-tuple-element.197), kind=kCustom, calls=%fused_computation.1 | custom fusion | bytes 98304 | tf_op jit(solution)/shard_map/gather | solution.py:54
  81.3 10.5 %while.24 = (s32[]{:T(128)}, u32[32]{0:T(128)S(1)}, u32[32]{0:T(128)S(1)}, s32[8192]{0:T(1024)S(1)}, s32[]{:T(128)}, /*index=5*/s32[]{:T(128)}, s32[]{}) while((s32[]{:T(128)}, u32[32]{0:T(128)S(1)}, u32[32]{0:T(128)S(1)}, s32[8192]{0:T(1024)S(1)}, s32[]{:T(128)}, /*index=5*/s32[]{:T(128)}, s32[]{}) %tuple.180), condition=%wide.region_2.0_spmd.clone, body=%wide.region_1.0_spmd.clone.sunk | while | flops 1444 | bytes 5732 | solution.py:55
  92.6 0.7 fusion.40
  93.3 4.4 compare_select_fusion.2
  97.8 2.5 compare_reduce_fusion.24
  100.3 15.9 %fusion.13 = s32[8192]{0:T(1024)S(1)} fusion(pred[8192]{0:T(1024)(128)(4,1)S(1)} %get-tuple-element.121, pred[8192]{0:T(1024)(128)(4,1)S(1)} %get-tuple-element.120, pred[8192]{0:T(1024)(128)(4,1)S(1)} %get-tuple-element.119, pred[8192]{0:T(1024)(128)(4,1)S(1)} %get-tuple-element.118, pred[8192]{0:T(1024)(128)(4,1)S(1)} %get-tuple-element.117, ...), kind=kLoop, calls=%fused_computation.127 | loop fusion | flops 229376 | bytes 303204 | tf_op jit(solution)/shard_map/add | solution.py:57
  116.2 30.7 %scatter_custom_fusion = s32[8192]{0:T(1024)S(1)} fusion(s32[8192]{0:T(1024)S(1)} %get-tuple-element.198, s32[8192]{0:T(1024)S(1)} %fusion.13, s32[]{:T(128)} %constant.112.clone.1), kind=kCustom, calls=%fused_computation.140 | custom fusion | bytes 32772 | tf_op jit(solution)/shard_map/scatter | solution.py:57
  147.5 31.0 %scatter_custom_fusion.1 = s32[16384]{0:T(1024)} fusion(s32[8192]{0:T(1024)S(1)} %get-tuple-element.194, s32[8192]{0:T(1024)S(1)} %bitcast.176, s32[]{:T(128)} %constant.111.clone.1), kind=kCustom, calls=%fused_computation.136 | custom fusion | bytes 65540 | tf_op jit(solution)/shard_map/scatter | solution.py:65
  178.6 7.3 all-to-all-start
  185.9 11.8 %psum.21 = f32[16,256]{1,0:T(8,128)S(1)} all-reduce(f32[16,256]{1,0:T(8,128)S(1)} %reduce_sum.9), channel_id=1, replica_groups=mesh['tm'=8,'det'=4] {'det'}, use_global_device_ids=true, to_apply=%region_6.7 | all-reduce | flops 4096 | bytes 32768 | tf_op jit(solution)/shard_map/psum | solution.py:40
  198.0 36.8 %all-reduce = (f32[32,16]{0,1:T(8,128)S(1)}, f32[16,16]{1,0:T(8,128)S(1)}) all-reduce(f32[32,16]{0,1:T(8,128)S(1)} %convolution_bitcast_fusion, f32[16,16]{1,0:T(8,128)S(1)} %fusion.20), channel_id=1, replica_groups=mesh['tm'=8,'det'=4] {'tm'}, use_global_device_ids=true, to_apply=%region_10.11 | all-reduce | flops 768 | bytes 6144 | tf_op jit(solution)/shard_map/psum | solution.py:43
  234.9 1.5 cholesky.17
  237.7 1.2 custom-call.10
  239.9 2.7 copy.43
  242.5 24.5 %scatter_custom_fusion.2 = f32[3,16384]{0,1:T(8,128)} fusion(s32[8192]{0:T(1024)S(1)} %get-tuple-element.194, f32[8192,3]{1,0:T(8,128)} %copy.43, f32[]{:T(128)} %constant.110.clone.1), kind=kCustom, calls=%fused_computation.20 | custom fusion | bytes 197120 | tf_op jit(solution)/shard_map/scatter | solution.py:62
  267.1 5.9 copy.44
  273.0 2.6 all-to-all-start.1
  275.8 10.4 %all-to-all-done.1 = f32[32,3,512]{2,1,0:T(4,128)S(1)} async-done(((f32[32,3,512]{2,1,0:T(4,128)}), f32[32,3,512]{2,1,0:T(4,128)S(1)}, u32[]{:S(2)}, u32[]{:S(2)}) %all-to-all-start.1) | async-done | bytes 196640 | tf_op jit(solution)/shard_map/all_to_all | solution.py:68
  287.0 1.0 stack.7
  288.0 4.6 copy.46
  292.6 111.5 %scatter_custom_fusion.3 = f32[9,32640]{0,1:T(8,128)} fusion(s32[16384]{0:T(1024)S(1)} %bitcast.163, f32[16384,9]{1,0:T(8,128)} %copy.46, f32[]{:T(128)} %constant.110.clone.1), kind=kCustom, calls=%fused_computation.18 | custom fusion | flops 147456 | bytes 1175552 | tf_op jit(solution)/shard_map/scatter-add | solution.py:98
  404.2 119.3 %slice_reduce_fusion.5 = (f32[32640]{0:T(1024)S(1)}, f32[32640]{0:T(1024)S(1)}, f32[32640]{0:T(1024)S(1)}, f32[32640]{0:T(1024)S(1)}, f32[32640]{0:T(1024)S(1)},...) fusion(f32[9,32640]{0,1:T(8,128)} %scatter_custom_fusion.3), kind=kLoop, calls=%fused_computation.173 | loop fusion | bytes 3133440 | tf_op jit(solution)/shard_map/slice | solution.py:19
  523.5 9.1 copy.64
  532.7 9.1 copy.63
  541.8 9.1 copy.62
  550.9 9.1 copy.61
  560.1 9.1 copy.60
  569.2 9.1 copy.59
  578.4 9.1 copy.58
  587.5 9.1 copy.57
  596.7 9.1 copy.65
  605.8 0.8 add_multiply_fusion.5
  606.6 1.9 add_multiply_fusion.4
  608.8 90.5 %gather_fusion.2 = f32[16384]{0:T(1024)S(1)} fusion(f32[32640]{0:T(1024)S(1)} %get-tuple-element.179, s32[16384]{0:T(1024)S(1)} %broadcast_clamp_fusion), kind=kCustom, calls=%fused_computation.2 | custom fusion | bytes 196608 | tf_op jit(solution)/shard_map/gather | solution.py:101
  699.3 90.5 %gather_fusion.3 = f32[16384]{0:T(1024)S(1)} fusion(f32[32640]{0:T(1024)S(1)} %get-tuple-element.180, s32[16384]{0:T(1024)S(1)} %broadcast_clamp_fusion), kind=kCustom, calls=%fused_computation.3 | custom fusion | bytes 196608 | tf_op jit(solution)/shard_map/gather | solution.py:101
  789.9 90.5 %gather_fusion.4 = f32[16384]{0:T(1024)S(1)} fusion(f32[32640]{0:T(1024)S(1)} %get-tuple-element.181, s32[16384]{0:T(1024)S(1)} %broadcast_clamp_fusion), kind=kCustom, calls=%fused_computation.4 | custom fusion | bytes 196608 | tf_op jit(solution)/shard_map/gather | solution.py:101
  881.2 20.4 %all-to-all-start.2 = ((f32[32,1,512]{2,1,0:T(1,128)}), f32[32,1,512]{2,1,0:T(1,128)S(1)}, u32[]{:S(2)}, u32[]{:S(2)}) async-start(f32[32,1,512]{2,1,0:T(1,128)} %copy.56), calls=%async_computation.2 | async-start | bytes 131072 | tf_op jit(solution)/shard_map/all_to_all | solution.py:103
  901.6 1.1 pad_maximum_fusion
  902.8 6.3 all-to-all-done.2
  909.1 45.5 %gather_fusion.5 = f32[8192]{0:T(1024)S(1)} fusion(f32[16384]{0:T(1024)S(1)} %bitcast.150, s32[8192]{0:T(1024)S(1)} %copy-done.7), kind=kCustom, calls=%fused_computation.5 | custom fusion | bytes 98304 | tf_op jit(solution)/shard_map/gather | solution.py:110
  (124 shorter events, 16.8 us)
Async XLA Ops:
  35.7 57.6 %copy-start.9 = (s32[1,32,256]{2,1,0:T(8,128)S(1)}, s32[1,32,256]{2,1,0:T(8,128)}, u32[]{:S(2)}) copy-start(s32[1,32,256]{2,1,0:T(8,128)} %param.9) | copy-start | bytes 98308
  35.7 150.1 %copy-start.4 = (f32[1,32,256]{2,1,0:T(8,128)S(1)}, f32[1,32,256]{2,1,0:T(8,128)}, u32[]{:S(2)}) copy-start(f32[1,32,256]{2,1,0:T(8,128)} %param.7) | copy-start | bytes 98308
  35.8 203.8 %copy-start.8 = (s32[1,32,256]{2,1,0:T(8,128)S(1)}, s32[1,32,256]{2,1,0:T(8,128)}, u32[]{:S(2)}) copy-start(s32[1,32,256]{2,1,0:T(8,128)} %param.10) | copy-start | bytes 98308
  178.6 94.4 %all-to-all-start = ((s32[32,1,512]{2,1,0:T(1,128)}), s32[32,1,512]{2,1,0:T(1,128)S(1)}, u32[]{:S(2)}, u32[]{:S(2)}) async-start(s32[32,1,512]{2,1,0:T(1,128)} %bitcast.67), calls=%async_computation | async-start | bytes 131072 | tf_op jit(solution)/shard_map/all_to_all | solution.py:69
  239.5 53.2 %copy-start.5 = (f32[32,256]{1,0:T(8,128)}, f32[32,256]{1,0:T(8,128)S(1)}, u32[]{:S(2)}) copy-start(f32[32,256]{1,0:T(8,128)S(1)} %convolution_subtract_fusion) | copy-start | bytes 98308
  273.0 14.0 %copy-start.2 = (s32[32,1,512]{2,1,0:T(1,128)}, s32[32,1,512]{2,1,0:T(1,128)S(1)}, u32[]{:S(2)}) copy-start(s32[32,1,512]{2,1,0:T(1,128)S(1)} %all-to-all-done) | copy-start | bytes 196612
  273.0 13.2 %all-to-all-start.1 = ((f32[32,3,512]{2,1,0:T(4,128)}), f32[32,3,512]{2,1,0:T(4,128)S(1)}, u32[]{:S(2)}, u32[]{:S(2)}) async-start(f32[32,3,512]{2,1,0:T(4,128)} %bitcast.76), calls=%async_computation.1 | async-start | bytes 524288 | tf_op jit(solution)/shard_map/all_to_all | solution.py:68
  286.2 0.8 copy-start
  789.9 90.6 %copy-start.1 = (f32[32,3,512]{2,0,1:T(8,128)S(1)}, f32[32,3,512]{2,0,1:T(8,128)}, u32[]{:S(2)}) copy-start(f32[32,3,512]{2,0,1:T(8,128)} %copy-done) | copy-start | bytes 589828
  789.9 90.6 %copy-start.3 = (s32[32,1,512]{2,1,0:T(1,128)S(1)}, s32[32,1,512]{2,1,0:T(1,128)}, u32[]{:S(2)}) copy-start(s32[32,1,512]{2,1,0:T(1,128)} %copy-done.2) | copy-start | bytes 196612
  789.9 119.2 %copy-start.7 = (s32[8192]{0:T(1024)S(1)}, s32[8192]{0:T(1024)}, u32[]{:S(2)}) copy-start(s32[8192]{0:T(1024)} %get-tuple-element.193) | copy-start | bytes 98308
  881.2 27.8 %all-to-all-start.2 = ((f32[32,1,512]{2,1,0:T(1,128)}), f32[32,1,512]{2,1,0:T(1,128)S(1)}, u32[]{:S(2)}, u32[]{:S(2)}) async-start(f32[32,1,512]{2,1,0:T(1,128)} %copy.56), calls=%async_computation.2 | async-start | bytes 131072 | tf_op jit(solution)/shard_map/all_to_all | solution.py:103
  909.0 45.6 %copy-start.6 = (f32[32,256]{1,0:T(8,128)S(1)}, f32[32,256]{1,0:T(8,128)}, u32[]{:S(2)}) copy-start(f32[32,256]{1,0:T(8,128)} %copy-done.5) | copy-start | bytes 98308
where the time goes:
time: 960 us; the launch traced here: 955 us
  local copies, waits for them, and re-layouts  683 us (71%)
  other arithmetic  174 us (18%)
  blocking collectives  48.6 us (5%)
  starting transfers between devices  30.3 us (3%)
  waiting for transfers between devices  16.6 us (2%)
    slice x1, local copies, waits for them, and re-layouts, solve_stokes(): a23 = sums[4]  119 us
    scatter-add x1, other arithmetic, shards(): sums = jnp.zeros((9, TILE_PIX), jnp.float32).at[:, pixel_in].add(contrib)  112 us
    gather x2, local copies, waits for them, and re-layouts, shards(): stokes_i[pixel_in]  90.5 us
    gather x2, local copies, waits for them, and re-layouts, shards(): stokes_q[pixel_in]  90.5 us
    gather x2, local copies, waits for them, and re-layouts, shards(): stokes_u[pixel_in]  90.5 us
    unnamed x41, local copies, waits for them, and re-layouts  84.3 us
    gather x2, local copies, waits for them, and re-layouts, shards(): model_signal = returned[slots]  45.5 us
    gather x1, local copies, waits for them, and re-layouts, shards(): sorted_owner = owner_of[order]  45.5 us
  transfers between devices with their start and end apart: 3, of which 2 were waited for; matrix products, arithmetic and copies ran while one was open for 4% of the time, Pallas kernels for 0%

commit v1 on v0

v1 whole, which is shorter than its diff:
```python
import functools

import jax
import jax.numpy as jnp
from jax import lax
from jax.experimental import pallas as pl
from jax.experimental.pallas import tpu as pltpu
from jax.sharding import PartitionSpec as P

MODES = 16
NBINS = 1024
TILE_PIX = 32640
RIDGE = 1.0
LANES = 128
LO = 256
HI = -(-TILE_PIX // LO)
WIN = 32
HIP = HI + WIN - 8
PIX_BITS = 15
HALF = LANES // 2
F32 = jnp.float32
BF16 = jnp.bfloat16
HIGHEST = lax.Precision.HIGHEST
NT = (((1,), (1,)), ((), ()))
NN = (((1,), (0,)), ((), ()))
VMEM_LIMIT = 48 * 1024 * 1024


def iota(shape, dim):
    return lax.broadcasted_iota(jnp.int32, shape, dim)


def split3(x):
    first = x.astype(BF16).astype(F32)
    rest = x - first
    second = rest.astype(BF16).astype(F32)
    return first, second, rest - second


def one_hot_cols(row, rows):
    ids = iota((rows, row.shape[1]), 0).astype(F32).astype(BF16)
    want = jnp.broadcast_to(row.astype(F32).astype(BF16), ids.shape)
    return jnp.where(ids == want, jnp.ones_like(ids), jnp.zeros_like(ids))


def route_kernel(owner_ref, key_ref, load_ref, send_ref, idx_ref, keys, loads):
    tiles, rows = idx_ref.shape[0], idx_ref.shape[1]
    depth = key_ref.shape[0]
    keys[0:depth, :] = key_ref[...]
    loads[0:depth, :] = load_ref[...]
    keys[depth:, :] = jnp.zeros((8, LANES), jnp.int32)
    loads[depth:, :] = jnp.zeros((8, LANES), jnp.int32)
    sorted_keys = key_ref[...]
    lane = iota((8, LANES), 1)
    slot = iota((8, LANES), 0) * LANES + lane
    starts = [jnp.int32(0)]
    for tile in range(1, tiles):
        below = (sorted_keys < (tile << PIX_BITS)).astype(F32)
        starts.append(jnp.sum(below).astype(jnp.int32))
    starts.append(jnp.int32(depth * LANES))
    for tile in range(tiles):
        start = starts[tile]
        count = starts[tile + 1] - start
        top = start // LANES
        shift = start % LANES
        back = lax.rem(LANES - shift, LANES)
        whole = lane < LANES - shift

        def run(ref):
            turned = pltpu.roll(ref[pl.ds(top, 8), :], back, 1)
            return jnp.where(whole, turned, pltpu.roll(turned, 7, 0))

        key = run(keys)
        load = run(loads)
        live = slot < count
        owner = owner_ref[tile]
        pixel = jnp.where(live, key & ((1 << PIX_BITS) - 1), -1)
        index = jnp.where(live, load >> 10, -1)
        send_ref[owner, 0:rows, :] = pixel[0:rows]
        send_ref[owner, rows : 2 * rows, :] = (load & (NBINS - 1))[0:rows]
        idx_ref[owner, :, :] = index[0:rows]


def route(key, load, owner_map, owners, rows):
    flat = key.shape[0]
    depth = flat // LANES
    return pl.pallas_call(
        route_kernel,
        out_shape=(
            jax.ShapeDtypeStruct((owners, 2 * rows, LANES), jnp.int32),
            jax.ShapeDtypeStruct((owners, rows, LANES), jnp.int32),
        ),
        in_specs=[
            pl.BlockSpec(memory_space=pltpu.SMEM),
            pl.BlockSpec(memory_space=pltpu.VMEM),
            pl.BlockSpec(memory_space=pltpu.VMEM),
        ],
        scratch_shapes=[
            pltpu.VMEM((depth + 8, LANES), jnp.int32),
            pltpu.VMEM((depth + 8, LANES), jnp.int32),
        ],
        name="route",
    )(owner_map, key.reshape(depth, LANES), load.reshape(depth, LANES))


def modes_kernel(members, copies, parts_ref, samples_ref, temp_ref, out_ref):
    templates = jnp.sum(parts_ref[...], axis=0) / members
    temp_ref[...] = templates
    both = jnp.concatenate([templates, samples_ref[...]], axis=0)
    products = lax.dot_general(templates, both, NT, precision=HIGHEST, preferred_element_type=F32)
    pad = jnp.zeros((MODES, HALF - products.shape[1]), F32)
    half = jnp.concatenate([products, pad], axis=1)
    packed = jnp.concatenate([half[: MODES // 2], half[MODES // 2 :]], axis=1)
    for i in range(copies):
        out_ref[i] = packed


def modes(parts, samples, members, copies):
    return pl.pallas_call(
        functools.partial(modes_kernel, members, copies),
        out_shape=(
            jax.ShapeDtypeStruct((MODES, samples.shape[1]), F32),
            jax.ShapeDtypeStruct((copies, MODES // 2, LANES), F32),
        ),
        name="modes",
    )(parts, samples)


def clean_kernel(sums_ref, temp_ref, samples_ref, idx_ref, clean_ref, pay_ref):
    det_local, length = samples_ref.shape
    owners, rows = idx_ref.shape[0], idx_ref.shape[1]
    packed = jnp.sum(sums_ref[...], axis=0)
    system = jnp.concatenate([packed, pltpu.roll(packed, HALF, 1)], axis=0)
    row_id = iota((MODES, LANES), 0)
    lane_id = iota((MODES, LANES), 1)
    system = system + jnp.where(row_id == lane_id, RIDGE, 0.0)
    for k in range(MODES):
        pivot = system[k : k + 1, :] / system[k : k + 1, k : k + 1]
        column = system[:, k : k + 1]
        system = jnp.where(row_id == k, pivot, system - column * pivot)
    coef = system[:, MODES : MODES + det_local]
    model = lax.dot_general(
        coef, temp_ref[...], (((0,), (0,)), ((), ())), precision=HIGHEST, preferred_element_type=F32
    )
    cleaned = samples_ref[...] - model
    clean_ref[...] = cleaned
    parts = jnp.concatenate([x.astype(BF16) for x in split3(cleaned)], axis=0)
    det_id = iota((det_local, 2 * LANES), 0)

    def step(pair, _):
        for r in range(rows):
            index = jnp.concatenate(
                [idx_ref[2 * pair, r : r + 1, :], idx_ref[2 * pair + 1, r : r + 1, :]], axis=1
            )
            picked = lax.dot_general(
                parts, one_hot_cols(index & (length - 1), length), NN, preferred_element_type=F32
            )
            total = picked[:det_local] + picked[det_local : 2 * det_local] + picked[2 * det_local :]
            here = jnp.where(det_id == index // length, total, 0.0)
            value = jnp.sum(here, axis=0, keepdims=True)
            pay_ref[2 * pair, r : r + 1, :] = value[:, :LANES]
            pay_ref[2 * pair + 1, r : r + 1, :] = value[:, LANES:]
        return 0

    lax.fori_loop(0, owners // 2, step, 0, unroll=2)


def clean(sums, templates, samples, idx):
    return pl.pallas_call(
        clean_kernel,
        out_shape=(
            jax.ShapeDtypeStruct(samples.shape, F32),
            jax.ShapeDtypeStruct(idx.shape, F32),
        ),
        name="clean",
    )(sums, templates, samples, idx)


def shuffle(first, second, lane):
    return (
        jnp.where(lane < HALF, first, pltpu.roll(second, HALF, 1)),
        jnp.where(lane < HALF, pltpu.roll(first, HALF, 1), second),
    )


def chunk_row(ref, half, quad, r):
    return jnp.concatenate(
        [ref[half, 2 * quad, pl.ds(r, 1), :], ref[half, 2 * quad + 1, pl.ds(r, 1), :]], axis=1
    )


def window(table_ref, half, quad, r):
    at = 2 * (2 * quad + half)
    return table_ref[r, at], table_ref[r, at + 1]


def scatter_add(acc_ref, first, row_hi, one_lo, terms):
    start = pl.multiple_of(first * 8, 8)
    here = (iota((WIN, row_hi.shape[1]), 0) + start) == row_hi
    stacked = [
        jnp.where(here, jnp.broadcast_to(piece, here.shape), 0.0).astype(BF16)
        for pieces in terms
        for piece in pieces
    ]
    found = lax.dot_general(
        jnp.concatenate(stacked, axis=0), one_lo, NT, preferred_element_type=F32
    )
    at = 0
    for q, pieces in enumerate(terms):
        total = found[at : at + WIN]
        at += WIN
        for _ in pieces[1:]:
            total = total + found[at : at + WIN]
            at += WIN
        acc_ref[q, pl.ds(start, WIN), :] += total


def over_chunks(quads, rows, table_ref, body):
    def step(quad, _):
        def live(r, half):
            lowest, highest = window(table_ref, half, quad, r)
            return highest - lowest

        spans = [live(r, half) for r in range(rows) for half in range(2)]
        widest = functools.reduce(jnp.maximum, spans)

        @pl.when(widest >= 0)
        def _():
            for r in range(rows):
                for half in range(2):
                    body(half, quad, r, window(table_ref, half, quad, r)[0], True)

        @pl.when(widest >= WIN // 8)
        def _():
            def chunk(i, _):
                r, half = i // 2, i % 2
                lowest, highest = window(table_ref, half, quad, r)

                def more(w, _):
                    body(half, quad, r, lowest + w * (WIN // 8), False)
                    return 0

                lax.fori_loop(1, (highest - lowest) // (WIN // 8) + 1, more, 0)
                return 0

            lax.fori_loop(0, 2 * rows, chunk, 0)

        return 0

    lax.fori_loop(0, quads, step, 0)


def angles_kernel(got_ref, acc_ref, pix_ref, cos_ref, sin_ref, table_ref, table_vmem, table, sem):
    owners, rows = got_ref.shape[0], got_ref.shape[1] // 2
    lane = iota((2 * rows, LANES), 1)
    table_lane = iota((rows, LANES), 1)
    windows = jnp.zeros((rows, LANES), jnp.int32)
    for quad in range(owners // 4):
        ends = [[], []]
        for sub in range(2):
            pair = 2 * quad + sub
            mixed = shuffle(got_ref[2 * pair], got_ref[2 * pair + 1], lane)
            for half in range(2):
                pixel = mixed[half][:rows]
                pix_ref[half, pair] = pixel
                angle = (jnp.pi * mixed[half][rows:].astype(F32) / NBINS) * 2.0
                cos_ref[half, pair] = jnp.cos(angle)
                sin_ref[half, pair] = jnp.sin(angle)
                ends[half].append(pixel)
        for half in range(2):
            a, b = ends[half]
            most = jnp.maximum(a, b)
            least = jnp.minimum(
                jnp.where(a < 0, TILE_PIX - 1, a), jnp.where(b < 0, TILE_PIX - 1, b)
            )
            most = jnp.max(most, axis=1, keepdims=True)
            least = jnp.min(least, axis=1, keepdims=True)
            high = most >> 11
            low = jnp.where(most < 0, 0, least >> 11)
            at = 2 * (2 * quad + half)
            windows = jnp.where(table_lane == at, low, windows)
            windows = jnp.where(table_lane == at + 1, high, windows)
    table_vmem[...] = windows
    table_ref[...] = windows
    copy = pltpu.make_async_copy(table_vmem, table, sem)
    copy.start()
    acc_ref[...] = jnp.zeros_like(acc_ref)
    copy.wait()

    def body(half, quad, r, first, _):
        pixel = chunk_row(pix_ref, half, quad, r)
        one_lo = one_hot_cols(pixel & (LO - 1), LO)
        cosine = chunk_row(cos_ref, half, quad, r)
        sine = chunk_row(sin_ref, half, quad, r)
        terms = [
            (jnp.ones_like(cosine),),
            split3(cosine),
            split3(sine),
            split3(cosine * cosine),
            split3(cosine * sine),
            split3(sine * sine),
        ]
        scatter_add(acc_ref, first, pixel >> 8, one_lo, terms)

    over_chunks(owners // 4, rows, table, body)


def angles(got):
    owners, rows = got.shape[0], got.shape[1] // 2
    mixed = (2, owners // 2, rows, LANES)
    return pl.pallas_call(
        angles_kernel,
        out_shape=(
            jax.ShapeDtypeStruct((6, HIP, LO), F32),
            jax.ShapeDtypeStruct(mixed, jnp.int32),
            jax.ShapeDtypeStruct(mixed, F32),
            jax.ShapeDtypeStruct(mixed, F32),
            jax.ShapeDtypeStruct((rows, LANES), jnp.int32),
        ),
        scratch_shapes=[
            pltpu.VMEM((rows, LANES), jnp.int32),
            pltpu.SMEM((rows, LANES), jnp.int32),
            pltpu.SemaphoreType.DMA,
        ],
        compiler_params=pltpu.CompilerParams(vmem_limit_bytes=VMEM_LIMIT),
        name="angles",
    )(got)


def solve_stokes(sums):
    a11 = sums[0] + RIDGE
    a12 = sums[1]
    a13 = sums[2]
    a22 = sums[3] + RIDGE
    a23 = sums[4]
    a33 = sums[5] + RIDGE
    c11 = a22 * a33 - a23 * a23
    c12 = a13 * a23 - a12 * a33
    c13 = a12 * a23 - a13 * a22
    c22 = a11 * a33 - a13 * a13
    c23 = a12 * a13 - a11 * a23
    c33 = a11 * a22 - a12 * a12
    inverse = 1.0 / (a11 * c11 + a12 * c12 + a13 * c13)
    stokes_i = (c11 * sums[6] + c12 * sums[7] + c13 * sums[8]) * inverse
    stokes_q = (c12 * sums[6] + c22 * sums[7] + c23 * sums[8]) * inverse
    stokes_u = (c13 * sums[6] + c23 * sums[7] + c33 * sums[8]) * inverse
    return (stokes_i, stokes_q, stokes_u)


def map_kernel(
    table, got_ref, acc_ref, pix_ref, cos_ref, sin_ref, sky_ref, back_ref, value_ref, rhs_ref
):
    owners, rows = got_ref.shape[0], got_ref.shape[1]
    lane = iota((rows, LANES), 1)
    for pair in range(owners // 2):
        mixed = shuffle(got_ref[2 * pair], got_ref[2 * pair + 1], lane)
        for half in range(2):
            value_ref[half, pair] = mixed[half]
    rhs_ref[...] = jnp.zeros_like(rhs_ref)

    def add(half, quad, r, first, _):
        pixel = chunk_row(pix_ref, half, quad, r)
        one_lo = one_hot_cols(pixel & (LO - 1), LO)
        value = chunk_row(value_ref, half, quad, r)
        terms = [
            split3(value),
            split3(chunk_row(cos_ref, half, quad, r) * value),
            split3(chunk_row(sin_ref, half, quad, r) * value),
        ]
        scatter_add(rhs_ref, first, pixel >> 8, one_lo, terms)

    over_chunks(owners // 4, rows, table, add)

    for block in range(HI // 8):
        at = pl.ds(block * 8, 8)
        stokes = solve_stokes([acc_ref[q, at, :] for q in range(6)] + [rhs_ref[q, at, :] for q in range(3)])
        for q in range(3):
            rhs_ref[q, at, :] = stokes[q]
            for i in range(8):
                first = (block * 8 + i) * LO
                width = min(LO, TILE_PIX - first)
                sky_ref[q : q + 1, first : first + width] = stokes[q][i : i + 1, :width]

    value_ref[...] = jnp.zeros_like(value_ref)

    def look(half, quad, r, first, fresh):
        pixel = chunk_row(pix_ref, half, quad, r)
        one_lo = one_hot_cols(pixel & (LO - 1), LO)
        start = pl.multiple_of(first * 8, 8)
        planes = [split3(rhs_ref[q, pl.ds(start, WIN), :]) for q in range(3)]
        found = lax.dot_general(
            jnp.concatenate([x.astype(BF16) for plane in planes for x in plane], axis=0),
            one_lo,
            NN,
            preferred_element_type=F32,
        )
        stokes = [
            found[3 * q * WIN : (3 * q + 1) * WIN]
            + found[(3 * q + 1) * WIN : (3 * q + 2) * WIN]
            + found[(3 * q + 2) * WIN : (3 * q + 3) * WIN]
            for q in range(3)
        ]
        cosine = chunk_row(cos_ref, half, quad, r)
        sine = chunk_row(sin_ref, half, quad, r)
        signal = stokes[0] + cosine * stokes[1] + sine * stokes[2]
        here = (iota(signal.shape, 0) + start) == (pixel >> 8)
        value = jnp.sum(jnp.where(here, signal, 0.0), axis=0, keepdims=True)
        for sub in range(2):
            part = value[:, sub * LANES : (sub + 1) * LANES]
            if fresh:
                value_ref[half, 2 * quad + sub, pl.ds(r, 1), :] = part
            else:
                value_ref[half, 2 * quad + sub, pl.ds(r, 1), :] += part

    over_chunks(owners // 4, rows, table, look)

    for pair in range(owners // 2):
        low, high = value_ref[0, pair], value_ref[1, pair]
        back_ref[2 * pair] = jnp.where(lane < HALF, low, pltpu.roll(high, HALF, 1))
        back_ref[2 * pair + 1] = jnp.where(lane < HALF, pltpu.roll(low, HALF, 1), high)


def make_map(table, got, acc, pixels, cosines, sines):
    vmem = pl.BlockSpec(memory_space=pltpu.VMEM)
    return pl.pallas_call(
        map_kernel,
        out_shape=(
            jax.ShapeDtypeStruct((3, TILE_PIX), F32),
            jax.ShapeDtypeStruct(got.shape, F32),
        ),
        in_specs=[pl.BlockSpec(memory_space=pltpu.SMEM)] + [vmem] * 5,
        scratch_shapes=[pltpu.VMEM(pixels.shape, F32), pltpu.VMEM((3, HIP, LO), F32)],
        compiler_params=pltpu.CompilerParams(vmem_limit_bytes=VMEM_LIMIT),
        name="make_map",
    )(table, got, acc, pixels, cosines, sines)


def residual_kernel(got_ref, idx_ref, clean_ref, out_ref):
    det_local, length = clean_ref.shape
    owners, rows = idx_ref.shape[0], idx_ref.shape[1]
    det_id = iota((det_local, 2 * LANES), 0)

    def step(pair, total):
        for r in range(rows):
            index = jnp.concatenate(
                [idx_ref[2 * pair, r : r + 1, :], idx_ref[2 * pair + 1, r : r + 1, :]], axis=1
            )
            value = jnp.concatenate(
                [got_ref[2 * pair, r : r + 1, :], got_ref[2 * pair + 1, r : r + 1, :]], axis=1
            )
            here = det_id == index // length
            stacked = [
                jnp.where(here, jnp.broadcast_to(piece, here.shape), 0.0).astype(BF16)
                for piece in split3(value)
            ]
            total = total + lax.dot_general(
                jnp.concatenate(stacked, axis=0),
                one_hot_cols(index & (length - 1), length),
                NT,
                preferred_element_type=F32,
            )
        return total

    total = lax.fori_loop(
        0, owners // 2, step, jnp.zeros((3 * det_local, length), F32), unroll=2
    )
    signal = total[:det_local] + total[det_local : 2 * det_local] + total[2 * det_local :]
    out_ref[...] = clean_ref[...] - signal


def residuals(got, idx, cleaned):
    return pl.pallas_call(
        residual_kernel, out_shape=jax.ShapeDtypeStruct(cleaned.shape, F32), name="residuals"
    )(got, idx, cleaned)


def shards(timestream, tile_index, pixel_index, angle_bin, owner_map):
    blocks, det_local, sample_local = timestream.shape
    samples = timestream[0]
    tm_count = lax.axis_size("tm")
    det_count = lax.axis_size("det")
    owners = tm_count * det_count
    flat = det_local * sample_local
    rows = flat // (owners // 2) // LANES

    partial = jnp.sum(samples.reshape(det_local // MODES, MODES, sample_local), axis=0)
    partials = lax.all_gather(partial, "det")
    templates, products = modes(partials, samples, det_local * det_count // MODES, tm_count)
    products = lax.all_to_all(products, "tm", split_axis=0, concat_axis=0, tiled=True)

    key = (tile_index.reshape(-1) << PIX_BITS) + pixel_index.reshape(-1)
    load = (jnp.arange(flat, dtype=jnp.int32) << 10) + angle_bin.reshape(-1)
    key, load = lax.sort((key, load), num_keys=1, is_stable=False)
    send, idx = route(key, load, owner_map, owners, rows)
    everywhere = functools.partial(
        lax.all_to_all, axis_name=("tm", "det"), split_axis=0, concat_axis=0, tiled=True
    )
    got = everywhere(send)
    acc, pixels, cosines, sines, table = angles(got)

    cleaned, pay = clean(products, templates, samples, idx)
    values = everywhere(pay)
    sky, back = make_map(table, values, acc, pixels, cosines, sines)
    residual = residuals(everywhere(back), idx, cleaned)
    return (sky, residual.reshape(blocks, det_local, sample_local))


def solution(mesh):
    placed = (
        P("tm", "det", None),
        P("tm", "det", None),
        P("tm", "det", None),
        P("tm", "det", None),
        P(),
    )
    return jax.shard_map(
        shards,
        mesh=mesh,
        in_specs=placed,
        out_specs=(P(None, ("tm", "det")), P("tm", "det", None)),
        check_vma=False,
    )
```

time: 960 us -> 81.4 us (0.08)
  local copies, waits for them, and re-layouts: 683 us -> 1.39 us
  other arithmetic: 174 us -> 7.07 us
  Pallas kernels: 0 us -> 31.4 us
  blocking collectives: 48.6 us -> 21.4 us
  starting transfers between devices: 30.3 us -> 15.7 us
  waiting for transfers between devices: 16.6 us -> 2.78 us
    gather x27 -> x0, local copies, waits for them, and re-layouts: 378 us -> none  [the longest x2 90.5 us: shards(): stokes_i[pixel_in]]
    slice x1 -> x0, local copies, waits for them, and re-layouts: 119 us -> none  [solve_stokes(): a23 = sums[4]]
    scatter-add x1 -> x0, other arithmetic: 112 us -> none  [shards(): sums = jnp.zeros((9, TILE_PIX), jnp.float32).at[:, pixel_in].add(contrib)]
    scatter x3 -> x0, local copies, waits for them, and re-layouts: 86.3 us -> none  [the longest x1 31 us: shards(): jnp.full((owners_all * capacity,), -1, jnp.int32).at[slots]]
    unnamed x41 -> x10, local copies, waits for them, and re-layouts: 84.3 us -> 1.39 us
    psum x2 -> x0, blocking collectives: 48.6 us -> none  [the longest x1 36.8 us: shards(): mode_gram, mode_proj = lax.psum((mode_gram, mode_proj), 'tm')]
    pallas_call x0 -> x6, Pallas kernels: none -> 31.4 us  [the longest x1 9.66 us: make_map(): pl.pallas_call(map_kernel, out_shape=(jax.ShapeDtypeStruct((3, TILE_PIX),...]
    add x17 -> x1, other arithmetic: 16.1 us -> 0.01 us  [shards(): load = (jnp.arange(flat, dtype=jnp.int32) << 10) + angle_bin.reshape(-1)]
  transfers between devices with their start and end apart: 3 -> 3, of which waited for: 2 -> 2; matrix products, arithmetic and copies ran while one was open for 4% -> 8% of each run, Pallas kernels for 0% -> 18%
where the time goes in v1:
time: 81.4 us; the launch traced here: 80.5 us
  Pallas kernels  31.4 us (39%)
  blocking collectives  21.4 us (26%)
  starting transfers between devices  15.7 us (19%)
  other arithmetic  7.07 us (9%)
  waiting for transfers between devices  2.78 us (3%)
  local copies, waits for them, and re-layouts  1.39 us (2%)
    all_to_all x1, blocking collectives, shards(): residual = residuals(everywhere(back), idx, cleaned)  14.8 us
    pallas_call x1, Pallas kernels, make_map(): pl.pallas_call(map_kernel, out_shape=(jax.ShapeDtypeStruct((3, TILE_PIX),...  9.66 us
    pallas_call x1, Pallas kernels, angles(): pl.pallas_call(angles_kernel, out_shape=(jax.ShapeDtypeStruct((6, HIP, LO...  7.19 us
    all_gather x1, blocking collectives, shards(): partials = lax.all_gather(partial, 'det')  6.63 us
    all_to_all x1, starting transfers between devices, shards(): lax.all_to_all(products, 'tm', split_axis=0, concat_axis=0, tiled=True)  6.44 us
    sort x1, other arithmetic, shards(): key, load = lax.sort((key, load), num_keys=1, is_stable=False)  6.29 us
    all_to_all x1, starting transfers between devices, shards(): got = everywhere(send)  6.03 us
    pallas_call x1, Pallas kernels, clean(): pl.pallas_call(clean_kernel, out_shape=(jax.ShapeDtypeStruct(samples.shap...  5.66 us
  transfers between devices with their start and end apart: 3, of which 2 were waited for; matrix products, arithmetic and copies ran while one was open for 8% of the time, Pallas kernels for 18%

profile of v1, /device:TPU:0, one launch (start us, length us, event | category | flops | bytes accessed | tf_op | source)
XLA Modules:
  0.0 80.5 jit_solution(4894982397257376982)
XLA Ops:
  0.6 0.8 reduce_sum.9
  1.4 6.6 %all-gather = f32[64,256]{1,0:T(8,128)} all-gather(f32[16,256]{1,0:T(8,128)S(1)} %reduce_sum.9), channel_id=2, replica_groups=mesh['tm'=8,'det'=4] {'det'}, dimensions={0}, use_global_device_ids=true | all-gather | bytes 81920 | tf_op jit(solution)/shard_map/all_gather | solution.py:487
  8.0 1.7 %modes.1 = (f32[16,256]{1,0:T(8,128)}, f32[8,8,128]{2,1,0:T(8,128)}) custom-call(f32[4,16,256]{2,1,0:T(8,128)} %bitcast.14, f32[32,256]{1,0:T(8,128)} %bitcast.12), custom_call_target="tpu_custom_call" | custom-call | tf_op jit(solution)/shard_map/modes/pallas_call | solution.py:119
  9.7 0.0 copy-start.3
  9.7 6.4 %all-to-all-start.1 = ((f32[8,8,128]{2,1,0:T(8,128)}), f32[8,8,128]{2,1,0:T(8,128)S(1)}, u32[]{:S(2)}, u32[]{:S(2)}) async-start(f32[8,8,128]{2,1,0:T(8,128)} %get-tuple-element.21), calls=%async_computation.1 | async-start | bytes 65536 | tf_op jit(solution)/shard_map/all_to_all | solution.py:489
  16.2 0.0 copy-done.3
  16.2 0.0 copy-start.1
  16.2 0.0 copy-start.2
  16.2 0.7 copy-done.1
  16.9 0.0 copy-done.2
  17.0 6.3 %sort.15 = (s32[8192]{0:T(1024)}, s32[8192]{0:T(1024)}) sort(s32[8192]{0:T(1024)S(1)} %bitcast.15, s32[8192]{0:T(1024)S(1)} %shift-left_add_fusion), dimensions={0}, to_apply=%region_0.0 | sort | flops 106496 | bytes 131072 | tf_op jit(solution)/shard_map/sort | solution.py:493
  23.3 2.0 %route.1 = (s32[32,8,128]{2,1,0:T(8,128)}, s32[32,4,128]{2,1,0:T(4,128)}) custom-call(s32[32]{0:T(128)} %owner_ref.1, s32[64,128]{1,0:T(8,128)} %bitcast.18, s32[64,128]{1,0:T(8,128)} %bitcast.19), custom_call_target="tpu_custom_call" | custom-call | tf_op jit(solution)/shard_map/route/pallas_call | solution.py:87
  25.2 0.0 all-to-all-done.1.sums_ref
  25.2 0.0 copy-start
  25.3 0.6 copy-done
  25.9 6.0 %all-to-all-start = ((s32[32,8,128]{2,1,0:T(8,128)}), s32[32,8,128]{2,1,0:T(8,128)S(1)}, u32[]{:S(2)}, u32[]{:S(2)}) async-start(s32[32,8,128]{2,1,0:T(8,128)} %get-tuple-element.19), calls=%async_computation | async-start | bytes 262144 | tf_op jit(solution)/shard_map/all_to_all | solution.py:498
  31.9 5.7 %clean.1 = (f32[32,256]{1,0:T(8,128)}, f32[32,4,128]{2,1,0:T(4,128)}) custom-call(f32[8,8,128]{2,1,0:T(8,128)} %copy-done, f32[16,256]{1,0:T(8,128)} %get-tuple-element.22.temp_ref, f32[32,256]{1,0:T(8,128)} %bitcast.13, s32[32,4,128]{2,1,0:T(4,128)} %get-tuple-element.23.idx_ref), custom_call_target="tpu_custom_call" | custom-call | tf_op jit(solution)/shard_map/clean/pallas_call | solution.py:169
  37.6 2.6 %all-to-all-done.got_ref = s32[32,8,128]{2,1,0:T(8,128)S(1)} async-done(((s32[32,8,128]{2,1,0:T(8,128)}), s32[32,8,128]{2,1,0:T(8,128)S(1)}, u32[]{:S(2)}, u32[]{:S(2)}) %all-to-all-start) | async-done | bytes 131104 | tf_op jit(solution)/shard_map/all_to_all | solution.py:498
  40.1 3.3 %all-to-all-start.2 = ((f32[32,4,128]{2,1,0:T(4,128)}), f32[32,4,128]{2,1,0:T(4,128)S(1)}, u32[]{:S(2)}, u32[]{:S(2)}) async-start(f32[32,4,128]{2,1,0:T(4,128)} %get-tuple-element.24), calls=%async_computation.2 | async-start | bytes 131072 | tf_op jit(solution)/shard_map/all_to_all | solution.py:502
  43.4 7.2 %angles.1 = (f32[6,152,256]{2,1,0:T(8,128)S(1)}, s32[2,16,4,128]{3,2,1,0:T(4,128)S(1)}, f32[2,16,4,128]{3,2,1,0:T(4,128)S(1)}, f32[2,16,4,128]{3,2,1,0:T(4,128)S(1)}, s32[4,128]{1,0:T(4,128)S(1)}) custom-call(s32[32,8,128]{2,1,0:T(8,128)S(1)} %all-to-all-done.got_ref), custom_call_target="tpu_custom_call" | custom-call | tf_op jit(solution)/shard_map/angles/pallas_call | solution.py:311
  50.6 0.2 all-to-all-done.2.got_ref
  50.8 9.7 %make_map.1 = (f32[3,32640]{1,0:T(4,128)}, f32[32,4,128]{2,1,0:T(4,128)S(1)}) custom-call(s32[4,128]{1,0:T(4,128)S(1)} %get-tuple-element.20.table, f32[32,4,128]{2,1,0:T(4,128)S(1)} %all-to-all-done.2.got_ref, f32[6,152,256]{2,1,0:T(8,128)S(1)} %get-tuple-element.25.acc_ref, s32[2,16,4,128]{3,2,1,0:T(4,128)S(1)} %get-tuple-element.26.pix_ref, ...), custom_call_target="tpu_custom_call" | custom-call | tf_op jit(solution)/shard_map/make_map/pallas_call | solution.py:425
  60.5 14.8 %all_to_all.20.got_ref = f32[32,4,128]{2,1,0:T(4,128)} all-to-all(f32[32,4,128]{2,1,0:T(4,128)S(1)} %get-tuple-element.30), channel_id=1, replica_groups=mesh['tm'=8,'det'=4] {'tm','det'}, dimensions={0} | all-to-all | bytes 131072 | tf_op jit(solution)/shard_map/all_to_all | solution.py:504
  75.3 5.2 %residuals.1 = f32[32,256]{1,0:T(8,128)} custom-call(f32[32,4,128]{2,1,0:T(4,128)} %all_to_all.20.got_ref, s32[32,4,128]{2,1,0:T(4,128)} %get-tuple-element.23.idx_ref, f32[32,256]{1,0:T(8,128)} %get-tuple-element.31.clean_ref), custom_call_target="tpu_custom_call" | custom-call | tf_op jit(solution)/shard_map/residuals/pallas_call | solution.py:472
  (4 shorter events, 0.0 us)
Async XLA Ops:
  9.7 6.4 %copy-start.3 = (s32[1,32,256]{2,1,0:T(8,128)S(1)}, s32[1,32,256]{2,1,0:T(8,128)}, u32[]{:S(2)}) copy-start(s32[1,32,256]{2,1,0:T(8,128)} %param.8) | copy-start | bytes 98308
  9.7 15.5 %all-to-all-start.1 = ((f32[8,8,128]{2,1,0:T(8,128)}), f32[8,8,128]{2,1,0:T(8,128)S(1)}, u32[]{:S(2)}, u32[]{:S(2)}) async-start(f32[8,8,128]{2,1,0:T(8,128)} %get-tuple-element.21), calls=%async_computation.1 | async-start | bytes 65536 | tf_op jit(solution)/shard_map/all_to_all | solution.py:489
  16.2 0.8 copy-start.1
  16.2 0.8 copy-start.2
  25.2 0.6 copy-start
  25.9 14.3 %all-to-all-start = ((s32[32,8,128]{2,1,0:T(8,128)}), s32[32,8,128]{2,1,0:T(8,128)S(1)}, u32[]{:S(2)}, u32[]{:S(2)}) async-start(s32[32,8,128]{2,1,0:T(8,128)} %get-tuple-element.19), calls=%async_computation | async-start | bytes 262144 | tf_op jit(solution)/shard_map/all_to_all | solution.py:498
  40.1 10.7 %all-to-all-start.2 = ((f32[32,4,128]{2,1,0:T(4,128)}), f32[32,4,128]{2,1,0:T(4,128)S(1)}, u32[]{:S(2)}, u32[]{:S(2)}) async-start(f32[32,4,128]{2,1,0:T(4,128)} %get-tuple-element.24), calls=%async_computation.2 | async-start | bytes 131072 | tf_op jit(solution)/shard_map/all_to_all | solution.py:502

commit v2 on v1

v2 whole, which is shorter than its diff:
```python
import functools

import jax
import jax.numpy as jnp
from jax import lax
from jax.experimental import pallas as pl
from jax.experimental.pallas import tpu as pltpu
from jax.sharding import PartitionSpec as P

MODES = 16
NBINS = 1024
TILE_PIX = 32640
RIDGE = 1.0
LANES = 128
LO = 256
HI = -(-TILE_PIX // LO)
WIN = 32
HIP = HI + WIN - 8
SUB = 32
WAYS = LANES // SUB
GROUP = 8
PIX_BITS = 15
HALF = LANES // 2
F32 = jnp.float32
BF16 = jnp.bfloat16
HIGHEST = lax.Precision.HIGHEST
NT = (((1,), (1,)), ((), ()))
NN = (((1,), (0,)), ((), ()))
VMEM_LIMIT = 24 * 1024 * 1024
VMEM_SPEC = pl.BlockSpec(memory_space=pltpu.VMEM)


def iota(shape, dim):
    return lax.broadcasted_iota(jnp.int32, shape, dim)


def split3(x):
    first = x.astype(BF16).astype(F32)
    rest = x - first
    second = rest.astype(BF16).astype(F32)
    return first, second, rest - second


def split2(x):
    return split3(x)[:2]


def one_hot_cols(row, rows):
    ids = iota((rows, row.shape[1]), 0).astype(F32).astype(BF16)
    want = jnp.broadcast_to(row.astype(F32).astype(BF16), ids.shape)
    return jnp.where(ids == want, jnp.ones_like(ids), jnp.zeros_like(ids))


def modes_kernel(members, copies, *refs):
    part_refs = refs[:-2]
    temp_ref, out_ref = refs[-2:]
    own_ref = part_refs[0]
    groups = own_ref.shape[0] // MODES
    templates = sum(ref[g * MODES : (g + 1) * MODES, :] for ref in part_refs for g in range(groups))
    templates = templates / members
    temp_ref[...] = templates
    both = jnp.concatenate([templates, own_ref[...]], axis=0)
    products = lax.dot_general(templates, both, NT, precision=HIGHEST, preferred_element_type=F32)
    pad = jnp.zeros((MODES, HALF - products.shape[1]), F32)
    half = jnp.concatenate([products, pad], axis=1)
    packed = jnp.concatenate([half[: MODES // 2], half[MODES // 2 :]], axis=1)
    for i in range(copies):
        out_ref[i] = packed


def modes(parts, members, copies):
    return pl.pallas_call(
        functools.partial(modes_kernel, members, copies),
        out_shape=(
            jax.ShapeDtypeStruct((MODES, parts[0].shape[1]), F32),
            jax.ShapeDtypeStruct((copies, MODES // 2, LANES), F32),
        ),
        in_specs=[VMEM_SPEC] * len(parts),
        out_specs=(VMEM_SPEC, VMEM_SPEC),
        compiler_params=pltpu.CompilerParams(vmem_limit_bytes=VMEM_LIMIT),
        name="modes",
    )(*parts)


def route_kernel(owner_ref, key_ref, load_ref, send_ref, idx_ref, keys, loads):
    tiles, rows = idx_ref.shape[0], idx_ref.shape[1]
    depth = key_ref.shape[0]
    keys[0:depth, :] = key_ref[...]
    loads[0:depth, :] = load_ref[...]
    keys[depth:, :] = jnp.zeros((8, LANES), jnp.int32)
    loads[depth:, :] = jnp.zeros((8, LANES), jnp.int32)
    sorted_keys = key_ref[...]
    lane = iota((8, LANES), 1)
    slot = iota((8, LANES), 0) * LANES + lane
    starts = [jnp.int32(0)]
    for tile in range(1, tiles):
        below = (sorted_keys < (tile << PIX_BITS)).astype(F32)
        starts.append(jnp.sum(below).astype(jnp.int32))
    starts.append(jnp.int32(depth * LANES))
    for tile in range(tiles):
        start = starts[tile]
        count = starts[tile + 1] - start
        top = start // LANES
        shift = start % LANES
        back = lax.rem(LANES - shift, LANES)
        whole = lane < LANES - shift

        def run(ref):
            turned = pltpu.roll(ref[pl.ds(top, 8), :], back, 1)
            return jnp.where(whole, turned, pltpu.roll(turned, 7, 0))

        key = run(keys)
        load = run(loads)
        live = slot < count
        owner = owner_ref[tile]
        pixel = jnp.where(live, key & ((1 << PIX_BITS) - 1), -1)
        index = jnp.where(live, load >> 10, -1)
        send_ref[owner, 0:rows, :] = pixel[0:rows]
        send_ref[owner, rows : 2 * rows, :] = (load & (NBINS - 1))[0:rows]
        idx_ref[owner, :, :] = index[0:rows]


def route(key, load, owner_map, owners, rows):
    flat = key.shape[0]
    depth = flat // LANES
    return pl.pallas_call(
        route_kernel,
        out_shape=(
            jax.ShapeDtypeStruct((owners, 2 * rows, LANES), jnp.int32),
            jax.ShapeDtypeStruct((owners, rows, LANES), jnp.int32),
        ),
        in_specs=[pl.BlockSpec(memory_space=pltpu.SMEM), VMEM_SPEC, VMEM_SPEC],
        out_specs=(VMEM_SPEC, VMEM_SPEC),
        scratch_shapes=[
            pltpu.VMEM((depth + 8, LANES), jnp.int32),
            pltpu.VMEM((depth + 8, LANES), jnp.int32),
        ],
        compiler_params=pltpu.CompilerParams(vmem_limit_bytes=VMEM_LIMIT),
        name="route",
    )(owner_map, key.reshape(depth, LANES), load.reshape(depth, LANES))


def clean_kernel(sums_ref, temp_ref, samples_ref, idx_ref, clean_ref, pay_ref):
    det_local, length = samples_ref.shape
    owners, rows = idx_ref.shape[0], idx_ref.shape[1]
    packed = jnp.sum(sums_ref[...], axis=0)
    system = jnp.concatenate([packed, pltpu.roll(packed, HALF, 1)], axis=0)
    row_id = iota((MODES, LANES), 0)
    lane_id = iota((MODES, LANES), 1)
    system = system + jnp.where(row_id == lane_id, RIDGE, 0.0)
    for k in range(MODES):
        pivot = system[k : k + 1, :] / system[k : k + 1, k : k + 1]
        column = system[:, k : k + 1]
        system = jnp.where(row_id == k, pivot, system - column * pivot)
    coef = system[:, MODES : MODES + det_local]
    model = lax.dot_general(
        coef, temp_ref[...], (((0,), (0,)), ((), ())), precision=HIGHEST, preferred_element_type=F32
    )
    cleaned = samples_ref[...] - model
    clean_ref[...] = cleaned
    parts = jnp.concatenate(split2(cleaned), axis=0).astype(BF16)
    det_id = iota((det_local, 2 * LANES), 0)

    def step(pair, _):
        for r in range(rows):
            index = jnp.concatenate(
                [idx_ref[2 * pair, r : r + 1, :], idx_ref[2 * pair + 1, r : r + 1, :]], axis=1
            )
            picked = lax.dot_general(
                parts, one_hot_cols(index & (length - 1), length), NN, preferred_element_type=F32
            )
            total = picked[:det_local] + picked[det_local:]
            here = jnp.where(det_id == index // length, total, 0.0)
            value = jnp.sum(here, axis=0, keepdims=True)
            pay_ref[2 * pair, r : r + 1, :] = value[:, :LANES]
            pay_ref[2 * pair + 1, r : r + 1, :] = value[:, LANES:]
        return 0

    lax.fori_loop(0, owners // 2, step, 0, unroll=4)


def clean(sums, templates, samples, idx):
    return pl.pallas_call(
        clean_kernel,
        out_shape=(
            jax.ShapeDtypeStruct(samples.shape, F32),
            jax.ShapeDtypeStruct(idx.shape, F32),
        ),
        in_specs=[VMEM_SPEC] * 4,
        out_specs=(VMEM_SPEC, VMEM_SPEC),
        compiler_params=pltpu.CompilerParams(vmem_limit_bytes=VMEM_LIMIT),
        name="clean",
    )(sums, templates, samples, idx)


def shuffle(blocks, lane):
    blocks = list(blocks)
    width = HALF
    while width >= SUB:
        low = (lane & width) == 0
        step = width // SUB
        for i in range(WAYS):
            if i & step == 0:
                a, b = blocks[i], blocks[i + step]
                blocks[i] = jnp.where(low, a, pltpu.roll(b, width, 1))
                blocks[i + step] = jnp.where(low, pltpu.roll(a, LANES - width, 1), b)
        width //= 2
    return blocks


def chunk_row(ref, run, group, r):
    return jnp.concatenate([ref[run, GROUP * group + i, r : r + 1, :] for i in range(GROUP)], axis=1)


def over_chunks(groups, rows, table_ref, body):
    def step(i, _):
        run, group = lax.rem(i, WAYS), lax.div(i, WAYS)
        ends = [(table_ref[r, 2 * i], table_ref[r, 2 * i + 1]) for r in range(rows)]
        widest = functools.reduce(jnp.maximum, [high - low for low, high in ends])

        for r in range(rows):
            body(run, group, r, ends[r][0], True)

        @pl.when(widest >= WIN // 8)
        def _():
            for r in range(rows):
                low, high = ends[r]

                def more(w, _):
                    body(run, group, r, low + w * (WIN // 8), False)
                    return 0

                lax.fori_loop(1, (high - low) // (WIN // 8) + 1, more, 0)

        return 0

    lax.fori_loop(0, groups * WAYS, step, 0)


def prepare_kernel(got_ref, mixed_ref):
    owners, rows = got_ref.shape[0], mixed_ref.shape[3]
    lane = iota((2 * rows, LANES), 1)
    for at in range(owners // WAYS):
        mixed = shuffle([got_ref[at * WAYS + i] for i in range(WAYS)], lane)
        for run in range(WAYS):
            mixed_ref[0, run, at] = mixed[run][:rows].astype(F32)
            angle = (jnp.pi * mixed[run][rows:].astype(F32) / NBINS) * 2.0
            mixed_ref[1, run, at] = jnp.cos(angle)
            mixed_ref[2, run, at] = jnp.sin(angle)


def prepare(got, rows):
    return pl.pallas_call(
        prepare_kernel,
        out_shape=jax.ShapeDtypeStruct((3, WAYS, got.shape[0] // WAYS, rows, LANES), F32),
        in_specs=[VMEM_SPEC],
        out_specs=VMEM_SPEC,
        compiler_params=pltpu.CompilerParams(vmem_limit_bytes=VMEM_LIMIT),
        name="prepare",
    )(got)


def windows_of(pix_ref, groups, rows):
    table_lane = iota((rows, LANES), 1)
    windows = jnp.zeros((rows, LANES), jnp.int32)
    for group in range(groups):
        for run in range(WAYS):
            ends = [pix_ref[run, group * GROUP + i] for i in range(GROUP)]
            most = functools.reduce(jnp.maximum, ends)
            least = functools.reduce(
                jnp.minimum, [jnp.where(x < 0, TILE_PIX - 1, x) for x in ends]
            )
            most = jnp.max(most, axis=1, keepdims=True)
            least = jnp.min(least, axis=1, keepdims=True)
            high = most >> 11
            low = jnp.where(most < 0, 0, least >> 11)
            at = 2 * (group * WAYS + run)
            windows = jnp.where(table_lane == at, low, windows)
            windows = jnp.where(table_lane == at + 1, high, windows)
    return windows


PARTS = 20


def solve_stokes(sums):
    a11 = sums[0] + RIDGE
    a12 = sums[1]
    a13 = sums[2]
    a22 = sums[3] + RIDGE
    a23 = sums[4]
    a33 = sums[5] + RIDGE
    c11 = a22 * a33 - a23 * a23
    c12 = a13 * a23 - a12 * a33
    c13 = a12 * a23 - a13 * a22
    c22 = a11 * a33 - a13 * a13
    c23 = a12 * a13 - a11 * a23
    c33 = a11 * a22 - a12 * a12
    inverse = 1.0 / (a11 * c11 + a12 * c12 + a13 * c13)
    stokes_i = (c11 * sums[6] + c12 * sums[7] + c13 * sums[8]) * inverse
    stokes_q = (c12 * sums[6] + c22 * sums[7] + c23 * sums[8]) * inverse
    stokes_u = (c13 * sums[6] + c23 * sums[7] + c33 * sums[8]) * inverse
    return (stokes_i, stokes_q, stokes_u)


def map_kernel(
    got_ref, mixed_ref, sky_ref, back_ref, pix_ref, parts_ref, sum_ref, table_vmem, table, sem
):
    owners, rows = got_ref.shape[0], got_ref.shape[1]
    groups = owners // WAYS // GROUP
    lane = iota((rows, LANES), 1)
    cos_ref, sin_ref = mixed_ref.at[1], mixed_ref.at[2]
    pix_ref[...] = mixed_ref[0].astype(jnp.int32)
    table_vmem[...] = windows_of(pix_ref, groups, rows)
    copy = pltpu.make_async_copy(table_vmem, table, sem)
    copy.start()
    for at in range(owners // WAYS):
        mixed = shuffle([got_ref[at * WAYS + i] for i in range(WAYS)], lane)
        for run in range(WAYS):
            value, cosine, sine = mixed[run], cos_ref[run, at], sin_ref[run, at]
            parts = (
                split3(cosine)
                + split3(sine)
                + split3(cosine * cosine)
                + split3(cosine * sine)
                + split2(value)
                + split3(cosine * value)
                + split3(sine * value)
            )
            for p, part in enumerate(parts):
                parts_ref[p, run, at] = part
    sum_ref[...] = jnp.zeros_like(sum_ref)
    copy.wait()
    terms = (1, 3, 3, 3, 3, 2, 3, 3)

    def add(run, group, r, first, _):
        pixel = chunk_row(pix_ref, run, group, r)
        start = pl.multiple_of(first * 8, 8)
        here = (iota((WIN, pixel.shape[1]), 0) + start) == (pixel >> 8)
        pieces = [jnp.ones(pixel.shape, F32)]
        pieces += [chunk_row(parts_ref.at[p], run, group, r) for p in range(PARTS)]
        stacked = [jnp.where(here, jnp.broadcast_to(x, here.shape), 0.0) for x in pieces]
        found = lax.dot_general(
            jnp.concatenate(stacked, axis=0).astype(BF16),
            one_hot_cols(pixel & (LO - 1), LO),
            NT,
            preferred_element_type=F32,
        )
        at = 0
        for q, count in enumerate(terms):
            total = found[at : at + WIN]
            for i in range(1, count):
                total = total + found[at + i * WIN : at + (i + 1) * WIN]
            at += count * WIN
            sum_ref[q, pl.ds(start, WIN), :] += total

    over_chunks(groups, rows, table, add)

    for block in range(HI // 8):
        at = pl.ds(block * 8, 8)
        sums = [sum_ref[q, at, :] for q in range(8)]
        stokes = solve_stokes(sums[:5] + [sums[0] - sums[3]] + sums[5:])
        for q in range(3):
            sum_ref[q, at, :] = stokes[q]
            for i in range(8):
                first = (block * 8 + i) * LO
                width = min(LO, TILE_PIX - first)
                sky_ref[q : q + 1, first : first + width] = stokes[q][i : i + 1, :width]

    def look(run, group, r, first, fresh):
        pixel = chunk_row(pix_ref, run, group, r)
        start = pl.multiple_of(first * 8, 8)
        planes = [x for q in range(3) for x in split2(sum_ref[q, pl.ds(start, WIN), :])]
        found = lax.dot_general(
            jnp.concatenate(planes, axis=0).astype(BF16),
            one_hot_cols(pixel & (LO - 1), LO),
            NN,
            preferred_element_type=F32,
        )
        stokes = [
            found[2 * q * WIN : (2 * q + 1) * WIN] + found[(2 * q + 1) * WIN : (2 * q + 2) * WIN]
            for q in range(3)
        ]
        cosine = chunk_row(cos_ref, run, group, r)
        sine = chunk_row(sin_ref, run, group, r)
        signal = stokes[0] + cosine * stokes[1] + sine * stokes[2]
        here = (iota(signal.shape, 0) + start) == (pixel >> 8)
        value = jnp.sum(jnp.where(here, signal, 0.0), axis=0, keepdims=True)
        for i in range(GROUP):
            part = value[:, i * LANES : (i + 1) * LANES]
            if fresh:
                parts_ref[0, run, GROUP * group + i, r : r + 1, :] = part
            else:
                parts_ref[0, run, GROUP * group + i, r : r + 1, :] += part

    over_chunks(groups, rows, table, look)

    for at in range(owners // WAYS):
        mixed = shuffle([parts_ref[0, run, at] for run in range(WAYS)], lane)
        for i in range(WAYS):
            back_ref[at * WAYS + i] = mixed[i]


def make_map(got, mixed):
    rows = got.shape[1]
    return pl.pallas_call(
        map_kernel,
        out_shape=(
            jax.ShapeDtypeStruct((3, TILE_PIX), F32),
            jax.ShapeDtypeStruct(got.shape, F32),
        ),
        in_specs=[VMEM_SPEC, VMEM_SPEC],
        out_specs=(VMEM_SPEC, VMEM_SPEC),
        scratch_shapes=[
            pltpu.VMEM(mixed.shape[1:], jnp.int32),
            pltpu.VMEM((PARTS,) + mixed.shape[1:], F32),
            pltpu.VMEM((8, HIP, LO), F32),
            pltpu.VMEM((rows, LANES), jnp.int32),
            pltpu.SMEM((rows, LANES), jnp.int32),
            pltpu.SemaphoreType.DMA,
        ],
        compiler_params=pltpu.CompilerParams(vmem_limit_bytes=VMEM_LIMIT),
        name="make_map",
    )(got, mixed)


def residual_kernel(got_ref, idx_ref, clean_ref, out_ref):
    det_local, length = clean_ref.shape
    owners, rows = idx_ref.shape[0], idx_ref.shape[1]
    det_id = iota((det_local, 2 * LANES), 0)

    def step(pair, total):
        for r in range(rows):
            index = jnp.concatenate(
                [idx_ref[2 * pair, r : r + 1, :], idx_ref[2 * pair + 1, r : r + 1, :]], axis=1
            )
            value = jnp.concatenate(
                [got_ref[2 * pair, r : r + 1, :], got_ref[2 * pair + 1, r : r + 1, :]], axis=1
            )
            here = det_id == index // length
            stacked = [
                jnp.where(here, jnp.broadcast_to(piece, here.shape), 0.0) for piece in split2(value)
            ]
            total = total + lax.dot_general(
                jnp.concatenate(stacked, axis=0).astype(BF16),
                one_hot_cols(index & (length - 1), length),
                NT,
                preferred_element_type=F32,
            )
        return total

    total = lax.fori_loop(
        0, owners // 2, step, jnp.zeros((2 * det_local, length), F32), unroll=4
    )
    signal = total[:det_local] + total[det_local:]
    out_ref[...] = clean_ref[...] - signal


def residuals(got, idx, cleaned):
    return pl.pallas_call(
        residual_kernel,
        out_shape=jax.ShapeDtypeStruct(cleaned.shape, F32),
        in_specs=[VMEM_SPEC] * 3,
        out_specs=VMEM_SPEC,
        compiler_params=pltpu.CompilerParams(vmem_limit_bytes=VMEM_LIMIT),
        name="residuals",
    )(got, idx, cleaned)


def shards(timestream, tile_index, pixel_index, angle_bin, owner_map):
    blocks, det_local, sample_local = timestream.shape
    samples = timestream[0]
    tm_count = lax.axis_size("tm")
    det_count = lax.axis_size("det")
    owners = tm_count * det_count
    flat = det_local * sample_local
    rows = flat // (owners // 2) // LANES

    parts = [samples] + [
        lax.ppermute(samples, "det", [(i, (i + k) % det_count) for i in range(det_count)])
        for k in range(1, det_count)
    ]
    def flatten(x):
        x = x.reshape(det_local // 8, 8, sample_local // LANES, LANES)
        return x.transpose(0, 2, 1, 3).reshape(flat)

    number = jnp.arange(flat, dtype=jnp.int32).reshape(tile_index.shape)
    key = flatten((tile_index << PIX_BITS) + pixel_index)
    load = flatten((number << 10) + angle_bin)
    key, load = lax.sort((key, load), num_keys=1, is_stable=False)
    key, load, parts = lax.optimization_barrier((key, load, parts))
    templates, products = modes(parts, det_local * det_count // MODES, tm_count)
    products = lax.all_to_all(products, "tm", split_axis=0, concat_axis=0, tiled=True)
    send, idx = route(key, load, owner_map, owners, rows)
    everywhere = functools.partial(
        lax.all_to_all, axis_name=("tm", "det"), split_axis=0, concat_axis=0, tiled=True
    )
    got = everywhere(send)
    cleaned, pay = clean(products, templates, samples, idx)
    mixed = prepare(got, rows)

    values = everywhere(pay)
    sky, back = make_map(values, mixed)
    residual = residuals(everywhere(back), idx, cleaned)
    return (sky, residual.reshape(blocks, det_local, sample_local))


def solution(mesh):
    placed = (
        P("tm", "det", None),
        P("tm", "det", None),
        P("tm", "det", None),
        P("tm", "det", None),
        P(),
    )
    return jax.shard_map(
        shards,
        mesh=mesh,
        in_specs=placed,
        out_specs=(P(None, ("tm", "det")), P("tm", "det", None)),
        check_vma=False,
    )
```

time: 81.4 us -> 69.6 us (0.86)
  waiting for transfers between devices: 2.78 us -> 15.3 us
  blocking collectives: 21.4 us -> 9.1 us
  Pallas kernels: 31.4 us -> 22.8 us
  starting transfers between devices: 15.7 us -> 14.2 us
    all_gather x1 -> x0, blocking collectives: 6.63 us -> none  [shards(): partials = lax.all_gather(partial, 'det')]
    all_to_all x1, waiting for transfers between devices: 0.21 us -> 6.78 us  [shards(): values = everywhere(pay)]
    pallas_call x1, Pallas kernels: 7.19 us -> 0.62 us  [prepare(): pl.pallas_call(prepare_kernel, out_shape=jax.ShapeDtypeStruct((3, WAYS, g...]
    all_to_all x1, blocking collectives: 14.8 us -> 9.1 us  [shards(): residual = residuals(everywhere(back), idx, cleaned)]
    all_to_all x1, waiting for transfers between devices: 0.01 us -> 4.45 us  [shards(): lax.all_to_all(products, 'tm', split_axis=0, concat_axis=0, tiled=True)]
    all_to_all x1, starting transfers between devices: 6.03 us -> 2.58 us  [shards(): got = everywhere(send)]
    ppermute x0 -> x3, starting transfers between devices: none -> 3.26 us  [shards(): lax.ppermute(samples, 'det', [(i, (i + k) % det_count) for i in range(det...]
    pallas_call x1, Pallas kernels: 9.66 us -> 11.7 us  [make_map(): pl.pallas_call(map_kernel, out_shape=(jax.ShapeDtypeStruct((3, TILE_PIX),...]
  transfers between devices with their start and end apart: 3 -> 6, of which waited for: 2 -> 3; matrix products, arithmetic and copies ran while one was open for 8% -> 9% of each run, Pallas kernels for 18% -> 9%
where the time goes in v2:
time: 69.6 us; the launch traced here: 69.2 us
  Pallas kernels  22.8 us (33%)
  waiting for transfers between devices  15.3 us (22%)
  starting transfers between devices  14.2 us (20%)
  blocking collectives  9.1 us (13%)
  other arithmetic  6.47 us (9%)
  between operations  0.72 us (1%)
    pallas_call x1, Pallas kernels, make_map(): pl.pallas_call(map_kernel, out_shape=(jax.ShapeDtypeStruct((3, TILE_PIX),...  11.7 us
    all_to_all x1, blocking collectives, shards(): residual = residuals(everywhere(back), idx, cleaned)  9.1 us
    all_to_all x1, waiting for transfers between devices, shards(): values = everywhere(pay)  6.78 us
    all_to_all x1, starting transfers between devices, shards(): lax.all_to_all(products, 'tm', split_axis=0, concat_axis=0, tiled=True)  5.8 us
    sort x1, other arithmetic, shards(): key, load = lax.sort((key, load), num_keys=1, is_stable=False)  5.68 us
    all_to_all x1, waiting for transfers between devices, shards(): lax.all_to_all(products, 'tm', split_axis=0, concat_axis=0, tiled=True)  4.45 us
    pallas_call x1, Pallas kernels, clean(): pl.pallas_call(clean_kernel, out_shape=(jax.ShapeDtypeStruct(samples.shap...  4.21 us
    all_to_all x1, waiting for transfers between devices, shards(): got = everywhere(send)  4.02 us
  transfers between devices with their start and end apart: 6, of which 3 were waited for; matrix products, arithmetic and copies ran while one was open for 9% of the time, Pallas kernels for 9%

profile of v2, /device:TPU:0, one launch (start us, length us, event | category | flops | bytes accessed | tf_op | source)
XLA Modules:
  0.0 69.2 jit_solution(5110641294258610268)
XLA Ops:
  0.6 0.0 copy-start.2
  0.6 2.5 %collective-permute-start.2 = (f32[32,256]{1,0:T(8,128)}, f32[32,256]{1,0:T(8,128)S(1)}, u32[]{:S(2)}, u32[]{:S(2)}) collective-permute-start(f32[32,256]{1,0:T(8,128)} %bitcast.14), channel_id=1, source_target_pairs={{0,3},{1,0},{2,1},{3,2},{4,7},{5,4},{6,5},{7,6},{8,11},{9,8},{10,9... | collective-permute-start | bytes 98312 | tf_op jit(solution)/shard_map/ppermute | solution.py:480
  3.1 0.6 collective-permute-start.1
  3.7 0.2 collective-permute-start
  3.9 0.8 %shift-left_add_fusion.1 = s32[1,32,256]{2,1,0:T(8,128)S(1)} fusion(s32[1,32,256]{2,1,0:T(8,128)} %param.7, s32[1,32,256]{2,1,0:T(8,128)} %param.6), kind=kLoop, calls=%fused_computation.1 | loop fusion | flops 16384 | bytes 98304 | tf_op jit(solution)/shard_map/add | solution.py:488
  4.7 0.0 copy-done.2
  4.7 0.0 copy-start
  4.7 5.7 %sort.15 = (s32[8192]{0:T(1024)S(1)}, s32[8192]{0:T(1024)S(1)}) sort(s32[8192]{0:T(1024)S(1)} %bitcast.21, s32[8192]{0:T(1024)S(1)} %bitcast.22), dimensions={0}, to_apply=%region_0.0 | sort | flops 106496 | bytes 131072 | tf_op jit(solution)/shard_map/sort | solution.py:490
  10.4 0.0 collective-permute-done.2.refs_3_
  10.4 0.0 collective-permute-done.1.refs_2_
  10.4 0.0 collective-permute-done.refs_1_
  10.4 0.0 copy-done
  10.4 0.9 %modes.1 = (f32[16,256]{1,0:T(8,128)S(1)}, f32[8,8,128]{2,1,0:T(8,128)}) custom-call(f32[32,256]{1,0:T(8,128)S(1)} %bitcast.17, f32[32,256]{1,0:T(8,128)S(1)} %collective-permute-done.refs_1_, f32[32,256]{1,0:T(8,128)S(1)} %collective-permute-done.1.refs_2_, f32[32,256]{1,0:T(8,128)S(1)} %collective-permute-done.2.refs_3_), custom_call_target="tpu_custom_call" | custom-call | tf_op jit(solution)/shard_map/modes/pallas_call | solution.py:72
  11.3 5.8 %all-to-all-start = ((f32[8,8,128]{2,1,0:T(8,128)}), f32[8,8,128]{2,1,0:T(8,128)S(1)}, u32[]{:S(2)}, u32[]{:S(2)}) async-start(f32[8,8,128]{2,1,0:T(8,128)} %get-tuple-element.24), calls=%async_computation | async-start | bytes 65536 | tf_op jit(solution)/shard_map/all_to_all | solution.py:493
  17.1 0.0 copy-start.1
  17.1 0.7 copy-done.1
  17.8 1.7 %route.1 = (s32[32,8,128]{2,1,0:T(8,128)}, s32[32,4,128]{2,1,0:T(4,128)S(1)}) custom-call(s32[32]{0:T(128)S(1)} %copy-done.1, s32[64,128]{1,0:T(8,128)S(1)} %bitcast.19, s32[64,128]{1,0:T(8,128)S(1)} %bitcast.20), custom_call_target="tpu_custom_call" | custom-call | tf_op jit(solution)/shard_map/route/pallas_call | solution.py:126
  19.5 4.5 %all-to-all-done.sums_ref = f32[8,8,128]{2,1,0:T(8,128)S(1)} async-done(((f32[8,8,128]{2,1,0:T(8,128)}), f32[8,8,128]{2,1,0:T(8,128)S(1)}, u32[]{:S(2)}, u32[]{:S(2)}) %all-to-all-start) | async-done | bytes 32800 | tf_op jit(solution)/shard_map/all_to_all | solution.py:493
  23.9 2.6 %all-to-all-start.2 = ((s32[32,8,128]{2,1,0:T(8,128)}), s32[32,8,128]{2,1,0:T(8,128)S(1)}, u32[]{:S(2)}, u32[]{:S(2)}) async-start(s32[32,8,128]{2,1,0:T(8,128)} %get-tuple-element.30), calls=%async_computation.2 | async-start | bytes 262144 | tf_op jit(solution)/shard_map/all_to_all | solution.py:498
  26.5 4.2 %clean.1 = (f32[32,256]{1,0:T(8,128)S(1)}, f32[32,4,128]{2,1,0:T(4,128)}) custom-call(f32[8,8,128]{2,1,0:T(8,128)S(1)} %all-to-all-done.sums_ref, f32[16,256]{1,0:T(8,128)S(1)} %get-tuple-element.25.temp_ref, f32[32,256]{1,0:T(8,128)S(1)} %bitcast.18, s32[32,4,128]{2,1,0:T(4,128)S(1)} %get-tuple-element.28.idx_ref), custom_call_target="tpu_custom_call" | custom-call | tf_op jit(solution)/shard_map/clean/pallas_call | solution.py:183
  30.7 4.0 %all-to-all-done.2.got_ref = s32[32,8,128]{2,1,0:T(8,128)S(1)} async-done(((s32[32,8,128]{2,1,0:T(8,128)}), s32[32,8,128]{2,1,0:T(8,128)S(1)}, u32[]{:S(2)}, u32[]{:S(2)}) %all-to-all-start.2) | async-done | bytes 131104 | tf_op jit(solution)/shard_map/all_to_all | solution.py:498
  34.7 2.5 %all-to-all-start.1 = ((f32[32,4,128]{2,1,0:T(4,128)}), f32[32,4,128]{2,1,0:T(4,128)S(1)}, u32[]{:S(2)}, u32[]{:S(2)}) async-start(f32[32,4,128]{2,1,0:T(4,128)} %get-tuple-element.29), calls=%async_computation.1 | async-start | bytes 131072 | tf_op jit(solution)/shard_map/all_to_all | solution.py:502
  37.3 0.6 prepare.1.mixed_ref
  37.9 6.8 %all-to-all-done.1.got_ref = f32[32,4,128]{2,1,0:T(4,128)S(1)} async-done(((f32[32,4,128]{2,1,0:T(4,128)}), f32[32,4,128]{2,1,0:T(4,128)S(1)}, u32[]{:S(2)}, u32[]{:S(2)}) %all-to-all-start.1) | async-done | bytes 65568 | tf_op jit(solution)/shard_map/all_to_all | solution.py:502
  44.7 11.7 %make_map.1 = (f32[3,32640]{1,0:T(4,128)}, f32[32,4,128]{2,1,0:T(4,128)S(1)}) custom-call(f32[32,4,128]{2,1,0:T(4,128)S(1)} %all-to-all-done.1.got_ref, f32[3,4,8,4,128]{4,3,2,1,0:T(4,128)S(1)} %prepare.1.mixed_ref), custom_call_target="tpu_custom_call" | custom-call | tf_op jit(solution)/shard_map/make_map/pallas_call | solution.py:406
  56.4 9.1 %all_to_all.20.got_ref = f32[32,4,128]{2,1,0:T(4,128)S(1)} all-to-all(f32[32,4,128]{2,1,0:T(4,128)S(1)} %get-tuple-element.32), channel_id=1, replica_groups=mesh['tm'=8,'det'=4] {'tm','det'}, dimensions={0} | all-to-all | bytes 131072 | tf_op jit(solution)/shard_map/all_to_all | solution.py:504
  65.5 3.7 %residuals.1 = f32[32,256]{1,0:T(8,128)} custom-call(f32[32,4,128]{2,1,0:T(4,128)S(1)} %all_to_all.20.got_ref, s32[32,4,128]{2,1,0:T(4,128)S(1)} %get-tuple-element.28.idx_ref, f32[32,256]{1,0:T(8,128)S(1)} %get-tuple-element.33.clean_ref), custom_call_target="tpu_custom_call" | custom-call | tf_op jit(solution)/shard_map/residuals/pallas_call | solution.py:460
  (1 shorter events, 0.0 us)
Async XLA Ops:
  0.6 4.1 %copy-start.2 = (s32[1,32,256]{2,1,0:T(8,128)S(1)}, s32[1,32,256]{2,1,0:T(8,128)}, u32[]{:S(2)}) copy-start(s32[1,32,256]{2,1,0:T(8,128)} %param.8) | copy-start | bytes 98308
  0.6 9.8 %collective-permute-start.2 = (f32[32,256]{1,0:T(8,128)}, f32[32,256]{1,0:T(8,128)S(1)}, u32[]{:S(2)}, u32[]{:S(2)}) collective-permute-start(f32[32,256]{1,0:T(8,128)} %bitcast.14), channel_id=1, source_target_pairs={{0,3},{1,0},{2,1},{3,2},{4,7},{5,4},{6,5},{7,6},{8,11},{9,8},{10,9... | collective-permute-start | bytes 98312 | tf_op jit(solution)/shard_map/ppermute | solution.py:480
  3.1 7.3 %collective-permute-start.1 = (f32[32,256]{1,0:T(8,128)}, f32[32,256]{1,0:T(8,128)S(1)}, u32[]{:S(2)}, u32[]{:S(2)}) collective-permute-start(f32[32,256]{1,0:T(8,128)} %bitcast.15), channel_id=1, source_target_pairs={{0,2},{1,3},{2,0},{3,1},{4,6},{5,7},{6,4},{7,5},{8,10},{9,11},{10,... | collective-permute-start | bytes 98312 | tf_op jit(solution)/shard_map/ppermute | solution.py:480
  3.7 6.7 %collective-permute-start = (f32[32,256]{1,0:T(8,128)}, f32[32,256]{1,0:T(8,128)S(1)}, u32[]{:S(2)}, u32[]{:S(2)}) collective-permute-start(f32[32,256]{1,0:T(8,128)} %bitcast.16), channel_id=1, source_target_pairs={{0,1},{1,2},{2,3},{3,0},{4,5},{5,6},{6,7},{7,4},{8,9},{9,10},{10,1... | collective-permute-start | bytes 98312 | tf_op jit(solution)/shard_map/ppermute | solution.py:480
  4.7 5.7 %copy-start = (f32[1,32,256]{2,1,0:T(8,128)S(1)}, f32[1,32,256]{2,1,0:T(8,128)}, u32[]{:S(2)}) copy-start(f32[1,32,256]{2,1,0:T(8,128)} %param.5) | copy-start | bytes 98308
  11.3 12.6 %all-to-all-start = ((f32[8,8,128]{2,1,0:T(8,128)}), f32[8,8,128]{2,1,0:T(8,128)S(1)}, u32[]{:S(2)}, u32[]{:S(2)}) async-start(f32[8,8,128]{2,1,0:T(8,128)} %get-tuple-element.24), calls=%async_computation | async-start | bytes 65536 | tf_op jit(solution)/shard_map/all_to_all | solution.py:493
  17.1 0.7 copy-start.1
  23.9 10.8 %all-to-all-start.2 = ((s32[32,8,128]{2,1,0:T(8,128)}), s32[32,8,128]{2,1,0:T(8,128)S(1)}, u32[]{:S(2)}, u32[]{:S(2)}) async-start(s32[32,8,128]{2,1,0:T(8,128)} %get-tuple-element.30), calls=%async_computation.2 | async-start | bytes 262144 | tf_op jit(solution)/shard_map/all_to_all | solution.py:498
  34.7 10.0 %all-to-all-start.1 = ((f32[32,4,128]{2,1,0:T(4,128)}), f32[32,4,128]{2,1,0:T(4,128)S(1)}, u32[]{:S(2)}, u32[]{:S(2)}) async-start(f32[32,4,128]{2,1,0:T(4,128)} %get-tuple-element.29), calls=%async_computation.1 | async-start | bytes 131072 | tf_op jit(solution)/shard_map/all_to_all | solution.py:502

commit v3 on v2

--- a/solution.py
+++ b/solution.py
@@ -51,7 +51,7 @@
     return jnp.where(ids == want, jnp.ones_like(ids), jnp.zeros_like(ids))
 
 
-def modes_kernel(members, copies, *refs):
+def modes_kernel(members, *refs):
     part_refs = refs[:-2]
     temp_ref, out_ref = refs[-2:]
     own_ref = part_refs[0]
@@ -63,17 +63,15 @@
     products = lax.dot_general(templates, both, NT, precision=HIGHEST, preferred_element_type=F32)
     pad = jnp.zeros((MODES, HALF - products.shape[1]), F32)
     half = jnp.concatenate([products, pad], axis=1)
-    packed = jnp.concatenate([half[: MODES // 2], half[MODES // 2 :]], axis=1)
-    for i in range(copies):
-        out_ref[i] = packed
-
-
-def modes(parts, members, copies):
+    out_ref[...] = jnp.concatenate([half[: MODES // 2], half[MODES // 2 :]], axis=1)
+
+
+def modes(parts, members):
     return pl.pallas_call(
-        functools.partial(modes_kernel, members, copies),
+        functools.partial(modes_kernel, members),
         out_shape=(
             jax.ShapeDtypeStruct((MODES, parts[0].shape[1]), F32),
-            jax.ShapeDtypeStruct((copies, MODES // 2, LANES), F32),
+            jax.ShapeDtypeStruct((MODES // 2, LANES), F32),
         ),
         in_specs=[VMEM_SPEC] * len(parts),
         out_specs=(VMEM_SPEC, VMEM_SPEC),
@@ -140,10 +138,11 @@
     )(owner_map, key.reshape(depth, LANES), load.reshape(depth, LANES))
 
 
-def clean_kernel(sums_ref, temp_ref, samples_ref, idx_ref, clean_ref, pay_ref):
+def clean_kernel(temp_ref, samples_ref, idx_ref, *refs):
+    clean_ref, pay_ref = refs[-2:]
     det_local, length = samples_ref.shape
     owners, rows = idx_ref.shape[0], idx_ref.shape[1]
-    packed = jnp.sum(sums_ref[...], axis=0)
+    packed = sum(ref[...] for ref in refs[:-2])
     system = jnp.concatenate([packed, pltpu.roll(packed, HALF, 1)], axis=0)
     row_id = iota((MODES, LANES), 0)
     lane_id = iota((MODES, LANES), 1)
@@ -186,11 +185,11 @@
             jax.ShapeDtypeStruct(samples.shape, F32),
             jax.ShapeDtypeStruct(idx.shape, F32),
         ),
-        in_specs=[VMEM_SPEC] * 4,
+        in_specs=[VMEM_SPEC] * (3 + len(sums)),
         out_specs=(VMEM_SPEC, VMEM_SPEC),
         compiler_params=pltpu.CompilerParams(vmem_limit_bytes=VMEM_LIMIT),
         name="clean",
-    )(sums, templates, samples, idx)
+    )(templates, samples, idx, *sums)
 
 
 def shuffle(blocks, lane):
@@ -237,29 +236,6 @@
     lax.fori_loop(0, groups * WAYS, step, 0)
 
 
-def prepare_kernel(got_ref, mixed_ref):
-    owners, rows = got_ref.shape[0], mixed_ref.shape[3]
-    lane = iota((2 * rows, LANES), 1)
-    for at in range(owners // WAYS):
-        mixed = shuffle([got_ref[at * WAYS + i] for i in range(WAYS)], lane)
-        for run in range(WAYS):
-            mixed_ref[0, run, at] = mixed[run][:rows].astype(F32)
-            angle = (jnp.pi * mixed[run][rows:].astype(F32) / NBINS) * 2.0
-            mixed_ref[1, run, at] = jnp.cos(angle)
-            mixed_ref[2, run, at] = jnp.sin(angle)
-
-
-def prepare(got, rows):
-    return pl.pallas_call(
-        prepare_kernel,
-        out_shape=jax.ShapeDtypeStruct((3, WAYS, got.shape[0] // WAYS, rows, LANES), F32),
-        in_specs=[VMEM_SPEC],
-        out_specs=VMEM_SPEC,
-        compiler_params=pltpu.CompilerParams(vmem_limit_bytes=VMEM_LIMIT),
-        name="prepare",
-    )(got)
-
-
 def windows_of(pix_ref, groups, rows):
     table_lane = iota((rows, LANES), 1)
     windows = jnp.zeros((rows, LANES), jnp.int32)
@@ -280,7 +256,85 @@
     return windows
 
 
-PARTS = 20
+def scatter_add(sum_ref, terms, pieces, pixel, first):
+    start = pl.multiple_of(first * 8, 8)
+    here = (iota((WIN, pixel.shape[1]), 0) + start) == (pixel >> 8)
+    stacked = [jnp.where(here, jnp.broadcast_to(x, here.shape), 0.0) for x in pieces]
+    found = lax.dot_general(
+        jnp.concatenate(stacked, axis=0).astype(BF16),
+        one_hot_cols(pixel & (LO - 1), LO),
+        NT,
+        preferred_element_type=F32,
+    )
+    at = 0
+    for q, count in enumerate(terms):
+        total = found[at : at + WIN]
+        for i in range(1, count):
+            total = total + found[at + i * WIN : at + (i + 1) * WIN]
+        at += count * WIN
+        sum_ref[q, pl.ds(start, WIN), :] += total
+
+
+ANGLE_TERMS = (1, 3, 3, 3, 3)
+VALUE_TERMS = (2, 3, 3)
+
+
+def angles_kernel(got_ref, mixed_ref, sum_ref, pix_ref, parts_ref, table_vmem, table, sem):
+    owners, rows = got_ref.shape[0], mixed_ref.shape[3]
+    groups = owners // WAYS // GROUP
+    lane = iota((2 * rows, LANES), 1)
+    for at in range(owners // WAYS):
+        mixed = shuffle([got_ref[at * WAYS + i] for i in range(WAYS)], lane)
+        for run in range(WAYS):
+            pix_ref[run, at] = mixed[run][:rows]
+            mixed_ref[0, run, at] = mixed[run][:rows].astype(F32)
+    table_vmem[...] = windows_of(pix_ref, groups, rows)
+    copy = pltpu.make_async_copy(table_vmem, table, sem)
+    copy.start()
+    for at in range(owners // WAYS):
+        mixed = shuffle([got_ref[at * WAYS + i] for i in range(WAYS)], lane)
+        for run in range(WAYS):
+            angle = (jnp.pi * mixed[run][rows:].astype(F32) / NBINS) * 2.0
+            cosine, sine = jnp.cos(angle), jnp.sin(angle)
+            mixed_ref[1, run, at] = cosine
+            mixed_ref[2, run, at] = sine
+            parts = (
+                split3(cosine) + split3(sine) + split3(cosine * cosine) + split3(cosine * sine)
+            )
+            for p, part in enumerate(parts):
+                parts_ref[p, run, at] = part
+    sum_ref[...] = jnp.zeros_like(sum_ref)
+    copy.wait()
+
+    def add(run, group, r, first, _):
+        pixel = chunk_row(pix_ref, run, group, r)
+        pieces = [jnp.ones(pixel.shape, F32)]
+        pieces += [chunk_row(parts_ref.at[p], run, group, r) for p in range(parts_ref.shape[0])]
+        scatter_add(sum_ref, ANGLE_TERMS, pieces, pixel, first)
+
+    over_chunks(groups, rows, table, add)
+
+
+def angles(got, rows):
+    mixed = (WAYS, got.shape[0] // WAYS, rows, LANES)
+    return pl.pallas_call(
+        angles_kernel,
+        out_shape=(
+            jax.ShapeDtypeStruct((3,) + mixed, F32),
+            jax.ShapeDtypeStruct((len(ANGLE_TERMS), HIP, LO), F32),
+        ),
+        in_specs=[VMEM_SPEC],
+        out_specs=(VMEM_SPEC, VMEM_SPEC),
+        scratch_shapes=[
+            pltpu.VMEM(mixed, jnp.int32),
+            pltpu.VMEM((sum(ANGLE_TERMS) - 1,) + mixed, F32),
+            pltpu.VMEM((rows, LANES), jnp.int32),
+            pltpu.SMEM((rows, LANES), jnp.int32),
+            pltpu.SemaphoreType.DMA,
+        ],
+        compiler_params=pltpu.CompilerParams(vmem_limit_bytes=VMEM_LIMIT),
+        name="angles",
+    )(got)
 
 
 def solve_stokes(sums):
@@ -304,7 +358,7 @@
 
 
 def map_kernel(
-    got_ref, mixed_ref, sky_ref, back_ref, pix_ref, parts_ref, sum_ref, table_vmem, table, sem
+    got_ref, mixed_ref, acc_ref, sky_ref, back_ref, pix_ref, parts_ref, sum_ref, table_vmem, table, sem
 ):
     owners, rows = got_ref.shape[0], got_ref.shape[1]
     groups = owners // WAYS // GROUP
@@ -318,48 +372,24 @@
         mixed = shuffle([got_ref[at * WAYS + i] for i in range(WAYS)], lane)
         for run in range(WAYS):
             value, cosine, sine = mixed[run], cos_ref[run, at], sin_ref[run, at]
-            parts = (
-                split3(cosine)
-                + split3(sine)
-                + split3(cosine * cosine)
-                + split3(cosine * sine)
-                + split2(value)
-                + split3(cosine * value)
-                + split3(sine * value)
-            )
+            parts = split2(value) + split3(cosine * value) + split3(sine * value)
             for p, part in enumerate(parts):
                 parts_ref[p, run, at] = part
     sum_ref[...] = jnp.zeros_like(sum_ref)
     copy.wait()
-    terms = (1, 3, 3, 3, 3, 2, 3, 3)
 
     def add(run, group, r, first, _):
         pixel = chunk_row(pix_ref, run, group, r)
-        start = pl.multiple_of(first * 8, 8)
-        here = (iota((WIN, pixel.shape[1]), 0) + start) == (pixel >> 8)
-        pieces = [jnp.ones(pixel.shape, F32)]
-        pieces += [chunk_row(parts_ref.at[p], run, group, r) for p in range(PARTS)]
-        stacked = [jnp.where(here, jnp.broadcast_to(x, here.shape), 0.0) for x in pieces]
-        found = lax.dot_general(
-            jnp.concatenate(stacked, axis=0).astype(BF16),
-            one_hot_cols(pixel & (LO - 1), LO),
-            NT,
-            preferred_element_type=F32,
-        )
-        at = 0
-        for q, count in enumerate(terms):
-            total = found[at : at + WIN]
-            for i in range(1, count):
-                total = total + found[at + i * WIN : at + (i + 1) * WIN]
-            at += count * WIN
-            sum_ref[q, pl.ds(start, WIN), :] += total
+        pieces = [chunk_row(parts_ref.at[p], run, group, r) for p in range(parts_ref.shape[0])]
+        scatter_add(sum_ref, VALUE_TERMS, pieces, pixel, first)
 
     over_chunks(groups, rows, table, add)
 
     for block in range(HI // 8):
         at = pl.ds(block * 8, 8)
-        sums = [sum_ref[q, at, :] for q in range(8)]
-        stokes = solve_stokes(sums[:5] + [sums[0] - sums[3]] + sums[5:])
+        sums = [acc_ref[q, at, :] for q in range(5)]
+        sums += [sums[0] - sums[3]] + [sum_ref[q, at, :] for q in range(3)]
+        stokes = solve_stokes(sums)
         for q in range(3):
             sum_ref[q, at, :] = stokes[q]
             for i in range(8):
@@ -401,7 +431,7 @@
             back_ref[at * WAYS + i] = mixed[i]
 
 
-def make_map(got, mixed):
+def make_map(got, mixed, acc):
     rows = got.shape[1]
     return pl.pallas_call(
         map_kernel,
@@ -409,19 +439,19 @@
             jax.ShapeDtypeStruct((3, TILE_PIX), F32),
             jax.ShapeDtypeStruct(got.shape, F32),
         ),
-        in_specs=[VMEM_SPEC, VMEM_SPEC],
+        in_specs=[VMEM_SPEC] * 3,
         out_specs=(VMEM_SPEC, VMEM_SPEC),
         scratch_shapes=[
             pltpu.VMEM(mixed.shape[1:], jnp.int32),
-            pltpu.VMEM((PARTS,) + mixed.shape[1:], F32),
-            pltpu.VMEM((8, HIP, LO), F32),
+            pltpu.VMEM((sum(VALUE_TERMS),) + mixed.shape[1:], F32),
+            pltpu.VMEM((len(VALUE_TERMS), HIP, LO), F32),
             pltpu.VMEM((rows, LANES), jnp.int32),
             pltpu.SMEM((rows, LANES), jnp.int32),
             pltpu.SemaphoreType.DMA,
         ],
         compiler_params=pltpu.CompilerParams(vmem_limit_bytes=VMEM_LIMIT),
         name="make_map",
-    )(got, mixed)
+    )(got, mixed, acc)
 
 
 def residual_kernel(got_ref, idx_ref, clean_ref, out_ref):
@@ -489,18 +519,24 @@
     load = flatten((number << 10) + angle_bin)
     key, load = lax.sort((key, load), num_keys=1, is_stable=False)
     key, load, parts = lax.optimization_barrier((key, load, parts))
-    templates, products = modes(parts, det_local * det_count // MODES, tm_count)
-    products = lax.all_to_all(products, "tm", split_axis=0, concat_axis=0, tiled=True)
+    templates, products = modes(parts, det_local * det_count // MODES)
+    key, load, products = lax.optimization_barrier((key, load, products))
     send, idx = route(key, load, owner_map, owners, rows)
+    products = products + lax.ppermute(products, "tm", [(i, i ^ 1) for i in range(tm_count)])
+    products, send = lax.optimization_barrier((products, send))
+    products = [products] + [
+        lax.ppermute(products, "tm", [(i, (i + k) % tm_count) for i in range(tm_count)])
+        for k in range(2, tm_count, 2)
+    ]
     everywhere = functools.partial(
         lax.all_to_all, axis_name=("tm", "det"), split_axis=0, concat_axis=0, tiled=True
     )
     got = everywhere(send)
     cleaned, pay = clean(products, templates, samples, idx)
-    mixed = prepare(got, rows)
+    mixed, acc = angles(got, rows)
 
     values = everywhere(pay)
-    sky, back = make_map(values, mixed)
+    sky, back = make_map(values, mixed, acc)
     residual = residuals(everywhere(back), idx, cleaned)
     return (sky, residual.reshape(blocks, det_local, sample_local))
 

time: 69.6 us -> 67.3 us (0.967)
  waiting for transfers between devices: 15.3 us -> 5.67 us
  starting transfers between devices: 14.2 us -> 18.2 us
  blocking collectives: 9.1 us -> 11.7 us
  Pallas kernels: 22.8 us -> 23.6 us
    ppermute x0 -> x4, starting transfers between devices: none -> 6.26 us  [the longest x3 4.75 us: shards(): lax.ppermute(products, 'tm', [(i, (i + k) % tm_count) for i in range(tm_c...]
    all_to_all x1 -> x0, starting transfers between devices: 5.8 us -> none  [shards(): lax.all_to_all(products, 'tm', split_axis=0, concat_axis=0, tiled=True)]
    all_to_all x1, waiting for transfers between devices: 6.78 us -> 1.33 us  [shards(): values = everywhere(pay)]
    pallas_call x2, Pallas kernels: 1.48 us -> 6.29 us  [the longest x1 6.07 us: angles(): pl.pallas_call(angles_kernel, out_shape=(jax.ShapeDtypeStruct((3,) + mixe...]
    all_to_all x1 -> x0, waiting for transfers between devices: 4.45 us -> none  [shards(): lax.all_to_all(products, 'tm', split_axis=0, concat_axis=0, tiled=True)]
    ppermute x0 -> x4, waiting for transfers between devices: none -> 4.33 us  [the longest x3 4.33 us: shards(): lax.ppermute(products, 'tm', [(i, (i + k) % tm_count) for i in range(tm_c...]
    pallas_call x1, Pallas kernels: 11.7 us -> 7.68 us  [make_map(): pl.pallas_call(map_kernel, out_shape=(jax.ShapeDtypeStruct((3, TILE_PIX),...]
    all_to_all x1, waiting for transfers between devices: 4.02 us -> 0.01 us  [shards(): got = everywhere(send)]
  transfers between devices with their start and end apart: 6 -> 9, of which waited for: 3 -> 4; matrix products, arithmetic and copies ran while one was open for 9% -> 10% of each run, Pallas kernels for 9% -> 18%
where the time goes in v3:
time: 67.3 us; the launch traced here: 67 us
  Pallas kernels  23.6 us (35%)
  starting transfers between devices  18.2 us (27%)
  blocking collectives  11.7 us (17%)
  other arithmetic  6.47 us (10%)
  waiting for transfers between devices  5.67 us (8%)
  between operations  0.73 us (1%)
    all_to_all x1, blocking collectives, shards(): residual = residuals(everywhere(back), idx, cleaned)  11.7 us
    pallas_call x1, Pallas kernels, make_map(): pl.pallas_call(map_kernel, out_shape=(jax.ShapeDtypeStruct((3, TILE_PIX),...  7.68 us
    pallas_call x1, Pallas kernels, angles(): pl.pallas_call(angles_kernel, out_shape=(jax.ShapeDtypeStruct((3,) + mixe...  6.07 us
    sort x1, other arithmetic, shards(): key, load = lax.sort((key, load), num_keys=1, is_stable=False)  5.68 us
    all_to_all x1, starting transfers between devices, shards(): got = everywhere(send)  5.31 us
    ppermute x3, starting transfers between devices, shards(): lax.ppermute(products, 'tm', [(i, (i + k) % tm_count) for i in range(tm_c...  4.75 us
    ppermute x3, waiting for transfers between devices, shards(): lax.ppermute(products, 'tm', [(i, (i + k) % tm_count) for i in range(tm_c...  4.33 us
    pallas_call x1, Pallas kernels, clean(): pl.pallas_call(clean_kernel, out_shape=(jax.ShapeDtypeStruct(samples.shap...  4.19 us
  transfers between devices with their start and end apart: 9, of which 4 were waited for; matrix products, arithmetic and copies ran while one was open for 10% of the time, Pallas kernels for 18%

profile of v3, /device:TPU:0, one launch (start us, length us, event | category | flops | bytes accessed | tf_op | source)
XLA Modules:
  0.0 67.0 jit_solution(14481309180460538436)
XLA Ops:
  0.6 0.0 copy-start.2
  0.6 2.5 %collective-permute-start.2 = (f32[32,256]{1,0:T(8,128)}, f32[32,256]{1,0:T(8,128)S(1)}, u32[]{:S(2)}, u32[]{:S(2)}) collective-permute-start(f32[32,256]{1,0:T(8,128)} %bitcast.14), channel_id=1, source_target_pairs={{0,3},{1,0},{2,1},{3,2},{4,7},{5,4},{6,5},{7,6},{8,11},{9,8},{10,9... | collective-permute-start | bytes 98312 | tf_op jit(solution)/shard_map/ppermute | solution.py:510
  3.1 0.6 collective-permute-start.1
  3.7 0.2 collective-permute-start
  3.9 0.8 %shift-left_add_fusion.1 = s32[1,32,256]{2,1,0:T(8,128)S(1)} fusion(s32[1,32,256]{2,1,0:T(8,128)} %param.7, s32[1,32,256]{2,1,0:T(8,128)} %param.6), kind=kLoop, calls=%fused_computation.1 | loop fusion | flops 16384 | bytes 98304 | tf_op jit(solution)/shard_map/add | solution.py:518
  4.7 0.0 copy-done.2
  4.7 0.0 copy-start
  4.7 5.7 %sort.15 = (s32[8192]{0:T(1024)S(1)}, s32[8192]{0:T(1024)S(1)}) sort(s32[8192]{0:T(1024)S(1)} %bitcast.21, s32[8192]{0:T(1024)S(1)} %bitcast.22), dimensions={0}, to_apply=%region_0.0 | sort | flops 106496 | bytes 131072 | tf_op jit(solution)/shard_map/sort | solution.py:520
  10.4 0.0 collective-permute-done.2.refs_3_
  10.4 0.0 collective-permute-done.1.refs_2_
  10.4 0.0 collective-permute-done.refs_1_
  10.4 0.0 copy-done
  10.4 0.2 modes.1
  10.7 1.5 %collective-permute-start.3 = (f32[8,128]{1,0:T(8,128)S(1)}, f32[8,128]{1,0:T(8,128)S(1)}, u32[]{:S(2)}, u32[]{:S(2)}) collective-permute-start(f32[8,128]{1,0:T(8,128)S(1)} %get-tuple-element.38), channel_id=1, source_target_pairs={{0,4},{4,0},{8,12},{12,8},{16,20},{20,16},{24,28},{28,24},{1,5},{5... | collective-permute-start | bytes 12296 | tf_op jit(solution)/shard_map/ppermute | solution.py:525
  12.2 0.0 copy-start.1
  12.2 0.7 copy-done.1
  12.8 1.7 %route.1 = (s32[32,8,128]{2,1,0:T(8,128)}, s32[32,4,128]{2,1,0:T(4,128)S(1)}) custom-call(s32[32]{0:T(128)S(1)} %copy-done.1, s32[64,128]{1,0:T(8,128)S(1)} %bitcast.19, s32[64,128]{1,0:T(8,128)S(1)} %bitcast.20), custom_call_target="tpu_custom_call" | custom-call | tf_op jit(solution)/shard_map/route/pallas_call | solution.py:124
  14.5 0.0 collective-permute-done.3
  14.5 5.3 %all-to-all-start.1 = ((s32[32,8,128]{2,1,0:T(8,128)}), s32[32,8,128]{2,1,0:T(8,128)S(1)}, u32[]{:S(2)}, u32[]{:S(2)}) async-start(s32[32,8,128]{2,1,0:T(8,128)} %get-tuple-element.42), calls=%async_computation.1 | async-start | bytes 262144 | tf_op jit(solution)/shard_map/all_to_all | solution.py:534
  19.8 3.7 %collective-permute-start.6 = (f32[8,128]{1,0:T(8,128)S(1)}, f32[8,128]{1,0:T(8,128)S(1)}, u32[]{:S(2)}, u32[]{:S(2)}) collective-permute-start(f32[8,128]{1,0:T(8,128)S(1)} %add.20.refs_0_), channel_id=1, source_target_pairs={{0,24},{4,28},{8,0},{12,4},{16,8},{20,12},{24,16},{28,20},{1,25},{... | collective-permute-start | bytes 12296 | tf_op jit(solution)/shard_map/ppermute | solution.py:528
  23.5 0.0 collective-permute-start.5
  23.5 1.1 %collective-permute-start.4 = (f32[8,128]{1,0:T(8,128)S(1)}, f32[8,128]{1,0:T(8,128)S(1)}, u32[]{:S(2)}, u32[]{:S(2)}) collective-permute-start(f32[8,128]{1,0:T(8,128)S(1)} %add.20.refs_0_), channel_id=1, source_target_pairs={{0,8},{4,12},{8,16},{12,20},{16,24},{20,28},{24,0},{28,4},{1,9},{5... | collective-permute-start | bytes 12296 | tf_op jit(solution)/shard_map/ppermute | solution.py:528
  24.6 0.2 collective-permute-done.6.refs_3_
  24.9 3.2 %collective-permute-done.5.refs_2_ = f32[8,128]{1,0:T(8,128)S(1)} collective-permute-done((f32[8,128]{1,0:T(8,128)S(1)}, f32[8,128]{1,0:T(8,128)S(1)}, u32[]{:S(2)}, u32[]{:S(2)}) %collective-permute-start.5) | collective-permute-done | bytes 4128 | tf_op jit(solution)/shard_map/ppermute | solution.py:528
  28.0 0.9 %collective-permute-done.4.refs_1_ = f32[8,128]{1,0:T(8,128)S(1)} collective-permute-done((f32[8,128]{1,0:T(8,128)S(1)}, f32[8,128]{1,0:T(8,128)S(1)}, u32[]{:S(2)}, u32[]{:S(2)}) %collective-permute-start.4) | collective-permute-done | bytes 4128 | tf_op jit(solution)/shard_map/ppermute | solution.py:528
  28.9 4.2 %clean.1 = (f32[32,256]{1,0:T(8,128)S(1)}, f32[32,4,128]{2,1,0:T(4,128)}) custom-call(f32[16,256]{1,0:T(8,128)S(1)} %get-tuple-element.31.temp_ref, f32[32,256]{1,0:T(8,128)S(1)} %bitcast.18, s32[32,4,128]{2,1,0:T(4,128)S(1)} %get-tuple-element.37.idx_ref, f32[8,128]{1,0:T(8,128)S(1)} %add.20.refs_0_, f32[8,128]{1,0:T(8,128)S(1)} %collective-permute-done.4.refs_1_, ...), custom_call_target="tpu_custom_call" | custom-call | tf_op jit(solution)/shard_map/clean/pallas_call | solution.py:182
  33.1 0.0 all-to-all-done.1.got_ref
  33.1 3.3 %all-to-all-start = ((f32[32,4,128]{2,1,0:T(4,128)}), f32[32,4,128]{2,1,0:T(4,128)S(1)}, u32[]{:S(2)}, u32[]{:S(2)}) async-start(f32[32,4,128]{2,1,0:T(4,128)} %get-tuple-element.41), calls=%async_computation | async-start | bytes 131072 | tf_op jit(solution)/shard_map/all_to_all | solution.py:538
  36.5 6.1 %angles.1 = (f32[3,4,8,4,128]{4,3,2,1,0:T(4,128)S(1)}, f32[5,152,256]{2,1,0:T(8,128)S(1)}) custom-call(s32[32,8,128]{2,1,0:T(8,128)S(1)} %all-to-all-done.1.got_ref), custom_call_target="tpu_custom_call" | custom-call | tf_op jit(solution)/shard_map/angles/pallas_call | solution.py:320
  42.5 1.3 %all-to-all-done.got_ref = f32[32,4,128]{2,1,0:T(4,128)S(1)} async-done(((f32[32,4,128]{2,1,0:T(4,128)}), f32[32,4,128]{2,1,0:T(4,128)S(1)}, u32[]{:S(2)}, u32[]{:S(2)}) %all-to-all-start) | async-done | bytes 65568 | tf_op jit(solution)/shard_map/all_to_all | solution.py:538
  43.9 7.7 %make_map.1 = (f32[3,32640]{1,0:T(4,128)}, f32[32,4,128]{2,1,0:T(4,128)S(1)}) custom-call(f32[32,4,128]{2,1,0:T(4,128)S(1)} %all-to-all-done.got_ref, f32[3,4,8,4,128]{4,3,2,1,0:T(4,128)S(1)} %get-tuple-element.43.mixed_ref, f32[5,152,256]{2,1,0:T(8,128)S(1)} %get-tuple-element.44.acc_ref), custom_call_target="tpu_custom_call" | custom-call | tf_op jit(solution)/shard_map/make_map/pallas_call | solution.py:436
  51.6 11.7 %all_to_all.15.got_ref = f32[32,4,128]{2,1,0:T(4,128)S(1)} all-to-all(f32[32,4,128]{2,1,0:T(4,128)S(1)} %get-tuple-element.46), channel_id=1, replica_groups=mesh['tm'=8,'det'=4] {'tm','det'}, dimensions={0} | all-to-all | bytes 131072 | tf_op jit(solution)/shard_map/all_to_all | solution.py:540
  63.3 3.7 %residuals.1 = f32[32,256]{1,0:T(8,128)} custom-call(f32[32,4,128]{2,1,0:T(4,128)S(1)} %all_to_all.15.got_ref, s32[32,4,128]{2,1,0:T(4,128)S(1)} %get-tuple-element.37.idx_ref, f32[32,256]{1,0:T(8,128)S(1)} %get-tuple-element.47.clean_ref), custom_call_target="tpu_custom_call" | custom-call | tf_op jit(solution)/shard_map/residuals/pallas_call | solution.py:490
  (2 shorter events, 0.0 us)
Async XLA Ops:
  0.6 4.1 %copy-start.2 = (s32[1,32,256]{2,1,0:T(8,128)S(1)}, s32[1,32,256]{2,1,0:T(8,128)}, u32[]{:S(2)}) copy-start(s32[1,32,256]{2,1,0:T(8,128)} %param.8) | copy-start | bytes 98308
  0.6 9.8 %collective-permute-start.2 = (f32[32,256]{1,0:T(8,128)}, f32[32,256]{1,0:T(8,128)S(1)}, u32[]{:S(2)}, u32[]{:S(2)}) collective-permute-start(f32[32,256]{1,0:T(8,128)} %bitcast.14), channel_id=1, source_target_pairs={{0,3},{1,0},{2,1},{3,2},{4,7},{5,4},{6,5},{7,6},{8,11},{9,8},{10,9... | collective-permute-start | bytes 98312 | tf_op jit(solution)/shard_map/ppermute | solution.py:510
  3.1 7.3 %collective-permute-start.1 = (f32[32,256]{1,0:T(8,128)}, f32[32,256]{1,0:T(8,128)S(1)}, u32[]{:S(2)}, u32[]{:S(2)}) collective-permute-start(f32[32,256]{1,0:T(8,128)} %bitcast.15), channel_id=1, source_target_pairs={{0,2},{1,3},{2,0},{3,1},{4,6},{5,7},{6,4},{7,5},{8,10},{9,11},{10,... | collective-permute-start | bytes 98312 | tf_op jit(solution)/shard_map/ppermute | solution.py:510
  3.7 6.7 %collective-permute-start = (f32[32,256]{1,0:T(8,128)}, f32[32,256]{1,0:T(8,128)S(1)}, u32[]{:S(2)}, u32[]{:S(2)}) collective-permute-start(f32[32,256]{1,0:T(8,128)} %bitcast.16), channel_id=1, source_target_pairs={{0,1},{1,2},{2,3},{3,0},{4,5},{5,6},{6,7},{7,4},{8,9},{9,10},{10,1... | collective-permute-start | bytes 98312 | tf_op jit(solution)/shard_map/ppermute | solution.py:510
  4.7 5.7 %copy-start = (f32[1,32,256]{2,1,0:T(8,128)S(1)}, f32[1,32,256]{2,1,0:T(8,128)}, u32[]{:S(2)}) copy-start(f32[1,32,256]{2,1,0:T(8,128)} %param.5) | copy-start | bytes 98308
  10.7 3.9 %collective-permute-start.3 = (f32[8,128]{1,0:T(8,128)S(1)}, f32[8,128]{1,0:T(8,128)S(1)}, u32[]{:S(2)}, u32[]{:S(2)}) collective-permute-start(f32[8,128]{1,0:T(8,128)S(1)} %get-tuple-element.38), channel_id=1, source_target_pairs={{0,4},{4,0},{8,12},{12,8},{16,20},{20,16},{24,28},{28,24},{1,5},{5... | collective-permute-start | bytes 12296 | tf_op jit(solution)/shard_map/ppermute | solution.py:525
  12.2 0.7 copy-start.1
  14.5 18.6 %all-to-all-start.1 = ((s32[32,8,128]{2,1,0:T(8,128)}), s32[32,8,128]{2,1,0:T(8,128)S(1)}, u32[]{:S(2)}, u32[]{:S(2)}) async-start(s32[32,8,128]{2,1,0:T(8,128)} %get-tuple-element.42), calls=%async_computation.1 | async-start | bytes 262144 | tf_op jit(solution)/shard_map/all_to_all | solution.py:534
  19.8 5.0 %collective-permute-start.6 = (f32[8,128]{1,0:T(8,128)S(1)}, f32[8,128]{1,0:T(8,128)S(1)}, u32[]{:S(2)}, u32[]{:S(2)}) collective-permute-start(f32[8,128]{1,0:T(8,128)S(1)} %add.20.refs_0_), channel_id=1, source_target_pairs={{0,24},{4,28},{8,0},{12,4},{16,8},{20,12},{24,16},{28,20},{1,25},{... | collective-permute-start | bytes 12296 | tf_op jit(solution)/shard_map/ppermute | solution.py:528
  23.5 4.5 %collective-permute-start.5 = (f32[8,128]{1,0:T(8,128)S(1)}, f32[8,128]{1,0:T(8,128)S(1)}, u32[]{:S(2)}, u32[]{:S(2)}) collective-permute-start(f32[8,128]{1,0:T(8,128)S(1)} %add.20.refs_0_), channel_id=1, source_target_pairs={{0,16},{4,20},{8,24},{12,28},{16,0},{20,4},{24,8},{28,12},{1,17},{... | collective-permute-start | bytes 12296 | tf_op jit(solution)/shard_map/ppermute | solution.py:528
  23.5 5.4 %collective-permute-start.4 = (f32[8,128]{1,0:T(8,128)S(1)}, f32[8,128]{1,0:T(8,128)S(1)}, u32[]{:S(2)}, u32[]{:S(2)}) collective-permute-start(f32[8,128]{1,0:T(8,128)S(1)} %add.20.refs_0_), channel_id=1, source_target_pairs={{0,8},{4,12},{8,16},{12,20},{16,24},{20,28},{24,0},{28,4},{1,9},{5... | collective-permute-start | bytes 12296 | tf_op jit(solution)/shard_map/ppermute | solution.py:528
  33.1 10.8 %all-to-all-start = ((f32[32,4,128]{2,1,0:T(4,128)}), f32[32,4,128]{2,1,0:T(4,128)S(1)}, u32[]{:S(2)}, u32[]{:S(2)}) async-start(f32[32,4,128]{2,1,0:T(4,128)} %get-tuple-element.41), calls=%async_computation | async-start | bytes 131072 | tf_op jit(solution)/shard_map/all_to_all | solution.py:538

commit v4 on v3

--- a/solution.py
+++ b/solution.py
@@ -175,7 +175,7 @@
             pay_ref[2 * pair + 1, r : r + 1, :] = value[:, LANES:]
         return 0
 
-    lax.fori_loop(0, owners // 2, step, 0, unroll=4)
+    lax.fori_loop(0, owners // 2, step, 0, unroll=16)
 
 
 def clean(sums, templates, samples, idx):
@@ -454,22 +454,22 @@
     )(got, mixed, acc)
 
 
-def residual_kernel(got_ref, idx_ref, clean_ref, out_ref):
-    det_local, length = clean_ref.shape
+def invert_kernel(idx_ref, slot_ref):
+    det_local, length = slot_ref.shape
     owners, rows = idx_ref.shape[0], idx_ref.shape[1]
     det_id = iota((det_local, 2 * LANES), 0)
+    lane = lax.rem(iota((1, 2 * LANES), 1), LANES).astype(F32)
+    second = (iota((1, 2 * LANES), 1) >= LANES).astype(jnp.int32)
 
     def step(pair, total):
         for r in range(rows):
             index = jnp.concatenate(
                 [idx_ref[2 * pair, r : r + 1, :], idx_ref[2 * pair + 1, r : r + 1, :]], axis=1
             )
-            value = jnp.concatenate(
-                [got_ref[2 * pair, r : r + 1, :], got_ref[2 * pair + 1, r : r + 1, :]], axis=1
-            )
+            row = ((2 * pair + second) * rows + r).astype(F32)
             here = det_id == index // length
             stacked = [
-                jnp.where(here, jnp.broadcast_to(piece, here.shape), 0.0) for piece in split2(value)
+                jnp.where(here, jnp.broadcast_to(piece, here.shape), 0.0) for piece in (row, lane)
             ]
             total = total + lax.dot_general(
                 jnp.concatenate(stacked, axis=0).astype(BF16),
@@ -480,21 +480,48 @@
         return total
 
     total = lax.fori_loop(
-        0, owners // 2, step, jnp.zeros((2 * det_local, length), F32), unroll=4
+        0, owners // 2, step, jnp.zeros((2 * det_local, length), F32), unroll=16
     )
-    signal = total[:det_local] + total[det_local:]
-    out_ref[...] = clean_ref[...] - signal
-
-
-def residuals(got, idx, cleaned):
+    slot_ref[...] = (total[:det_local] * LANES + total[det_local:]).astype(jnp.int32)
+
+
+def invert(idx, shape):
+    return pl.pallas_call(
+        invert_kernel,
+        out_shape=jax.ShapeDtypeStruct(shape, jnp.int32),
+        in_specs=[VMEM_SPEC],
+        out_specs=VMEM_SPEC,
+        compiler_params=pltpu.CompilerParams(vmem_limit_bytes=VMEM_LIMIT),
+        name="invert",
+    )(idx)
+
+
+def residual_kernel(got_ref, slot_ref, clean_ref, out_ref, rows_ref):
+    owners, rows = got_ref.shape[0], got_ref.shape[1]
+    for o in range(owners):
+        rows_ref[o * rows : (o + 1) * rows, :] = got_ref[o]
+    parts = jnp.concatenate(split2(rows_ref[...]), axis=0).astype(BF16)
+    depth = owners * rows
+    row_id = iota((depth, slot_ref.shape[1]), 0)
+    for d in range(slot_ref.shape[0]):
+        slot = slot_ref[d : d + 1, :]
+        found = lax.dot_general(
+            parts, one_hot_cols(slot & (LANES - 1), LANES), NN, preferred_element_type=F32
+        )
+        here = jnp.where(row_id == slot >> 7, found[:depth] + found[depth:], 0.0)
+        out_ref[d : d + 1, :] = clean_ref[d : d + 1, :] - jnp.sum(here, axis=0, keepdims=True)
+
+
+def residuals(got, slot, cleaned):
     return pl.pallas_call(
         residual_kernel,
         out_shape=jax.ShapeDtypeStruct(cleaned.shape, F32),
         in_specs=[VMEM_SPEC] * 3,
         out_specs=VMEM_SPEC,
+        scratch_shapes=[pltpu.VMEM((got.shape[0] * got.shape[1], LANES), F32)],
         compiler_params=pltpu.CompilerParams(vmem_limit_bytes=VMEM_LIMIT),
         name="residuals",
-    )(got, idx, cleaned)
+    )(got, slot, cleaned)
 
 
 def shards(timestream, tile_index, pixel_index, angle_bin, owner_map):
@@ -537,7 +564,7 @@
 
     values = everywhere(pay)
     sky, back = make_map(values, mixed, acc)
-    residual = residuals(everywhere(back), idx, cleaned)
+    residual = residuals(everywhere(back), invert(idx, samples.shape), cleaned)
     return (sky, residual.reshape(blocks, det_local, sample_local))
 
 

time: 67.3 us -> 65.4 us (0.972)
  blocking collectives: 11.7 us -> 0 us
  waiting for transfers between devices: 5.67 us -> 10.3 us
  starting transfers between devices: 18.2 us -> 22.8 us
    all_to_all x1 -> x0, blocking collectives: 11.7 us -> none  [shards(): residual = residuals(everywhere(back), idx, cleaned)]
    all_to_all x0 -> x1, starting transfers between devices: none -> 4.67 us  [shards(): residual = residuals(everywhere(back), invert(idx, samples.shape), cleaned)]
    all_to_all x0 -> x1, waiting for transfers between devices: none -> 4.56 us  [shards(): residual = residuals(everywhere(back), invert(idx, samples.shape), cleaned)]
    pallas_call x0 -> x1, Pallas kernels: none -> 2.66 us  [invert(): pl.pallas_call(invert_kernel, out_shape=jax.ShapeDtypeStruct(shape, jnp.i...]
    pallas_call x1, Pallas kernels: 3.7 us -> 1.87 us  [residuals(): pl.pallas_call(residual_kernel, out_shape=jax.ShapeDtypeStruct(cleaned.sh...]
  transfers between devices with their start and end apart: 9 -> 10, of which waited for: 4 -> 5; matrix products, arithmetic and copies ran while one was open for 10% -> 10% of each run, Pallas kernels for 18% -> 22%
where the time goes in v4:
time: 65.4 us; the launch traced here: 65.1 us
  Pallas kernels  24.1 us (37%)
  starting transfers between devices  22.8 us (35%)
  waiting for transfers between devices  10.3 us (16%)
  other arithmetic  6.47 us (10%)
  between operations  0.74 us (1%)
  local copies, waits for them, and re-layouts  0.67 us (1%)
    pallas_call x1, Pallas kernels, make_map(): pl.pallas_call(map_kernel, out_shape=(jax.ShapeDtypeStruct((3, TILE_PIX),...  7.66 us
    pallas_call x1, Pallas kernels, angles(): pl.pallas_call(angles_kernel, out_shape=(jax.ShapeDtypeStruct((3,) + mixe...  6.05 us
    sort x1, other arithmetic, shards(): key, load = lax.sort((key, load), num_keys=1, is_stable=False)  5.68 us
    all_to_all x1, starting transfers between devices, shards(): got = everywhere(send)  5.31 us
    ppermute x3, starting transfers between devices, shards(): lax.ppermute(products, 'tm', [(i, (i + k) % tm_count) for i in range(tm_c...  4.75 us
    all_to_all x1, starting transfers between devices, shards(): residual = residuals(everywhere(back), invert(idx, samples.shape), cleaned)  4.67 us
    all_to_all x1, waiting for transfers between devices, shards(): residual = residuals(everywhere(back), invert(idx, samples.shape), cleaned)  4.56 us
    ppermute x3, waiting for transfers between devices, shards(): lax.ppermute(products, 'tm', [(i, (i + k) % tm_count) for i in range(tm_c...  4.33 us
  transfers between devices with their start and end apart: 10, of which 5 were waited for; matrix products, arithmetic and copies ran while one was open for 10% of the time, Pallas kernels for 22%

profile of v4, /device:TPU:0, one launch (start us, length us, event | category | flops | bytes accessed | tf_op | source)
XLA Modules:
  0.0 65.1 jit_solution(6437752929601891276)
XLA Ops:
  0.6 0.0 copy-start.2
  0.6 2.5 %collective-permute-start.2 = (f32[32,256]{1,0:T(8,128)}, f32[32,256]{1,0:T(8,128)S(1)}, u32[]{:S(2)}, u32[]{:S(2)}) collective-permute-start(f32[32,256]{1,0:T(8,128)} %bitcast.14), channel_id=1, source_target_pairs={{0,3},{1,0},{2,1},{3,2},{4,7},{5,4},{6,5},{7,6},{8,11},{9,8},{10,9... | collective-permute-start | bytes 98312 | tf_op jit(solution)/shard_map/ppermute | solution.py:537
  3.1 0.6 collective-permute-start.1
  3.7 0.2 collective-permute-start
  3.9 0.8 %shift-left_add_fusion.1 = s32[1,32,256]{2,1,0:T(8,128)S(1)} fusion(s32[1,32,256]{2,1,0:T(8,128)} %param.7, s32[1,32,256]{2,1,0:T(8,128)} %param.6), kind=kLoop, calls=%fused_computation.1 | loop fusion | flops 16384 | bytes 98304 | tf_op jit(solution)/shard_map/add | solution.py:545
  4.7 0.0 copy-done.2
  4.7 0.0 copy-start
  4.7 5.7 %sort.15 = (s32[8192]{0:T(1024)S(1)}, s32[8192]{0:T(1024)S(1)}) sort(s32[8192]{0:T(1024)S(1)} %bitcast.21, s32[8192]{0:T(1024)S(1)} %bitcast.22), dimensions={0}, to_apply=%region_0.0 | sort | flops 106496 | bytes 131072 | tf_op jit(solution)/shard_map/sort | solution.py:547
  10.4 0.0 collective-permute-done.2.refs_3_
  10.4 0.0 collective-permute-done.1.refs_2_
  10.4 0.0 collective-permute-done.refs_1_
  10.4 0.0 copy-done
  10.4 0.2 modes.1
  10.7 1.5 %collective-permute-start.3 = (f32[8,128]{1,0:T(8,128)S(1)}, f32[8,128]{1,0:T(8,128)S(1)}, u32[]{:S(2)}, u32[]{:S(2)}) collective-permute-start(f32[8,128]{1,0:T(8,128)S(1)} %get-tuple-element.38), channel_id=1, source_target_pairs={{0,4},{4,0},{8,12},{12,8},{16,20},{20,16},{24,28},{28,24},{1,5},{5... | collective-permute-start | bytes 12296 | tf_op jit(solution)/shard_map/ppermute | solution.py:552
  12.2 0.0 copy-start.1
  12.2 0.7 %copy-done.1 = s32[32]{0:T(128)S(1)} copy-done((s32[32]{0:T(128)S(1)}, s32[32]{0:T(128)}, u32[]{:S(2)}) %copy-start.1) | copy-done | bytes 152
  12.8 1.7 %route.1 = (s32[32,8,128]{2,1,0:T(8,128)}, s32[32,4,128]{2,1,0:T(4,128)S(1)}) custom-call(s32[32]{0:T(128)S(1)} %copy-done.1, s32[64,128]{1,0:T(8,128)S(1)} %bitcast.19, s32[64,128]{1,0:T(8,128)S(1)} %bitcast.20), custom_call_target="tpu_custom_call" | custom-call | tf_op jit(solution)/shard_map/route/pallas_call | solution.py:124
  14.5 0.0 collective-permute-done.3
  14.5 5.3 %all-to-all-start.1 = ((s32[32,8,128]{2,1,0:T(8,128)}), s32[32,8,128]{2,1,0:T(8,128)S(1)}, u32[]{:S(2)}, u32[]{:S(2)}) async-start(s32[32,8,128]{2,1,0:T(8,128)} %get-tuple-element.42), calls=%async_computation.1 | async-start | bytes 262144 | tf_op jit(solution)/shard_map/all_to_all | solution.py:561
  19.9 3.7 %collective-permute-start.6 = (f32[8,128]{1,0:T(8,128)S(1)}, f32[8,128]{1,0:T(8,128)S(1)}, u32[]{:S(2)}, u32[]{:S(2)}) collective-permute-start(f32[8,128]{1,0:T(8,128)S(1)} %add.20.refs_0_), channel_id=1, source_target_pairs={{0,24},{4,28},{8,0},{12,4},{16,8},{20,12},{24,16},{28,20},{1,25},{... | collective-permute-start | bytes 12296 | tf_op jit(solution)/shard_map/ppermute | solution.py:555
  23.5 0.0 collective-permute-start.5
  23.5 1.1 %collective-permute-start.4 = (f32[8,128]{1,0:T(8,128)S(1)}, f32[8,128]{1,0:T(8,128)S(1)}, u32[]{:S(2)}, u32[]{:S(2)}) collective-permute-start(f32[8,128]{1,0:T(8,128)S(1)} %add.20.refs_0_), channel_id=1, source_target_pairs={{0,8},{4,12},{8,16},{12,20},{16,24},{20,28},{24,0},{28,4},{1,9},{5... | collective-permute-start | bytes 12296 | tf_op jit(solution)/shard_map/ppermute | solution.py:555
  24.6 0.2 collective-permute-done.6.refs_3_
  24.9 3.2 %collective-permute-done.5.refs_2_ = f32[8,128]{1,0:T(8,128)S(1)} collective-permute-done((f32[8,128]{1,0:T(8,128)S(1)}, f32[8,128]{1,0:T(8,128)S(1)}, u32[]{:S(2)}, u32[]{:S(2)}) %collective-permute-start.5) | collective-permute-done | bytes 4128 | tf_op jit(solution)/shard_map/ppermute | solution.py:555
  28.0 0.9 %collective-permute-done.4.refs_1_ = f32[8,128]{1,0:T(8,128)S(1)} collective-permute-done((f32[8,128]{1,0:T(8,128)S(1)}, f32[8,128]{1,0:T(8,128)S(1)}, u32[]{:S(2)}, u32[]{:S(2)}) %collective-permute-start.4) | collective-permute-done | bytes 4128 | tf_op jit(solution)/shard_map/ppermute | solution.py:555
  28.9 3.9 %clean.1 = (f32[32,256]{1,0:T(8,128)S(1)}, f32[32,4,128]{2,1,0:T(4,128)}) custom-call(f32[16,256]{1,0:T(8,128)S(1)} %get-tuple-element.31.temp_ref, f32[32,256]{1,0:T(8,128)S(1)} %bitcast.18, s32[32,4,128]{2,1,0:T(4,128)S(1)} %get-tuple-element.37.idx_ref, f32[8,128]{1,0:T(8,128)S(1)} %add.20.refs_0_, f32[8,128]{1,0:T(8,128)S(1)} %collective-permute-done.4.refs_1_, ...), custom_call_target="tpu_custom_call" | custom-call | tf_op jit(solution)/shard_map/clean/pallas_call | solution.py:182
  32.9 0.0 all-to-all-done.1.got_ref
  32.9 3.3 %all-to-all-start = ((f32[32,4,128]{2,1,0:T(4,128)}), f32[32,4,128]{2,1,0:T(4,128)S(1)}, u32[]{:S(2)}, u32[]{:S(2)}) async-start(f32[32,4,128]{2,1,0:T(4,128)} %get-tuple-element.41), calls=%async_computation | async-start | bytes 131072 | tf_op jit(solution)/shard_map/all_to_all | solution.py:565
  36.2 6.0 %angles.1 = (f32[3,4,8,4,128]{4,3,2,1,0:T(4,128)S(1)}, f32[5,152,256]{2,1,0:T(8,128)S(1)}) custom-call(s32[32,8,128]{2,1,0:T(8,128)S(1)} %all-to-all-done.1.got_ref), custom_call_target="tpu_custom_call" | custom-call | tf_op jit(solution)/shard_map/angles/pallas_call | solution.py:320
  42.3 1.4 %all-to-all-done.got_ref = f32[32,4,128]{2,1,0:T(4,128)S(1)} async-done(((f32[32,4,128]{2,1,0:T(4,128)}), f32[32,4,128]{2,1,0:T(4,128)S(1)}, u32[]{:S(2)}, u32[]{:S(2)}) %all-to-all-start) | async-done | bytes 65568 | tf_op jit(solution)/shard_map/all_to_all | solution.py:565
  43.6 7.7 %make_map.1 = (f32[3,32640]{1,0:T(4,128)}, f32[32,4,128]{2,1,0:T(4,128)}) custom-call(f32[32,4,128]{2,1,0:T(4,128)S(1)} %all-to-all-done.got_ref, f32[3,4,8,4,128]{4,3,2,1,0:T(4,128)S(1)} %get-tuple-element.43.mixed_ref, f32[5,152,256]{2,1,0:T(8,128)S(1)} %get-tuple-element.44.acc_ref), custom_call_target="tpu_custom_call" | custom-call | tf_op jit(solution)/shard_map/make_map/pallas_call | solution.py:436
  51.3 4.7 %all-to-all-start.2 = ((f32[32,4,128]{2,1,0:T(4,128)}), f32[32,4,128]{2,1,0:T(4,128)S(1)}, u32[]{:S(2)}, u32[]{:S(2)}) async-start(f32[32,4,128]{2,1,0:T(4,128)} %get-tuple-element.46), calls=%async_computation.2 | async-start | bytes 131072 | tf_op jit(solution)/shard_map/all_to_all | solution.py:567
  56.0 2.7 %invert.1.slot_ref = s32[32,256]{1,0:T(8,128)S(1)} custom-call(s32[32,4,128]{2,1,0:T(4,128)S(1)} %get-tuple-element.37.idx_ref), custom_call_target="tpu_custom_call" | custom-call | tf_op jit(solution)/shard_map/invert/pallas_call | solution.py:489
  58.6 4.6 %all-to-all-done.2.got_ref = f32[32,4,128]{2,1,0:T(4,128)S(1)} async-done(((f32[32,4,128]{2,1,0:T(4,128)}), f32[32,4,128]{2,1,0:T(4,128)S(1)}, u32[]{:S(2)}, u32[]{:S(2)}) %all-to-all-start.2) | async-done | bytes 65568 | tf_op jit(solution)/shard_map/all_to_all | solution.py:567
  63.2 1.9 %residuals.1 = f32[32,256]{1,0:T(8,128)} custom-call(f32[32,4,128]{2,1,0:T(4,128)S(1)} %all-to-all-done.2.got_ref, s32[32,256]{1,0:T(8,128)S(1)} %invert.1.slot_ref, f32[32,256]{1,0:T(8,128)S(1)} %get-tuple-element.47.clean_ref), custom_call_target="tpu_custom_call" | custom-call | tf_op jit(solution)/shard_map/residuals/pallas_call | solution.py:516
  (2 shorter events, 0.0 us)
Async XLA Ops:
  0.6 4.1 %copy-start.2 = (s32[1,32,256]{2,1,0:T(8,128)S(1)}, s32[1,32,256]{2,1,0:T(8,128)}, u32[]{:S(2)}) copy-start(s32[1,32,256]{2,1,0:T(8,128)} %param.8) | copy-start | bytes 98308
  0.6 9.8 %collective-permute-start.2 = (f32[32,256]{1,0:T(8,128)}, f32[32,256]{1,0:T(8,128)S(1)}, u32[]{:S(2)}, u32[]{:S(2)}) collective-permute-start(f32[32,256]{1,0:T(8,128)} %bitcast.14), channel_id=1, source_target_pairs={{0,3},{1,0},{2,1},{3,2},{4,7},{5,4},{6,5},{7,6},{8,11},{9,8},{10,9... | collective-permute-start | bytes 98312 | tf_op jit(solution)/shard_map/ppermute | solution.py:537
  3.1 7.3 %collective-permute-start.1 = (f32[32,256]{1,0:T(8,128)}, f32[32,256]{1,0:T(8,128)S(1)}, u32[]{:S(2)}, u32[]{:S(2)}) collective-permute-start(f32[32,256]{1,0:T(8,128)} %bitcast.15), channel_id=1, source_target_pairs={{0,2},{1,3},{2,0},{3,1},{4,6},{5,7},{6,4},{7,5},{8,10},{9,11},{10,... | collective-permute-start | bytes 98312 | tf_op jit(solution)/shard_map/ppermute | solution.py:537
  3.7 6.7 %collective-permute-start = (f32[32,256]{1,0:T(8,128)}, f32[32,256]{1,0:T(8,128)S(1)}, u32[]{:S(2)}, u32[]{:S(2)}) collective-permute-start(f32[32,256]{1,0:T(8,128)} %bitcast.16), channel_id=1, source_target_pairs={{0,1},{1,2},{2,3},{3,0},{4,5},{5,6},{6,7},{7,4},{8,9},{9,10},{10,1... | collective-permute-start | bytes 98312 | tf_op jit(solution)/shard_map/ppermute | solution.py:537
  4.7 5.7 %copy-start = (f32[1,32,256]{2,1,0:T(8,128)S(1)}, f32[1,32,256]{2,1,0:T(8,128)}, u32[]{:S(2)}) copy-start(f32[1,32,256]{2,1,0:T(8,128)} %param.5) | copy-start | bytes 98308
  10.7 3.9 %collective-permute-start.3 = (f32[8,128]{1,0:T(8,128)S(1)}, f32[8,128]{1,0:T(8,128)S(1)}, u32[]{:S(2)}, u32[]{:S(2)}) collective-permute-start(f32[8,128]{1,0:T(8,128)S(1)} %get-tuple-element.38), channel_id=1, source_target_pairs={{0,4},{4,0},{8,12},{12,8},{16,20},{20,16},{24,28},{28,24},{1,5},{5... | collective-permute-start | bytes 12296 | tf_op jit(solution)/shard_map/ppermute | solution.py:552
  12.2 0.7 %copy-start.1 = (s32[32]{0:T(128)S(1)}, s32[32]{0:T(128)}, u32[]{:S(2)}) copy-start(s32[32]{0:T(128)} %owner_ref.1) | copy-start | bytes 388
  14.5 18.3 %all-to-all-start.1 = ((s32[32,8,128]{2,1,0:T(8,128)}), s32[32,8,128]{2,1,0:T(8,128)S(1)}, u32[]{:S(2)}, u32[]{:S(2)}) async-start(s32[32,8,128]{2,1,0:T(8,128)} %get-tuple-element.42), calls=%async_computation.1 | async-start | bytes 262144 | tf_op jit(solution)/shard_map/all_to_all | solution.py:561
  19.9 5.0 %collective-permute-start.6 = (f32[8,128]{1,0:T(8,128)S(1)}, f32[8,128]{1,0:T(8,128)S(1)}, u32[]{:S(2)}, u32[]{:S(2)}) collective-permute-start(f32[8,128]{1,0:T(8,128)S(1)} %add.20.refs_0_), channel_id=1, source_target_pairs={{0,24},{4,28},{8,0},{12,4},{16,8},{20,12},{24,16},{28,20},{1,25},{... | collective-permute-start | bytes 12296 | tf_op jit(solution)/shard_map/ppermute | solution.py:555
  23.5 4.5 %collective-permute-start.5 = (f32[8,128]{1,0:T(8,128)S(1)}, f32[8,128]{1,0:T(8,128)S(1)}, u32[]{:S(2)}, u32[]{:S(2)}) collective-permute-start(f32[8,128]{1,0:T(8,128)S(1)} %add.20.refs_0_), channel_id=1, source_target_pairs={{0,16},{4,20},{8,24},{12,28},{16,0},{20,4},{24,8},{28,12},{1,17},{... | collective-permute-start | bytes 12296 | tf_op jit(solution)/shard_map/ppermute | solution.py:555
  23.5 5.4 %collective-permute-start.4 = (f32[8,128]{1,0:T(8,128)S(1)}, f32[8,128]{1,0:T(8,128)S(1)}, u32[]{:S(2)}, u32[]{:S(2)}) collective-permute-start(f32[8,128]{1,0:T(8,128)S(1)} %add.20.refs_0_), channel_id=1, source_target_pairs={{0,8},{4,12},{8,16},{12,20},{16,24},{20,28},{24,0},{28,4},{1,9},{5... | collective-permute-start | bytes 12296 | tf_op jit(solution)/shard_map/ppermute | solution.py:555
  32.9 10.8 %all-to-all-start = ((f32[32,4,128]{2,1,0:T(4,128)}), f32[32,4,128]{2,1,0:T(4,128)S(1)}, u32[]{:S(2)}, u32[]{:S(2)}) async-start(f32[32,4,128]{2,1,0:T(4,128)} %get-tuple-element.41), calls=%async_computation | async-start | bytes 131072 | tf_op jit(solution)/shard_map/all_to_all | solution.py:565
  51.3 11.9 %all-to-all-start.2 = ((f32[32,4,128]{2,1,0:T(4,128)}), f32[32,4,128]{2,1,0:T(4,128)S(1)}, u32[]{:S(2)}, u32[]{:S(2)}) async-start(f32[32,4,128]{2,1,0:T(4,128)} %get-tuple-element.46), calls=%async_computation.2 | async-start | bytes 131072 | tf_op jit(solution)/shard_map/all_to_all | solution.py:567

commit v5 on v4

--- a/solution.py
+++ b/solution.py
@@ -138,9 +138,53 @@
     )(owner_map, key.reshape(depth, LANES), load.reshape(depth, LANES))
 
 
-def clean_kernel(temp_ref, samples_ref, idx_ref, *refs):
-    clean_ref, pay_ref = refs[-2:]
+def pair_row(ref, pair, r):
+    return jnp.concatenate([ref[2 * pair, r : r + 1, :], ref[2 * pair + 1, r : r + 1, :]], axis=1)
+
+
+def pick_kernel(temp_ref, samples_ref, idx_ref, raw_ref, there_ref):
     det_local, length = samples_ref.shape
+    owners, rows = idx_ref.shape[0], idx_ref.shape[1]
+    terms = split3(samples_ref[...]) + split3(temp_ref[...])
+    parts = jnp.concatenate(terms, axis=0).astype(BF16)
+    det_id = iota((det_local, 2 * LANES), 0)
+
+    def step(pair, _):
+        for r in range(rows):
+            index = pair_row(idx_ref, pair, r)
+            found = lax.dot_general(
+                parts, one_hot_cols(index & (length - 1), length), NN, preferred_element_type=F32
+            )
+            own = sum(found[i * det_local : (i + 1) * det_local] for i in range(3))
+            here = jnp.where(det_id == index // length, own, 0.0)
+            value = jnp.sum(here, axis=0, keepdims=True)
+            raw_ref[2 * pair, r : r + 1, :] = value[:, :LANES]
+            raw_ref[2 * pair + 1, r : r + 1, :] = value[:, LANES:]
+            found = found[3 * det_local :]
+            there_ref[pair, r] = sum(found[i * MODES : (i + 1) * MODES] for i in range(3))
+        return 0
+
+    lax.fori_loop(0, owners // 2, step, 0, unroll=16)
+
+
+def pick(templates, samples, idx):
+    owners, rows = idx.shape[:2]
+    return pl.pallas_call(
+        pick_kernel,
+        out_shape=(
+            jax.ShapeDtypeStruct(idx.shape, F32),
+            jax.ShapeDtypeStruct((owners // 2, rows, MODES, 2 * LANES), F32),
+        ),
+        in_specs=[VMEM_SPEC] * 3,
+        out_specs=(VMEM_SPEC, VMEM_SPEC),
+        compiler_params=pltpu.CompilerParams(vmem_limit_bytes=VMEM_LIMIT),
+        name="pick",
+    )(templates, samples, idx)
+
+
+def clean_kernel(length, raw_ref, there_ref, idx_ref, *refs):
+    coef_ref, pay_ref = refs[-2:]
+    det_local = coef_ref.shape[1]
     owners, rows = idx_ref.shape[0], idx_ref.shape[1]
     packed = sum(ref[...] for ref in refs[:-2])
     system = jnp.concatenate([packed, pltpu.roll(packed, HALF, 1)], axis=0)
@@ -152,25 +196,21 @@
         column = system[:, k : k + 1]
         system = jnp.where(row_id == k, pivot, system - column * pivot)
     coef = system[:, MODES : MODES + det_local]
-    model = lax.dot_general(
-        coef, temp_ref[...], (((0,), (0,)), ((), ())), precision=HIGHEST, preferred_element_type=F32
-    )
-    cleaned = samples_ref[...] - model
-    clean_ref[...] = cleaned
-    parts = jnp.concatenate(split2(cleaned), axis=0).astype(BF16)
-    det_id = iota((det_local, 2 * LANES), 0)
+    coef_ref[...] = coef
+    parts = jnp.concatenate(split3(coef), axis=0).astype(BF16)
 
     def step(pair, _):
         for r in range(rows):
-            index = jnp.concatenate(
-                [idx_ref[2 * pair, r : r + 1, :], idx_ref[2 * pair + 1, r : r + 1, :]], axis=1
+            index = pair_row(idx_ref, pair, r)
+            found = lax.dot_general(
+                parts,
+                one_hot_cols(jnp.where(index < 0, det_local, index // length), det_local),
+                NN,
+                preferred_element_type=F32,
             )
-            picked = lax.dot_general(
-                parts, one_hot_cols(index & (length - 1), length), NN, preferred_element_type=F32
-            )
-            total = picked[:det_local] + picked[det_local:]
-            here = jnp.where(det_id == index // length, total, 0.0)
-            value = jnp.sum(here, axis=0, keepdims=True)
+            weight = sum(found[i * MODES : (i + 1) * MODES] for i in range(3))
+            model = jnp.sum(weight * there_ref[pair, r], axis=0, keepdims=True)
+            value = pair_row(raw_ref, pair, r) - model
             pay_ref[2 * pair, r : r + 1, :] = value[:, :LANES]
             pay_ref[2 * pair + 1, r : r + 1, :] = value[:, LANES:]
         return 0
@@ -178,18 +218,19 @@
     lax.fori_loop(0, owners // 2, step, 0, unroll=16)
 
 
-def clean(sums, templates, samples, idx):
-    return pl.pallas_call(
-        clean_kernel,
+def clean(sums, raw, there, idx, shape):
+    det_local, length = shape
+    return pl.pallas_call(
+        functools.partial(clean_kernel, length),
         out_shape=(
-            jax.ShapeDtypeStruct(samples.shape, F32),
+            jax.ShapeDtypeStruct((MODES, det_local), F32),
             jax.ShapeDtypeStruct(idx.shape, F32),
         ),
         in_specs=[VMEM_SPEC] * (3 + len(sums)),
         out_specs=(VMEM_SPEC, VMEM_SPEC),
         compiler_params=pltpu.CompilerParams(vmem_limit_bytes=VMEM_LIMIT),
         name="clean",
-    )(templates, samples, idx, *sums)
+    )(raw, there, idx, *sums)
 
 
 def shuffle(blocks, lane):
@@ -454,8 +495,15 @@
     )(got, mixed, acc)
 
 
-def invert_kernel(idx_ref, slot_ref):
+def invert_kernel(idx_ref, coef_ref, temp_ref, samples_ref, slot_ref, clean_ref):
     det_local, length = slot_ref.shape
+    clean_ref[...] = samples_ref[...] - lax.dot_general(
+        coef_ref[...],
+        temp_ref[...],
+        (((0,), (0,)), ((), ())),
+        precision=HIGHEST,
+        preferred_element_type=F32,
+    )
     owners, rows = idx_ref.shape[0], idx_ref.shape[1]
     det_id = iota((det_local, 2 * LANES), 0)
     lane = lax.rem(iota((1, 2 * LANES), 1), LANES).astype(F32)
@@ -485,15 +533,18 @@
     slot_ref[...] = (total[:det_local] * LANES + total[det_local:]).astype(jnp.int32)
 
 
-def invert(idx, shape):
+def invert(idx, coef, templates, samples):
     return pl.pallas_call(
         invert_kernel,
-        out_shape=jax.ShapeDtypeStruct(shape, jnp.int32),
-        in_specs=[VMEM_SPEC],
-        out_specs=VMEM_SPEC,
+        out_shape=(
+            jax.ShapeDtypeStruct(samples.shape, jnp.int32),
+            jax.ShapeDtypeStruct(samples.shape, F32),
+        ),
+        in_specs=[VMEM_SPEC] * 4,
+        out_specs=(VMEM_SPEC, VMEM_SPEC),
         compiler_params=pltpu.CompilerParams(vmem_limit_bytes=VMEM_LIMIT),
         name="invert",
-    )(idx)
+    )(idx, coef, templates, samples)
 
 
 def residual_kernel(got_ref, slot_ref, clean_ref, out_ref, rows_ref):
@@ -544,27 +595,39 @@
     number = jnp.arange(flat, dtype=jnp.int32).reshape(tile_index.shape)
     key = flatten((tile_index << PIX_BITS) + pixel_index)
     load = flatten((number << 10) + angle_bin)
+    templates, products = modes(parts, det_local * det_count // MODES)
+
+    def partners(x, bit):
+        return lax.ppermute(x, "tm", [(i, i ^ bit) for i in range(tm_count)])
+
+    key, load, products = lax.optimization_barrier((key, load, products))
+    found = partners(products, 1)
     key, load = lax.sort((key, load), num_keys=1, is_stable=False)
-    key, load, parts = lax.optimization_barrier((key, load, parts))
-    templates, products = modes(parts, det_local * det_count // MODES)
-    key, load, products = lax.optimization_barrier((key, load, products))
+    key, load, found = lax.optimization_barrier((key, load, found))
+    products = products + found
+    found = partners(products, 2)
     send, idx = route(key, load, owner_map, owners, rows)
-    products = products + lax.ppermute(products, "tm", [(i, i ^ 1) for i in range(tm_count)])
-    products, send = lax.optimization_barrier((products, send))
-    products = [products] + [
-        lax.ppermute(products, "tm", [(i, (i + k) % tm_count) for i in range(tm_count)])
-        for k in range(2, tm_count, 2)
-    ]
+    send, found = lax.optimization_barrier((send, found))
+    products = products + found
+    bit = 4
+    while bit < tm_count:
+        found = partners(products, bit)
+        bit *= 2
+        if bit < tm_count:
+            products = products + found
+    products = [products, found]
     everywhere = functools.partial(
         lax.all_to_all, axis_name=("tm", "det"), split_axis=0, concat_axis=0, tiled=True
     )
     got = everywhere(send)
-    cleaned, pay = clean(products, templates, samples, idx)
+    raw, there = pick(templates, samples, idx)
+    coef, pay = clean(products, raw, there, idx, samples.shape)
     mixed, acc = angles(got, rows)
 
     values = everywhere(pay)
     sky, back = make_map(values, mixed, acc)
-    residual = residuals(everywhere(back), invert(idx, samples.shape), cleaned)
+    slot, cleaned = invert(idx, coef, templates, samples)
+    residual = residuals(everywhere(back), slot, cleaned)
     return (sky, residual.reshape(blocks, det_local, sample_local))
 
 

time: 65.4 us -> 64.7 us (0.989)
  waiting for transfers between devices: 10.3 us -> 8.69 us
    ppermute x4 -> x3, waiting for transfers between devices: 4.33 us -> 1.8 us  [partners(): return lax.ppermute(x, 'tm', [(i, i ^ bit) for i in range(tm_count)])]
    all_to_all x1, starting transfers between devices: 5.31 us -> 3.95 us  [shards(): got = everywhere(send)]
    ppermute x3, starting transfers between devices: 3.26 us -> 4.48 us  [shards(): lax.ppermute(samples, 'det', [(i, (i + k) % det_count) for i in range(det...]
    ppermute x3, waiting for transfers between devices: 0.01 us -> 1.08 us  [shards(): lax.ppermute(samples, 'det', [(i, (i + k) % det_count) for i in range(det...]
    all_to_all x1, starting transfers between devices: 3.34 us -> 4.41 us  [shards(): values = everywhere(pay)]
    pallas_call x2 -> x3, Pallas kernels: 6.6 us -> 7.08 us  [the longest x1 2.76 us: invert(): pl.pallas_call(invert_kernel, out_shape=(jax.ShapeDtypeStruct(samples.sha...]
    ppermute x4 -> x3, starting transfers between devices: 6.26 us -> 5.89 us  [partners(): return lax.ppermute(x, 'tm', [(i, i ^ bit) for i in range(tm_count)])]
  transfers between devices with their start and end apart: 10 -> 9, of which waited for: 5 -> 4; matrix products, arithmetic and copies ran while one was open for 10% -> 10% of each run, Pallas kernels for 22% -> 23%
where the time goes in v5:
time: 64.7 us; the launch traced here: 64.4 us
  Pallas kernels  24.6 us (38%)
  starting transfers between devices  23.2 us (36%)
  waiting for transfers between devices  8.69 us (13%)
  other arithmetic  6.48 us (10%)
  between operations  0.74 us (1%)
  local copies, waits for them, and re-layouts  0.67 us (1%)
    pallas_call x1, Pallas kernels, make_map(): pl.pallas_call(map_kernel, out_shape=(jax.ShapeDtypeStruct((3, TILE_PIX),...  7.67 us
    pallas_call x1, Pallas kernels, angles(): pl.pallas_call(angles_kernel, out_shape=(jax.ShapeDtypeStruct((3,) + mixe...  6.07 us
    ppermute x3, starting transfers between devices, partners(): return lax.ppermute(x, 'tm', [(i, i ^ bit) for i in range(tm_count)])  5.89 us
    sort x1, other arithmetic, shards(): key, load = lax.sort((key, load), num_keys=1, is_stable=False)  5.68 us
    all_to_all x1, waiting for transfers between devices, shards(): residual = residuals(everywhere(back), slot, cleaned)  4.65 us
    ppermute x3, starting transfers between devices, shards(): lax.ppermute(samples, 'det', [(i, (i + k) % det_count) for i in range(det...  4.48 us
    all_to_all x1, starting transfers between devices, shards(): residual = residuals(everywhere(back), slot, cleaned)  4.48 us
    all_to_all x1, starting transfers between devices, shards(): values = everywhere(pay)  4.41 us
  transfers between devices with their start and end apart: 9, of which 4 were waited for; matrix products, arithmetic and copies ran while one was open for 10% of the time, Pallas kernels for 23%

profile of v5, /device:TPU:0, one launch (start us, length us, event | category | flops | bytes accessed | tf_op | source)
XLA Modules:
  0.0 64.4 jit_solution(9342034186609818965)
XLA Ops:
  0.6 0.0 copy-start.2
  0.6 0.5 collective-permute-start
  1.1 2.6 %collective-permute-start.1 = (f32[32,256]{1,0:T(8,128)}, f32[32,256]{1,0:T(8,128)S(1)}, u32[]{:S(2)}, u32[]{:S(2)}) collective-permute-start(f32[32,256]{1,0:T(8,128)} %bitcast.15), channel_id=1, source_target_pairs={{0,2},{1,3},{2,0},{3,1},{4,6},{5,7},{6,4},{7,5},{8,10},{9,11},{10,... | collective-permute-start | bytes 98312 | tf_op jit(solution)/shard_map/ppermute | solution.py:588
  3.7 1.4 %collective-permute-start.2 = (f32[32,256]{1,0:T(8,128)}, f32[32,256]{1,0:T(8,128)S(1)}, u32[]{:S(2)}, u32[]{:S(2)}) collective-permute-start(f32[32,256]{1,0:T(8,128)} %bitcast.16), channel_id=1, source_target_pairs={{0,3},{1,0},{2,1},{3,2},{4,7},{5,4},{6,5},{7,6},{8,11},{9,8},{10,9... | collective-permute-start | bytes 98312 | tf_op jit(solution)/shard_map/ppermute | solution.py:588
  5.1 0.8 %shift-left_add_fusion.1 = s32[1,32,256]{2,1,0:T(8,128)S(1)} fusion(s32[1,32,256]{2,1,0:T(8,128)} %param.7, s32[1,32,256]{2,1,0:T(8,128)} %param.6), kind=kLoop, calls=%fused_computation.1 | loop fusion | flops 16384 | bytes 98304 | tf_op jit(solution)/shard_map/add | solution.py:596
  5.9 0.0 copy-done.2
  5.9 0.0 copy-start
  5.9 0.0 collective-permute-done.refs_1_
  6.0 0.0 collective-permute-done.1.refs_2_
  6.0 1.1 %collective-permute-done.2.refs_3_ = f32[32,256]{1,0:T(8,128)S(1)} collective-permute-done((f32[32,256]{1,0:T(8,128)}, f32[32,256]{1,0:T(8,128)S(1)}, u32[]{:S(2)}, u32[]{:S(2)}) %collective-permute-start.2) | collective-permute-done | bytes 32800 | tf_op jit(solution)/shard_map/ppermute | solution.py:588
  7.0 0.0 copy-done
  7.0 0.2 modes.1
  7.3 1.5 %collective-permute-start.3 = (f32[8,128]{1,0:T(8,128)S(1)}, f32[8,128]{1,0:T(8,128)S(1)}, u32[]{:S(2)}, u32[]{:S(2)}) collective-permute-start(f32[8,128]{1,0:T(8,128)S(1)} %get-tuple-element.32), channel_id=1, source_target_pairs={{0,4},{4,0},{8,12},{12,8},{16,20},{20,16},{24,28},{28,24},{1,5},{5... | collective-permute-start | bytes 12296 | tf_op jit(solution)/shard_map/ppermute | solution.py:601
  8.8 5.7 %sort.15 = (s32[8192]{0:T(1024)S(1)}, s32[8192]{0:T(1024)S(1)}) sort(s32[8192]{0:T(1024)S(1)} %bitcast.22, s32[8192]{0:T(1024)S(1)} %bitcast.23), dimensions={0}, to_apply=%region_0.0 | sort | flops 106496 | bytes 131072 | tf_op jit(solution)/shard_map/sort | solution.py:605
  14.5 0.0 collective-permute-done.3
  14.5 1.6 %collective-permute-start.4 = (f32[8,128]{1,0:T(8,128)S(1)}, f32[8,128]{1,0:T(8,128)S(1)}, u32[]{:S(2)}, u32[]{:S(2)}) collective-permute-start(f32[8,128]{1,0:T(8,128)S(1)} %add.23), channel_id=1, source_target_pairs={{0,8},{4,12},{8,0},{12,4},{16,24},{20,28},{24,16},{28,20},{1,9},{5... | collective-permute-start | bytes 12296 | tf_op jit(solution)/shard_map/ppermute | solution.py:601
  16.1 0.0 copy-start.1
  16.1 0.7 %copy-done.1 = s32[32]{0:T(128)S(1)} copy-done((s32[32]{0:T(128)S(1)}, s32[32]{0:T(128)}, u32[]{:S(2)}) %copy-start.1) | copy-done | bytes 152
  16.8 1.7 %route.1 = (s32[32,8,128]{2,1,0:T(8,128)}, s32[32,4,128]{2,1,0:T(4,128)S(1)}) custom-call(s32[32]{0:T(128)S(1)} %copy-done.1, s32[64,128]{1,0:T(8,128)S(1)} %bitcast.20, s32[64,128]{1,0:T(8,128)S(1)} %bitcast.21), custom_call_target="tpu_custom_call" | custom-call | tf_op jit(solution)/shard_map/route/pallas_call | solution.py:124
  18.5 0.0 collective-permute-done.4
  18.5 3.9 %all-to-all-start.1 = ((s32[32,8,128]{2,1,0:T(8,128)}), s32[32,8,128]{2,1,0:T(8,128)S(1)}, u32[]{:S(2)}, u32[]{:S(2)}) async-start(s32[32,8,128]{2,1,0:T(8,128)} %get-tuple-element.42), calls=%async_computation.1 | async-start | bytes 262144 | tf_op jit(solution)/shard_map/all_to_all | solution.py:622
  22.4 2.7 %collective-permute-start.5 = (f32[8,128]{1,0:T(8,128)S(1)}, f32[8,128]{1,0:T(8,128)S(1)}, u32[]{:S(2)}, u32[]{:S(2)}) collective-permute-start(f32[8,128]{1,0:T(8,128)S(1)} %add.24.refs_0_), channel_id=1, source_target_pairs={{0,16},{4,20},{8,24},{12,28},{16,0},{20,4},{24,8},{28,12},{1,17},{... | collective-permute-start | bytes 12296 | tf_op jit(solution)/shard_map/ppermute | solution.py:601
  25.2 1.6 %pick.1 = (f32[32,4,128]{2,1,0:T(4,128)S(1)}, f32[16,4,16,256]{3,2,1,0:T(8,128)S(1)}) custom-call(f32[16,256]{1,0:T(8,128)S(1)} %get-tuple-element.26.temp_ref, f32[32,256]{1,0:T(8,128)S(1)} %bitcast.18, s32[32,4,128]{2,1,0:T(4,128)S(1)} %get-tuple-element.35.idx_ref), custom_call_target="tpu_custom_call" | custom-call | tf_op jit(solution)/shard_map/pick/pallas_call | solution.py:172
  26.8 1.8 %collective-permute-done.5.refs_1_ = f32[8,128]{1,0:T(8,128)S(1)} collective-permute-done((f32[8,128]{1,0:T(8,128)S(1)}, f32[8,128]{1,0:T(8,128)S(1)}, u32[]{:S(2)}, u32[]{:S(2)}) %collective-permute-start.5) | collective-permute-done | bytes 4128 | tf_op jit(solution)/shard_map/ppermute | solution.py:601
  28.6 2.7 %clean.1 = (f32[16,32]{1,0:T(8,128)S(1)}, f32[32,4,128]{2,1,0:T(4,128)}) custom-call(f32[32,4,128]{2,1,0:T(4,128)S(1)} %get-tuple-element.36.raw_ref, f32[16,4,16,256]{3,2,1,0:T(8,128)S(1)} %get-tuple-element.37.there_ref, s32[32,4,128]{2,1,0:T(4,128)S(1)} %get-tuple-element.35.idx_ref, f32[8,128]{1,0:T(8,128)S(1)} %add.24.refs_0_, ...), custom_call_target="tpu_custom_call" | custom-call | tf_op jit(solution)/shard_map/clean/pallas_call | solution.py:223
  31.3 0.0 all-to-all-done.1.got_ref
  31.3 4.4 %all-to-all-start = ((f32[32,4,128]{2,1,0:T(4,128)}), f32[32,4,128]{2,1,0:T(4,128)S(1)}, u32[]{:S(2)}, u32[]{:S(2)}) async-start(f32[32,4,128]{2,1,0:T(4,128)} %get-tuple-element.41), calls=%async_computation | async-start | bytes 131072 | tf_op jit(solution)/shard_map/all_to_all | solution.py:627
  35.7 6.1 %angles.1 = (f32[3,4,8,4,128]{4,3,2,1,0:T(4,128)S(1)}, f32[5,152,256]{2,1,0:T(8,128)S(1)}) custom-call(s32[32,8,128]{2,1,0:T(8,128)S(1)} %all-to-all-done.1.got_ref), custom_call_target="tpu_custom_call" | custom-call | tf_op jit(solution)/shard_map/angles/pallas_call | solution.py:361
  41.8 1.2 %all-to-all-done.got_ref = f32[32,4,128]{2,1,0:T(4,128)S(1)} async-done(((f32[32,4,128]{2,1,0:T(4,128)}), f32[32,4,128]{2,1,0:T(4,128)S(1)}, u32[]{:S(2)}, u32[]{:S(2)}) %all-to-all-start) | async-done | bytes 65568 | tf_op jit(solution)/shard_map/all_to_all | solution.py:627
  43.0 7.7 %make_map.1 = (f32[3,32640]{1,0:T(4,128)}, f32[32,4,128]{2,1,0:T(4,128)}) custom-call(f32[32,4,128]{2,1,0:T(4,128)S(1)} %all-to-all-done.got_ref, f32[3,4,8,4,128]{4,3,2,1,0:T(4,128)S(1)} %get-tuple-element.43.mixed_ref, f32[5,152,256]{2,1,0:T(8,128)S(1)} %get-tuple-element.44.acc_ref), custom_call_target="tpu_custom_call" | custom-call | tf_op jit(solution)/shard_map/make_map/pallas_call | solution.py:477
  50.6 4.5 %all-to-all-start.2 = ((f32[32,4,128]{2,1,0:T(4,128)}), f32[32,4,128]{2,1,0:T(4,128)S(1)}, u32[]{:S(2)}, u32[]{:S(2)}) async-start(f32[32,4,128]{2,1,0:T(4,128)} %get-tuple-element.46), calls=%async_computation.2 | async-start | bytes 131072 | tf_op jit(solution)/shard_map/all_to_all | solution.py:630
  55.1 2.8 %invert.1 = (s32[32,256]{1,0:T(8,128)S(1)}, f32[32,256]{1,0:T(8,128)S(1)}) custom-call(s32[32,4,128]{2,1,0:T(4,128)S(1)} %get-tuple-element.35.idx_ref, f32[16,32]{1,0:T(8,128)S(1)} %get-tuple-element.47.coef_ref, f32[16,256]{1,0:T(8,128)S(1)} %get-tuple-element.26.temp_ref, f32[32,256]{1,0:T(8,128)S(1)} %bitcast.19), custom_call_target="tpu_custom_call" | custom-call | tf_op jit(solution)/shard_map/invert/pallas_call | solution.py:537
  57.9 4.6 %all-to-all-done.2.got_ref = f32[32,4,128]{2,1,0:T(4,128)S(1)} async-done(((f32[32,4,128]{2,1,0:T(4,128)}), f32[32,4,128]{2,1,0:T(4,128)S(1)}, u32[]{:S(2)}, u32[]{:S(2)}) %all-to-all-start.2) | async-done | bytes 65568 | tf_op jit(solution)/shard_map/all_to_all | solution.py:630
  62.5 1.9 %residuals.1 = f32[32,256]{1,0:T(8,128)} custom-call(f32[32,4,128]{2,1,0:T(4,128)S(1)} %all-to-all-done.2.got_ref, s32[32,256]{1,0:T(8,128)S(1)} %get-tuple-element.48.slot_ref, f32[32,256]{1,0:T(8,128)S(1)} %get-tuple-element.49.clean_ref), custom_call_target="tpu_custom_call" | custom-call | tf_op jit(solution)/shard_map/residuals/pallas_call | solution.py:567
  (3 shorter events, 0.0 us)
Async XLA Ops:
  0.6 5.3 %copy-start.2 = (s32[1,32,256]{2,1,0:T(8,128)S(1)}, s32[1,32,256]{2,1,0:T(8,128)}, u32[]{:S(2)}) copy-start(s32[1,32,256]{2,1,0:T(8,128)} %param.8) | copy-start | bytes 98308
  0.6 5.3 %collective-permute-start = (f32[32,256]{1,0:T(8,128)}, f32[32,256]{1,0:T(8,128)S(1)}, u32[]{:S(2)}, u32[]{:S(2)}) collective-permute-start(f32[32,256]{1,0:T(8,128)} %bitcast.14), channel_id=1, source_target_pairs={{0,1},{1,2},{2,3},{3,0},{4,5},{5,6},{6,7},{7,4},{8,9},{9,10},{10,1... | collective-permute-start | bytes 98312 | tf_op jit(solution)/shard_map/ppermute | solution.py:588
  1.1 4.8 %collective-permute-start.1 = (f32[32,256]{1,0:T(8,128)}, f32[32,256]{1,0:T(8,128)S(1)}, u32[]{:S(2)}, u32[]{:S(2)}) collective-permute-start(f32[32,256]{1,0:T(8,128)} %bitcast.15), channel_id=1, source_target_pairs={{0,2},{1,3},{2,0},{3,1},{4,6},{5,7},{6,4},{7,5},{8,10},{9,11},{10,... | collective-permute-start | bytes 98312 | tf_op jit(solution)/shard_map/ppermute | solution.py:588
  3.7 3.3 %collective-permute-start.2 = (f32[32,256]{1,0:T(8,128)}, f32[32,256]{1,0:T(8,128)S(1)}, u32[]{:S(2)}, u32[]{:S(2)}) collective-permute-start(f32[32,256]{1,0:T(8,128)} %bitcast.16), channel_id=1, source_target_pairs={{0,3},{1,0},{2,1},{3,2},{4,7},{5,4},{6,5},{7,6},{8,11},{9,8},{10,9... | collective-permute-start | bytes 98312 | tf_op jit(solution)/shard_map/ppermute | solution.py:588
  5.9 1.1 %copy-start = (f32[1,32,256]{2,1,0:T(8,128)S(1)}, f32[1,32,256]{2,1,0:T(8,128)}, u32[]{:S(2)}) copy-start(f32[1,32,256]{2,1,0:T(8,128)} %param.5) | copy-start | bytes 98308
  7.3 7.2 %collective-permute-start.3 = (f32[8,128]{1,0:T(8,128)S(1)}, f32[8,128]{1,0:T(8,128)S(1)}, u32[]{:S(2)}, u32[]{:S(2)}) collective-permute-start(f32[8,128]{1,0:T(8,128)S(1)} %get-tuple-element.32), channel_id=1, source_target_pairs={{0,4},{4,0},{8,12},{12,8},{16,20},{20,16},{24,28},{28,24},{1,5},{5... | collective-permute-start | bytes 12296 | tf_op jit(solution)/shard_map/ppermute | solution.py:601
  14.5 4.0 %collective-permute-start.4 = (f32[8,128]{1,0:T(8,128)S(1)}, f32[8,128]{1,0:T(8,128)S(1)}, u32[]{:S(2)}, u32[]{:S(2)}) collective-permute-start(f32[8,128]{1,0:T(8,128)S(1)} %add.23), channel_id=1, source_target_pairs={{0,8},{4,12},{8,0},{12,4},{16,24},{20,28},{24,16},{28,20},{1,9},{5... | collective-permute-start | bytes 12296 | tf_op jit(solution)/shard_map/ppermute | solution.py:601
  16.1 0.7 %copy-start.1 = (s32[32]{0:T(128)S(1)}, s32[32]{0:T(128)}, u32[]{:S(2)}) copy-start(s32[32]{0:T(128)} %owner_ref.1) | copy-start | bytes 388
  18.5 12.8 %all-to-all-start.1 = ((s32[32,8,128]{2,1,0:T(8,128)}), s32[32,8,128]{2,1,0:T(8,128)S(1)}, u32[]{:S(2)}, u32[]{:S(2)}) async-start(s32[32,8,128]{2,1,0:T(8,128)} %get-tuple-element.42), calls=%async_computation.1 | async-start | bytes 262144 | tf_op jit(solution)/shard_map/all_to_all | solution.py:622
  22.4 6.2 %collective-permute-start.5 = (f32[8,128]{1,0:T(8,128)S(1)}, f32[8,128]{1,0:T(8,128)S(1)}, u32[]{:S(2)}, u32[]{:S(2)}) collective-permute-start(f32[8,128]{1,0:T(8,128)S(1)} %add.24.refs_0_), channel_id=1, source_target_pairs={{0,16},{4,20},{8,24},{12,28},{16,0},{20,4},{24,8},{28,12},{1,17},{... | collective-permute-start | bytes 12296 | tf_op jit(solution)/shard_map/ppermute | solution.py:601
  31.3 11.6 %all-to-all-start = ((f32[32,4,128]{2,1,0:T(4,128)}), f32[32,4,128]{2,1,0:T(4,128)S(1)}, u32[]{:S(2)}, u32[]{:S(2)}) async-start(f32[32,4,128]{2,1,0:T(4,128)} %get-tuple-element.41), calls=%async_computation | async-start | bytes 131072 | tf_op jit(solution)/shard_map/all_to_all | solution.py:627
  50.6 11.9 %all-to-all-start.2 = ((f32[32,4,128]{2,1,0:T(4,128)}), f32[32,4,128]{2,1,0:T(4,128)S(1)}, u32[]{:S(2)}, u32[]{:S(2)}) async-start(f32[32,4,128]{2,1,0:T(4,128)} %get-tuple-element.46), calls=%async_computation.2 | async-start | bytes 131072 | tf_op jit(solution)/shard_map/all_to_all | solution.py:630

commit v6 on v5

--- a/solution.py
+++ b/solution.py
@@ -136,6 +136,25 @@
         compiler_params=pltpu.CompilerParams(vmem_limit_bytes=VMEM_LIMIT),
         name="route",
     )(owner_map, key.reshape(depth, LANES), load.reshape(depth, LANES))
+
+
+def sky_kernel(stokes_ref, sky_ref):
+    for row in range(HI):
+        first = row * LO
+        width = min(LO, TILE_PIX - first)
+        for q in range(3):
+            sky_ref[q : q + 1, first : first + width] = stokes_ref[q, row : row + 1, :width]
+
+
+def lay_out(stokes):
+    return pl.pallas_call(
+        sky_kernel,
+        out_shape=jax.ShapeDtypeStruct((3, TILE_PIX), F32),
+        in_specs=[VMEM_SPEC],
+        out_specs=VMEM_SPEC,
+        compiler_params=pltpu.CompilerParams(vmem_limit_bytes=VMEM_LIMIT),
+        name="lay_out",
+    )(stokes)
 
 
 def pair_row(ref, pair, r):
@@ -399,7 +418,7 @@
 
 
 def map_kernel(
-    got_ref, mixed_ref, acc_ref, sky_ref, back_ref, pix_ref, parts_ref, sum_ref, table_vmem, table, sem
+    got_ref, mixed_ref, acc_ref, sum_ref, back_ref, pix_ref, parts_ref, table_vmem, table, sem
 ):
     owners, rows = got_ref.shape[0], got_ref.shape[1]
     groups = owners // WAYS // GROUP
@@ -433,10 +452,6 @@
         stokes = solve_stokes(sums)
         for q in range(3):
             sum_ref[q, at, :] = stokes[q]
-            for i in range(8):
-                first = (block * 8 + i) * LO
-                width = min(LO, TILE_PIX - first)
-                sky_ref[q : q + 1, first : first + width] = stokes[q][i : i + 1, :width]
 
     def look(run, group, r, first, fresh):
         pixel = chunk_row(pix_ref, run, group, r)
@@ -477,7 +492,7 @@
     return pl.pallas_call(
         map_kernel,
         out_shape=(
-            jax.ShapeDtypeStruct((3, TILE_PIX), F32),
+            jax.ShapeDtypeStruct((3, HIP, LO), F32),
             jax.ShapeDtypeStruct(got.shape, F32),
         ),
         in_specs=[VMEM_SPEC] * 3,
@@ -485,7 +500,6 @@
         scratch_shapes=[
             pltpu.VMEM(mixed.shape[1:], jnp.int32),
             pltpu.VMEM((sum(VALUE_TERMS),) + mixed.shape[1:], F32),
-            pltpu.VMEM((len(VALUE_TERMS), HIP, LO), F32),
             pltpu.VMEM((rows, LANES), jnp.int32),
             pltpu.SMEM((rows, LANES), jnp.int32),
             pltpu.SemaphoreType.DMA,
@@ -600,21 +614,18 @@
     def partners(x, bit):
         return lax.ppermute(x, "tm", [(i, i ^ bit) for i in range(tm_count)])
 
+    bits = [1 << i for i in reversed(range(tm_count.bit_length() - 1))]
     key, load, products = lax.optimization_barrier((key, load, products))
-    found = partners(products, 1)
+    found = partners(products, bits[0])
     key, load = lax.sort((key, load), num_keys=1, is_stable=False)
     key, load, found = lax.optimization_barrier((key, load, found))
     products = products + found
-    found = partners(products, 2)
+    found = partners(products, bits[1])
     send, idx = route(key, load, owner_map, owners, rows)
     send, found = lax.optimization_barrier((send, found))
-    products = products + found
-    bit = 4
-    while bit < tm_count:
+    for bit in bits[2:]:
+        products = products + found
         found = partners(products, bit)
-        bit *= 2
-        if bit < tm_count:
-            products = products + found
     products = [products, found]
     everywhere = functools.partial(
         lax.all_to_all, axis_name=("tm", "det"), split_axis=0, concat_axis=0, tiled=True
@@ -625,10 +636,10 @@
     mixed, acc = angles(got, rows)
 
     values = everywhere(pay)
-    sky, back = make_map(values, mixed, acc)
+    stokes, back = make_map(values, mixed, acc)
     slot, cleaned = invert(idx, coef, templates, samples)
     residual = residuals(everywhere(back), slot, cleaned)
-    return (sky, residual.reshape(blocks, det_local, sample_local))
+    return (lay_out(stokes), residual.reshape(blocks, det_local, sample_local))
 
 
 def solution(mesh):

time: 64.7 us -> 63.7 us (0.985)
  starting transfers between devices: 23.2 us -> 21.9 us
  Pallas kernels: 24.6 us -> 25.5 us
    all_to_all x1, waiting for transfers between devices: 0.01 us -> 1.86 us  [shards(): got = everywhere(send)]
    ppermute x3, waiting for transfers between devices: 1.8 us -> 0.21 us  [partners(): return lax.ppermute(x, 'tm', [(i, i ^ bit) for i in range(tm_count)])]
    all_to_all x1, starting transfers between devices: 3.95 us -> 2.85 us  [shards(): got = everywhere(send)]
    all_to_all x1, waiting for transfers between devices: 4.65 us -> 3.65 us  [shards(): residual = residuals(everywhere(back), slot, cleaned)]
    pallas_call x1 -> x2, Pallas kernels: 7.67 us -> 8.51 us  [the longest x1 7.51 us: make_map(): pl.pallas_call(map_kernel, out_shape=(jax.ShapeDtypeStruct((3, HIP, LO),...]
  transfers between devices with their start and end apart: 9 -> 9, of which waited for: 4 -> 5; matrix products, arithmetic and copies ran while one was open for 10% -> 10% of each run, Pallas kernels for 23% -> 25%
where the time goes in v6:
time: 63.7 us; the launch traced here: 63.4 us
  Pallas kernels  25.5 us (40%)
  starting transfers between devices  21.9 us (34%)
  waiting for transfers between devices  8.13 us (13%)
  other arithmetic  6.48 us (10%)
  between operations  0.74 us (1%)
  local copies, waits for them, and re-layouts  0.67 us (1%)
    pallas_call x1, Pallas kernels, make_map(): pl.pallas_call(map_kernel, out_shape=(jax.ShapeDtypeStruct((3, HIP, LO),...  7.51 us
    ppermute x3, starting transfers between devices, partners(): return lax.ppermute(x, 'tm', [(i, i ^ bit) for i in range(tm_count)])  6.08 us
    pallas_call x1, Pallas kernels, angles(): pl.pallas_call(angles_kernel, out_shape=(jax.ShapeDtypeStruct((3,) + mixe...  6.07 us
    sort x1, other arithmetic, shards(): key, load = lax.sort((key, load), num_keys=1, is_stable=False)  5.68 us
    all_to_all x1, starting transfers between devices, shards(): residual = residuals(everywhere(back), slot, cleaned)  4.56 us
    ppermute x3, starting transfers between devices, shards(): lax.ppermute(samples, 'det', [(i, (i + k) % det_count) for i in range(det...  4.48 us
    all_to_all x1, starting transfers between devices, shards(): values = everywhere(pay)  3.98 us
    all_to_all x1, waiting for transfers between devices, shards(): residual = residuals(everywhere(back), slot, cleaned)  3.65 us
  transfers between devices with their start and end apart: 9, of which 5 were waited for; matrix products, arithmetic and copies ran while one was open for 10% of the time, Pallas kernels for 25%

profile of v6, /device:TPU:0, one launch (start us, length us, event | category | flops | bytes accessed | tf_op | source)
XLA Modules:
  0.0 63.4 jit_solution(17197757068875877814)
XLA Ops:
  0.6 0.0 copy-start.2
  0.6 0.5 collective-permute-start
  1.1 2.6 %collective-permute-start.1 = (f32[32,256]{1,0:T(8,128)}, f32[32,256]{1,0:T(8,128)S(1)}, u32[]{:S(2)}, u32[]{:S(2)}) collective-permute-start(f32[32,256]{1,0:T(8,128)} %bitcast.15), channel_id=1, source_target_pairs={{0,2},{1,3},{2,0},{3,1},{4,6},{5,7},{6,4},{7,5},{8,10},{9,11},{10,... | collective-permute-start | bytes 98312 | tf_op jit(solution)/shard_map/ppermute | solution.py:602
  3.7 1.4 %collective-permute-start.2 = (f32[32,256]{1,0:T(8,128)}, f32[32,256]{1,0:T(8,128)S(1)}, u32[]{:S(2)}, u32[]{:S(2)}) collective-permute-start(f32[32,256]{1,0:T(8,128)} %bitcast.16), channel_id=1, source_target_pairs={{0,3},{1,0},{2,1},{3,2},{4,7},{5,4},{6,5},{7,6},{8,11},{9,8},{10,9... | collective-permute-start | bytes 98312 | tf_op jit(solution)/shard_map/ppermute | solution.py:602
  5.1 0.8 %shift-left_add_fusion.1 = s32[1,32,256]{2,1,0:T(8,128)S(1)} fusion(s32[1,32,256]{2,1,0:T(8,128)} %param.7, s32[1,32,256]{2,1,0:T(8,128)} %param.6), kind=kLoop, calls=%fused_computation.1 | loop fusion | flops 16384 | bytes 98304 | tf_op jit(solution)/shard_map/add | solution.py:610
  5.9 0.0 copy-done.2
  5.9 0.0 copy-start
  5.9 0.0 collective-permute-done.refs_1_
  6.0 0.0 collective-permute-done.1.refs_2_
  6.0 1.1 %collective-permute-done.2.refs_3_ = f32[32,256]{1,0:T(8,128)S(1)} collective-permute-done((f32[32,256]{1,0:T(8,128)}, f32[32,256]{1,0:T(8,128)S(1)}, u32[]{:S(2)}, u32[]{:S(2)}) %collective-permute-start.2) | collective-permute-done | bytes 32800 | tf_op jit(solution)/shard_map/ppermute | solution.py:602
  7.0 0.0 copy-done
  7.0 0.2 modes.1
  7.3 2.6 %collective-permute-start.3 = (f32[8,128]{1,0:T(8,128)S(1)}, f32[8,128]{1,0:T(8,128)S(1)}, u32[]{:S(2)}, u32[]{:S(2)}) collective-permute-start(f32[8,128]{1,0:T(8,128)S(1)} %get-tuple-element.32), channel_id=1, source_target_pairs={{0,16},{4,20},{8,24},{12,28},{16,0},{20,4},{24,8},{28,12},{1,17},{... | collective-permute-start | bytes 12296 | tf_op jit(solution)/shard_map/ppermute | solution.py:615
  9.9 5.7 %sort.15 = (s32[8192]{0:T(1024)S(1)}, s32[8192]{0:T(1024)S(1)}) sort(s32[8192]{0:T(1024)S(1)} %bitcast.22, s32[8192]{0:T(1024)S(1)} %bitcast.23), dimensions={0}, to_apply=%region_0.0 | sort | flops 106496 | bytes 131072 | tf_op jit(solution)/shard_map/sort | solution.py:620
  15.5 0.0 collective-permute-done.3
  15.6 1.6 %collective-permute-start.4 = (f32[8,128]{1,0:T(8,128)S(1)}, f32[8,128]{1,0:T(8,128)S(1)}, u32[]{:S(2)}, u32[]{:S(2)}) collective-permute-start(f32[8,128]{1,0:T(8,128)S(1)} %add.23), channel_id=1, source_target_pairs={{0,8},{4,12},{8,0},{12,4},{16,24},{20,28},{24,16},{28,20},{1,9},{5... | collective-permute-start | bytes 12296 | tf_op jit(solution)/shard_map/ppermute | solution.py:615
  17.2 0.0 copy-start.1
  17.2 0.7 %copy-done.1 = s32[32]{0:T(128)S(1)} copy-done((s32[32]{0:T(128)S(1)}, s32[32]{0:T(128)}, u32[]{:S(2)}) %copy-start.1) | copy-done | bytes 152
  17.9 1.7 %route.1 = (s32[32,8,128]{2,1,0:T(8,128)}, s32[32,4,128]{2,1,0:T(4,128)S(1)}) custom-call(s32[32]{0:T(128)S(1)} %copy-done.1, s32[64,128]{1,0:T(8,128)S(1)} %bitcast.20, s32[64,128]{1,0:T(8,128)S(1)} %bitcast.21), custom_call_target="tpu_custom_call" | custom-call | tf_op jit(solution)/shard_map/route/pallas_call | solution.py:124
  19.6 0.0 collective-permute-done.4
  19.6 2.8 %all-to-all-start.1 = ((s32[32,8,128]{2,1,0:T(8,128)}), s32[32,8,128]{2,1,0:T(8,128)S(1)}, u32[]{:S(2)}, u32[]{:S(2)}) async-start(s32[32,8,128]{2,1,0:T(8,128)} %get-tuple-element.42), calls=%async_computation.1 | async-start | bytes 262144 | tf_op jit(solution)/shard_map/all_to_all | solution.py:633
  22.4 1.8 %collective-permute-start.5 = (f32[8,128]{1,0:T(8,128)S(1)}, f32[8,128]{1,0:T(8,128)S(1)}, u32[]{:S(2)}, u32[]{:S(2)}) collective-permute-start(f32[8,128]{1,0:T(8,128)S(1)} %add.24.refs_0_), channel_id=1, source_target_pairs={{0,4},{4,0},{8,12},{12,8},{16,20},{20,16},{24,28},{28,24},{1,5},{5... | collective-permute-start | bytes 12296 | tf_op jit(solution)/shard_map/ppermute | solution.py:615
  24.3 1.6 %pick.1 = (f32[32,4,128]{2,1,0:T(4,128)S(1)}, f32[16,4,16,256]{3,2,1,0:T(8,128)S(1)}) custom-call(f32[16,256]{1,0:T(8,128)S(1)} %get-tuple-element.26.temp_ref, f32[32,256]{1,0:T(8,128)S(1)} %bitcast.18, s32[32,4,128]{2,1,0:T(4,128)S(1)} %get-tuple-element.35.idx_ref), custom_call_target="tpu_custom_call" | custom-call | tf_op jit(solution)/shard_map/pick/pallas_call | solution.py:191
  25.9 0.2 collective-permute-done.5.refs_1_
  26.1 2.7 %clean.1 = (f32[16,32]{1,0:T(8,128)S(1)}, f32[32,4,128]{2,1,0:T(4,128)}) custom-call(f32[32,4,128]{2,1,0:T(4,128)S(1)} %get-tuple-element.36.raw_ref, f32[16,4,16,256]{3,2,1,0:T(8,128)S(1)} %get-tuple-element.37.there_ref, s32[32,4,128]{2,1,0:T(4,128)S(1)} %get-tuple-element.35.idx_ref, f32[8,128]{1,0:T(8,128)S(1)} %add.24.refs_0_, ...), custom_call_target="tpu_custom_call" | custom-call | tf_op jit(solution)/shard_map/clean/pallas_call | solution.py:242
  28.8 1.9 %all-to-all-done.1.got_ref = s32[32,8,128]{2,1,0:T(8,128)S(1)} async-done(((s32[32,8,128]{2,1,0:T(8,128)}), s32[32,8,128]{2,1,0:T(8,128)S(1)}, u32[]{:S(2)}, u32[]{:S(2)}) %all-to-all-start.1) | async-done | bytes 131104 | tf_op jit(solution)/shard_map/all_to_all | solution.py:633
  30.7 4.0 %all-to-all-start = ((f32[32,4,128]{2,1,0:T(4,128)}), f32[32,4,128]{2,1,0:T(4,128)S(1)}, u32[]{:S(2)}, u32[]{:S(2)}) async-start(f32[32,4,128]{2,1,0:T(4,128)} %get-tuple-element.41), calls=%async_computation | async-start | bytes 131072 | tf_op jit(solution)/shard_map/all_to_all | solution.py:638
  34.6 6.1 %angles.1 = (f32[3,4,8,4,128]{4,3,2,1,0:T(4,128)S(1)}, f32[5,152,256]{2,1,0:T(8,128)S(1)}) custom-call(s32[32,8,128]{2,1,0:T(8,128)S(1)} %all-to-all-done.1.got_ref), custom_call_target="tpu_custom_call" | custom-call | tf_op jit(solution)/shard_map/angles/pallas_call | solution.py:380
  40.7 1.3 %all-to-all-done.got_ref = f32[32,4,128]{2,1,0:T(4,128)S(1)} async-done(((f32[32,4,128]{2,1,0:T(4,128)}), f32[32,4,128]{2,1,0:T(4,128)S(1)}, u32[]{:S(2)}, u32[]{:S(2)}) %all-to-all-start) | async-done | bytes 65568 | tf_op jit(solution)/shard_map/all_to_all | solution.py:638
  42.1 7.5 %make_map.1 = (f32[3,152,256]{2,1,0:T(8,128)S(1)}, f32[32,4,128]{2,1,0:T(4,128)}) custom-call(f32[32,4,128]{2,1,0:T(4,128)S(1)} %all-to-all-done.got_ref, f32[3,4,8,4,128]{4,3,2,1,0:T(4,128)S(1)} %get-tuple-element.43.mixed_ref, f32[5,152,256]{2,1,0:T(8,128)S(1)} %get-tuple-element.44.acc_ref), custom_call_target="tpu_custom_call" | custom-call | tf_op jit(solution)/shard_map/make_map/pallas_call | solution.py:492
  49.6 4.6 %all-to-all-start.2 = ((f32[32,4,128]{2,1,0:T(4,128)}), f32[32,4,128]{2,1,0:T(4,128)S(1)}, u32[]{:S(2)}, u32[]{:S(2)}) async-start(f32[32,4,128]{2,1,0:T(4,128)} %get-tuple-element.46), calls=%async_computation.2 | async-start | bytes 131072 | tf_op jit(solution)/shard_map/all_to_all | solution.py:641
  54.1 2.8 %invert.1 = (s32[32,256]{1,0:T(8,128)S(1)}, f32[32,256]{1,0:T(8,128)S(1)}) custom-call(s32[32,4,128]{2,1,0:T(4,128)S(1)} %get-tuple-element.35.idx_ref, f32[16,32]{1,0:T(8,128)S(1)} %get-tuple-element.47.coef_ref, f32[16,256]{1,0:T(8,128)S(1)} %get-tuple-element.26.temp_ref, f32[32,256]{1,0:T(8,128)S(1)} %bitcast.19), custom_call_target="tpu_custom_call" | custom-call | tf_op jit(solution)/shard_map/invert/pallas_call | solution.py:551
  56.9 1.0 %lay_out.1 = f32[3,32640]{1,0:T(4,128)} custom-call(f32[3,152,256]{2,1,0:T(8,128)S(1)} %get-tuple-element.45.stokes_ref), custom_call_target="tpu_custom_call" | custom-call | tf_op jit(solution)/shard_map/lay_out/pallas_call | solution.py:150
  57.9 3.7 %all-to-all-done.2.got_ref = f32[32,4,128]{2,1,0:T(4,128)S(1)} async-done(((f32[32,4,128]{2,1,0:T(4,128)}), f32[32,4,128]{2,1,0:T(4,128)S(1)}, u32[]{:S(2)}, u32[]{:S(2)}) %all-to-all-start.2) | async-done | bytes 65568 | tf_op jit(solution)/shard_map/all_to_all | solution.py:641
  61.5 1.9 %residuals.1 = f32[32,256]{1,0:T(8,128)} custom-call(f32[32,4,128]{2,1,0:T(4,128)S(1)} %all-to-all-done.2.got_ref, s32[32,256]{1,0:T(8,128)S(1)} %get-tuple-element.48.slot_ref, f32[32,256]{1,0:T(8,128)S(1)} %get-tuple-element.49.clean_ref), custom_call_target="tpu_custom_call" | custom-call | tf_op jit(solution)/shard_map/residuals/pallas_call | solution.py:581
  (3 shorter events, 0.0 us)
Async XLA Ops:
  0.6 5.3 %copy-start.2 = (s32[1,32,256]{2,1,0:T(8,128)S(1)}, s32[1,32,256]{2,1,0:T(8,128)}, u32[]{:S(2)}) copy-start(s32[1,32,256]{2,1,0:T(8,128)} %param.8) | copy-start | bytes 98308
  0.6 5.3 %collective-permute-start = (f32[32,256]{1,0:T(8,128)}, f32[32,256]{1,0:T(8,128)S(1)}, u32[]{:S(2)}, u32[]{:S(2)}) collective-permute-start(f32[32,256]{1,0:T(8,128)} %bitcast.14), channel_id=1, source_target_pairs={{0,1},{1,2},{2,3},{3,0},{4,5},{5,6},{6,7},{7,4},{8,9},{9,10},{10,1... | collective-permute-start | bytes 98312 | tf_op jit(solution)/shard_map/ppermute | solution.py:602
  1.1 4.8 %collective-permute-start.1 = (f32[32,256]{1,0:T(8,128)}, f32[32,256]{1,0:T(8,128)S(1)}, u32[]{:S(2)}, u32[]{:S(2)}) collective-permute-start(f32[32,256]{1,0:T(8,128)} %bitcast.15), channel_id=1, source_target_pairs={{0,2},{1,3},{2,0},{3,1},{4,6},{5,7},{6,4},{7,5},{8,10},{9,11},{10,... | collective-permute-start | bytes 98312 | tf_op jit(solution)/shard_map/ppermute | solution.py:602
  3.7 3.3 %collective-permute-start.2 = (f32[32,256]{1,0:T(8,128)}, f32[32,256]{1,0:T(8,128)S(1)}, u32[]{:S(2)}, u32[]{:S(2)}) collective-permute-start(f32[32,256]{1,0:T(8,128)} %bitcast.16), channel_id=1, source_target_pairs={{0,3},{1,0},{2,1},{3,2},{4,7},{5,4},{6,5},{7,6},{8,11},{9,8},{10,9... | collective-permute-start | bytes 98312 | tf_op jit(solution)/shard_map/ppermute | solution.py:602
  5.9 1.1 %copy-start = (f32[1,32,256]{2,1,0:T(8,128)S(1)}, f32[1,32,256]{2,1,0:T(8,128)}, u32[]{:S(2)}) copy-start(f32[1,32,256]{2,1,0:T(8,128)} %param.5) | copy-start | bytes 98308
  7.3 8.3 %collective-permute-start.3 = (f32[8,128]{1,0:T(8,128)S(1)}, f32[8,128]{1,0:T(8,128)S(1)}, u32[]{:S(2)}, u32[]{:S(2)}) collective-permute-start(f32[8,128]{1,0:T(8,128)S(1)} %get-tuple-element.32), channel_id=1, source_target_pairs={{0,16},{4,20},{8,24},{12,28},{16,0},{20,4},{24,8},{28,12},{1,17},{... | collective-permute-start | bytes 12296 | tf_op jit(solution)/shard_map/ppermute | solution.py:615
  15.6 4.0 %collective-permute-start.4 = (f32[8,128]{1,0:T(8,128)S(1)}, f32[8,128]{1,0:T(8,128)S(1)}, u32[]{:S(2)}, u32[]{:S(2)}) collective-permute-start(f32[8,128]{1,0:T(8,128)S(1)} %add.23), channel_id=1, source_target_pairs={{0,8},{4,12},{8,0},{12,4},{16,24},{20,28},{24,16},{28,20},{1,9},{5... | collective-permute-start | bytes 12296 | tf_op jit(solution)/shard_map/ppermute | solution.py:615
  17.2 0.7 %copy-start.1 = (s32[32]{0:T(128)S(1)}, s32[32]{0:T(128)}, u32[]{:S(2)}) copy-start(s32[32]{0:T(128)} %owner_ref.1) | copy-start | bytes 388
  19.6 11.1 %all-to-all-start.1 = ((s32[32,8,128]{2,1,0:T(8,128)}), s32[32,8,128]{2,1,0:T(8,128)S(1)}, u32[]{:S(2)}, u32[]{:S(2)}) async-start(s32[32,8,128]{2,1,0:T(8,128)} %get-tuple-element.42), calls=%async_computation.1 | async-start | bytes 262144 | tf_op jit(solution)/shard_map/all_to_all | solution.py:633
  22.4 3.7 %collective-permute-start.5 = (f32[8,128]{1,0:T(8,128)S(1)}, f32[8,128]{1,0:T(8,128)S(1)}, u32[]{:S(2)}, u32[]{:S(2)}) collective-permute-start(f32[8,128]{1,0:T(8,128)S(1)} %add.24.refs_0_), channel_id=1, source_target_pairs={{0,4},{4,0},{8,12},{12,8},{16,20},{20,16},{24,28},{28,24},{1,5},{5... | collective-permute-start | bytes 12296 | tf_op jit(solution)/shard_map/ppermute | solution.py:615
  30.7 11.4 %all-to-all-start = ((f32[32,4,128]{2,1,0:T(4,128)}), f32[32,4,128]{2,1,0:T(4,128)S(1)}, u32[]{:S(2)}, u32[]{:S(2)}) async-start(f32[32,4,128]{2,1,0:T(4,128)} %get-tuple-element.41), calls=%async_computation | async-start | bytes 131072 | tf_op jit(solution)/shard_map/all_to_all | solution.py:638
  49.6 12.0 %all-to-all-start.2 = ((f32[32,4,128]{2,1,0:T(4,128)}), f32[32,4,128]{2,1,0:T(4,128)S(1)}, u32[]{:S(2)}, u32[]{:S(2)}) async-start(f32[32,4,128]{2,1,0:T(4,128)} %get-tuple-element.46), calls=%async_computation.2 | async-start | bytes 131072 | tf_op jit(solution)/shard_map/all_to_all | solution.py:641

commit v7 on v6

--- a/solution.py
+++ b/solution.py
@@ -293,7 +293,7 @@
 
         return 0
 
-    lax.fori_loop(0, groups * WAYS, step, 0)
+    lax.fori_loop(0, groups * WAYS, step, 0, unroll=2)
 
 
 def windows_of(pix_ref, groups, rows):

time: 63.7 us -> 64.1 us (level)
  no operation moved by 1% of the time
where the time goes in v7:
time: 64.1 us; the launch traced here: 63.5 us
  Pallas kernels  25.6 us (40%)
  starting transfers between devices  22.4 us (35%)
  waiting for transfers between devices  7.62 us (12%)
  other arithmetic  6.48 us (10%)
  between operations  0.75 us (1%)
  local copies, waits for them, and re-layouts  0.67 us (1%)
    pallas_call x1, Pallas kernels, make_map(): pl.pallas_call(map_kernel, out_shape=(jax.ShapeDtypeStruct((3, HIP, LO),...  7.54 us
    pallas_call x1, Pallas kernels, angles(): pl.pallas_call(angles_kernel, out_shape=(jax.ShapeDtypeStruct((3,) + mixe...  6.19 us
    ppermute x3, starting transfers between devices, partners(): return lax.ppermute(x, 'tm', [(i, i ^ bit) for i in range(tm_count)])  6.08 us
    sort x1, other arithmetic, shards(): key, load = lax.sort((key, load), num_keys=1, is_stable=False)  5.68 us
    all_to_all x1, starting transfers between devices, shards(): residual = residuals(everywhere(back), slot, cleaned)  4.85 us
    ppermute x3, starting transfers between devices, shards(): lax.ppermute(samples, 'det', [(i, (i + k) % det_count) for i in range(det...  4.48 us
    all_to_all x1, starting transfers between devices, shards(): values = everywhere(pay)  4.16 us
    all_to_all x1, waiting for transfers between devices, shards(): residual = residuals(everywhere(back), slot, cleaned)  3.43 us
  transfers between devices with their start and end apart: 9, of which 5 were waited for; matrix products, arithmetic and copies ran while one was open for 10% of the time, Pallas kernels for 25%

profile of v7, /device:TPU:0, one launch (start us, length us, event | category | flops | bytes accessed | tf_op | source)
XLA Modules:
  0.0 63.5 jit_solution(11584353817134004599)
XLA Ops:
  0.6 0.0 copy-start.2
  0.6 0.5 collective-permute-start
  1.1 2.6 %collective-permute-start.1 = (f32[32,256]{1,0:T(8,128)}, f32[32,256]{1,0:T(8,128)S(1)}, u32[]{:S(2)}, u32[]{:S(2)}) collective-permute-start(f32[32,256]{1,0:T(8,128)} %bitcast.15), channel_id=1, source_target_pairs={{0,2},{1,3},{2,0},{3,1},{4,6},{5,7},{6,4},{7,5},{8,10},{9,11},{10,... | collective-permute-start | bytes 98312 | tf_op jit(solution)/shard_map/ppermute | solution.py:602
  3.7 1.4 %collective-permute-start.2 = (f32[32,256]{1,0:T(8,128)}, f32[32,256]{1,0:T(8,128)S(1)}, u32[]{:S(2)}, u32[]{:S(2)}) collective-permute-start(f32[32,256]{1,0:T(8,128)} %bitcast.16), channel_id=1, source_target_pairs={{0,3},{1,0},{2,1},{3,2},{4,7},{5,4},{6,5},{7,6},{8,11},{9,8},{10,9... | collective-permute-start | bytes 98312 | tf_op jit(solution)/shard_map/ppermute | solution.py:602
  5.1 0.8 %shift-left_add_fusion.1 = s32[1,32,256]{2,1,0:T(8,128)S(1)} fusion(s32[1,32,256]{2,1,0:T(8,128)} %param.7, s32[1,32,256]{2,1,0:T(8,128)} %param.6), kind=kLoop, calls=%fused_computation.1 | loop fusion | flops 16384 | bytes 98304 | tf_op jit(solution)/shard_map/add | solution.py:610
  5.9 0.0 copy-done.2
  5.9 0.0 copy-start
  5.9 0.0 collective-permute-done.refs_1_
  6.0 0.0 collective-permute-done.1.refs_2_
  6.0 1.1 %collective-permute-done.2.refs_3_ = f32[32,256]{1,0:T(8,128)S(1)} collective-permute-done((f32[32,256]{1,0:T(8,128)}, f32[32,256]{1,0:T(8,128)S(1)}, u32[]{:S(2)}, u32[]{:S(2)}) %collective-permute-start.2) | collective-permute-done | bytes 32800 | tf_op jit(solution)/shard_map/ppermute | solution.py:602
  7.0 0.0 copy-done
  7.0 0.2 modes.1
  7.3 2.6 %collective-permute-start.3 = (f32[8,128]{1,0:T(8,128)S(1)}, f32[8,128]{1,0:T(8,128)S(1)}, u32[]{:S(2)}, u32[]{:S(2)}) collective-permute-start(f32[8,128]{1,0:T(8,128)S(1)} %get-tuple-element.32), channel_id=1, source_target_pairs={{0,16},{4,20},{8,24},{12,28},{16,0},{20,4},{24,8},{28,12},{1,17},{... | collective-permute-start | bytes 12296 | tf_op jit(solution)/shard_map/ppermute | solution.py:615
  9.9 5.7 %sort.15 = (s32[8192]{0:T(1024)S(1)}, s32[8192]{0:T(1024)S(1)}) sort(s32[8192]{0:T(1024)S(1)} %bitcast.22, s32[8192]{0:T(1024)S(1)} %bitcast.23), dimensions={0}, to_apply=%region_0.0 | sort | flops 106496 | bytes 131072 | tf_op jit(solution)/shard_map/sort | solution.py:620
  15.5 0.0 collective-permute-done.3
  15.6 1.6 %collective-permute-start.4 = (f32[8,128]{1,0:T(8,128)S(1)}, f32[8,128]{1,0:T(8,128)S(1)}, u32[]{:S(2)}, u32[]{:S(2)}) collective-permute-start(f32[8,128]{1,0:T(8,128)S(1)} %add.23), channel_id=1, source_target_pairs={{0,8},{4,12},{8,0},{12,4},{16,24},{20,28},{24,16},{28,20},{1,9},{5... | collective-permute-start | bytes 12296 | tf_op jit(solution)/shard_map/ppermute | solution.py:615
  17.2 0.0 copy-start.1
  17.2 0.7 %copy-done.1 = s32[32]{0:T(128)S(1)} copy-done((s32[32]{0:T(128)S(1)}, s32[32]{0:T(128)}, u32[]{:S(2)}) %copy-start.1) | copy-done | bytes 152
  17.9 1.7 %route.1 = (s32[32,8,128]{2,1,0:T(8,128)}, s32[32,4,128]{2,1,0:T(4,128)S(1)}) custom-call(s32[32]{0:T(128)S(1)} %copy-done.1, s32[64,128]{1,0:T(8,128)S(1)} %bitcast.20, s32[64,128]{1,0:T(8,128)S(1)} %bitcast.21), custom_call_target="tpu_custom_call" | custom-call | tf_op jit(solution)/shard_map/route/pallas_call | solution.py:124
  19.6 0.0 collective-permute-done.4
  19.6 2.8 %all-to-all-start.1 = ((s32[32,8,128]{2,1,0:T(8,128)}), s32[32,8,128]{2,1,0:T(8,128)S(1)}, u32[]{:S(2)}, u32[]{:S(2)}) async-start(s32[32,8,128]{2,1,0:T(8,128)} %get-tuple-element.42), calls=%async_computation.1 | async-start | bytes 262144 | tf_op jit(solution)/shard_map/all_to_all | solution.py:633
  22.4 1.8 %collective-permute-start.5 = (f32[8,128]{1,0:T(8,128)S(1)}, f32[8,128]{1,0:T(8,128)S(1)}, u32[]{:S(2)}, u32[]{:S(2)}) collective-permute-start(f32[8,128]{1,0:T(8,128)S(1)} %add.24.refs_0_), channel_id=1, source_target_pairs={{0,4},{4,0},{8,12},{12,8},{16,20},{20,16},{24,28},{28,24},{1,5},{5... | collective-permute-start | bytes 12296 | tf_op jit(solution)/shard_map/ppermute | solution.py:615
  24.3 1.6 %pick.1 = (f32[32,4,128]{2,1,0:T(4,128)S(1)}, f32[16,4,16,256]{3,2,1,0:T(8,128)S(1)}) custom-call(f32[16,256]{1,0:T(8,128)S(1)} %get-tuple-element.26.temp_ref, f32[32,256]{1,0:T(8,128)S(1)} %bitcast.18, s32[32,4,128]{2,1,0:T(4,128)S(1)} %get-tuple-element.35.idx_ref), custom_call_target="tpu_custom_call" | custom-call | tf_op jit(solution)/shard_map/pick/pallas_call | solution.py:191
  25.9 0.2 collective-permute-done.5.refs_1_
  26.1 2.7 %clean.1 = (f32[16,32]{1,0:T(8,128)S(1)}, f32[32,4,128]{2,1,0:T(4,128)}) custom-call(f32[32,4,128]{2,1,0:T(4,128)S(1)} %get-tuple-element.36.raw_ref, f32[16,4,16,256]{3,2,1,0:T(8,128)S(1)} %get-tuple-element.37.there_ref, s32[32,4,128]{2,1,0:T(4,128)S(1)} %get-tuple-element.35.idx_ref, f32[8,128]{1,0:T(8,128)S(1)} %add.24.refs_0_, ...), custom_call_target="tpu_custom_call" | custom-call | tf_op jit(solution)/shard_map/clean/pallas_call | solution.py:242
  28.8 1.9 %all-to-all-done.1.got_ref = s32[32,8,128]{2,1,0:T(8,128)S(1)} async-done(((s32[32,8,128]{2,1,0:T(8,128)}), s32[32,8,128]{2,1,0:T(8,128)S(1)}, u32[]{:S(2)}, u32[]{:S(2)}) %all-to-all-start.1) | async-done | bytes 131104 | tf_op jit(solution)/shard_map/all_to_all | solution.py:633
  30.7 4.2 %all-to-all-start = ((f32[32,4,128]{2,1,0:T(4,128)}), f32[32,4,128]{2,1,0:T(4,128)S(1)}, u32[]{:S(2)}, u32[]{:S(2)}) async-start(f32[32,4,128]{2,1,0:T(4,128)} %get-tuple-element.41), calls=%async_computation | async-start | bytes 131072 | tf_op jit(solution)/shard_map/all_to_all | solution.py:638
  34.8 6.2 %angles.1 = (f32[3,4,8,4,128]{4,3,2,1,0:T(4,128)S(1)}, f32[5,152,256]{2,1,0:T(8,128)S(1)}) custom-call(s32[32,8,128]{2,1,0:T(8,128)S(1)} %all-to-all-done.1.got_ref), custom_call_target="tpu_custom_call" | custom-call | tf_op jit(solution)/shard_map/angles/pallas_call | solution.py:380
  41.0 1.0 %all-to-all-done.got_ref = f32[32,4,128]{2,1,0:T(4,128)S(1)} async-done(((f32[32,4,128]{2,1,0:T(4,128)}), f32[32,4,128]{2,1,0:T(4,128)S(1)}, u32[]{:S(2)}, u32[]{:S(2)}) %all-to-all-start) | async-done | bytes 65568 | tf_op jit(solution)/shard_map/all_to_all | solution.py:638
  42.1 7.5 %make_map.1 = (f32[3,152,256]{2,1,0:T(8,128)S(1)}, f32[32,4,128]{2,1,0:T(4,128)}) custom-call(f32[32,4,128]{2,1,0:T(4,128)S(1)} %all-to-all-done.got_ref, f32[3,4,8,4,128]{4,3,2,1,0:T(4,128)S(1)} %get-tuple-element.43.mixed_ref, f32[5,152,256]{2,1,0:T(8,128)S(1)} %get-tuple-element.44.acc_ref), custom_call_target="tpu_custom_call" | custom-call | tf_op jit(solution)/shard_map/make_map/pallas_call | solution.py:492
  49.6 4.8 %all-to-all-start.2 = ((f32[32,4,128]{2,1,0:T(4,128)}), f32[32,4,128]{2,1,0:T(4,128)S(1)}, u32[]{:S(2)}, u32[]{:S(2)}) async-start(f32[32,4,128]{2,1,0:T(4,128)} %get-tuple-element.46), calls=%async_computation.2 | async-start | bytes 131072 | tf_op jit(solution)/shard_map/all_to_all | solution.py:641
  54.5 2.8 %invert.1 = (s32[32,256]{1,0:T(8,128)S(1)}, f32[32,256]{1,0:T(8,128)S(1)}) custom-call(s32[32,4,128]{2,1,0:T(4,128)S(1)} %get-tuple-element.35.idx_ref, f32[16,32]{1,0:T(8,128)S(1)} %get-tuple-element.47.coef_ref, f32[16,256]{1,0:T(8,128)S(1)} %get-tuple-element.26.temp_ref, f32[32,256]{1,0:T(8,128)S(1)} %bitcast.19), custom_call_target="tpu_custom_call" | custom-call | tf_op jit(solution)/shard_map/invert/pallas_call | solution.py:551
  57.2 1.0 %lay_out.1 = f32[3,32640]{1,0:T(4,128)} custom-call(f32[3,152,256]{2,1,0:T(8,128)S(1)} %get-tuple-element.45.stokes_ref), custom_call_target="tpu_custom_call" | custom-call | tf_op jit(solution)/shard_map/lay_out/pallas_call | solution.py:150
  58.2 3.4 %all-to-all-done.2.got_ref = f32[32,4,128]{2,1,0:T(4,128)S(1)} async-done(((f32[32,4,128]{2,1,0:T(4,128)}), f32[32,4,128]{2,1,0:T(4,128)S(1)}, u32[]{:S(2)}, u32[]{:S(2)}) %all-to-all-start.2) | async-done | bytes 65568 | tf_op jit(solution)/shard_map/all_to_all | solution.py:641
  61.6 1.9 %residuals.1 = f32[32,256]{1,0:T(8,128)} custom-call(f32[32,4,128]{2,1,0:T(4,128)S(1)} %all-to-all-done.2.got_ref, s32[32,256]{1,0:T(8,128)S(1)} %get-tuple-element.48.slot_ref, f32[32,256]{1,0:T(8,128)S(1)} %get-tuple-element.49.clean_ref), custom_call_target="tpu_custom_call" | custom-call | tf_op jit(solution)/shard_map/residuals/pallas_call | solution.py:581
  (3 shorter events, 0.0 us)
Async XLA Ops:
  0.6 5.3 %copy-start.2 = (s32[1,32,256]{2,1,0:T(8,128)S(1)}, s32[1,32,256]{2,1,0:T(8,128)}, u32[]{:S(2)}) copy-start(s32[1,32,256]{2,1,0:T(8,128)} %param.8) | copy-start | bytes 98308
  0.6 5.3 %collective-permute-start = (f32[32,256]{1,0:T(8,128)}, f32[32,256]{1,0:T(8,128)S(1)}, u32[]{:S(2)}, u32[]{:S(2)}) collective-permute-start(f32[32,256]{1,0:T(8,128)} %bitcast.14), channel_id=1, source_target_pairs={{0,1},{1,2},{2,3},{3,0},{4,5},{5,6},{6,7},{7,4},{8,9},{9,10},{10,1... | collective-permute-start | bytes 98312 | tf_op jit(solution)/shard_map/ppermute | solution.py:602
  1.1 4.8 %collective-permute-start.1 = (f32[32,256]{1,0:T(8,128)}, f32[32,256]{1,0:T(8,128)S(1)}, u32[]{:S(2)}, u32[]{:S(2)}) collective-permute-start(f32[32,256]{1,0:T(8,128)} %bitcast.15), channel_id=1, source_target_pairs={{0,2},{1,3},{2,0},{3,1},{4,6},{5,7},{6,4},{7,5},{8,10},{9,11},{10,... | collective-permute-start | bytes 98312 | tf_op jit(solution)/shard_map/ppermute | solution.py:602
  3.7 3.3 %collective-permute-start.2 = (f32[32,256]{1,0:T(8,128)}, f32[32,256]{1,0:T(8,128)S(1)}, u32[]{:S(2)}, u32[]{:S(2)}) collective-permute-start(f32[32,256]{1,0:T(8,128)} %bitcast.16), channel_id=1, source_target_pairs={{0,3},{1,0},{2,1},{3,2},{4,7},{5,4},{6,5},{7,6},{8,11},{9,8},{10,9... | collective-permute-start | bytes 98312 | tf_op jit(solution)/shard_map/ppermute | solution.py:602
  5.9 1.1 %copy-start = (f32[1,32,256]{2,1,0:T(8,128)S(1)}, f32[1,32,256]{2,1,0:T(8,128)}, u32[]{:S(2)}) copy-start(f32[1,32,256]{2,1,0:T(8,128)} %param.5) | copy-start | bytes 98308
  7.3 8.3 %collective-permute-start.3 = (f32[8,128]{1,0:T(8,128)S(1)}, f32[8,128]{1,0:T(8,128)S(1)}, u32[]{:S(2)}, u32[]{:S(2)}) collective-permute-start(f32[8,128]{1,0:T(8,128)S(1)} %get-tuple-element.32), channel_id=1, source_target_pairs={{0,16},{4,20},{8,24},{12,28},{16,0},{20,4},{24,8},{28,12},{1,17},{... | collective-permute-start | bytes 12296 | tf_op jit(solution)/shard_map/ppermute | solution.py:615
  15.6 4.0 %collective-permute-start.4 = (f32[8,128]{1,0:T(8,128)S(1)}, f32[8,128]{1,0:T(8,128)S(1)}, u32[]{:S(2)}, u32[]{:S(2)}) collective-permute-start(f32[8,128]{1,0:T(8,128)S(1)} %add.23), channel_id=1, source_target_pairs={{0,8},{4,12},{8,0},{12,4},{16,24},{20,28},{24,16},{28,20},{1,9},{5... | collective-permute-start | bytes 12296 | tf_op jit(solution)/shard_map/ppermute | solution.py:615
  17.2 0.7 %copy-start.1 = (s32[32]{0:T(128)S(1)}, s32[32]{0:T(128)}, u32[]{:S(2)}) copy-start(s32[32]{0:T(128)} %owner_ref.1) | copy-start | bytes 388
  19.6 11.1 %all-to-all-start.1 = ((s32[32,8,128]{2,1,0:T(8,128)}), s32[32,8,128]{2,1,0:T(8,128)S(1)}, u32[]{:S(2)}, u32[]{:S(2)}) async-start(s32[32,8,128]{2,1,0:T(8,128)} %get-tuple-element.42), calls=%async_computation.1 | async-start | bytes 262144 | tf_op jit(solution)/shard_map/all_to_all | solution.py:633
  22.4 3.7 %collective-permute-start.5 = (f32[8,128]{1,0:T(8,128)S(1)}, f32[8,128]{1,0:T(8,128)S(1)}, u32[]{:S(2)}, u32[]{:S(2)}) collective-permute-start(f32[8,128]{1,0:T(8,128)S(1)} %add.24.refs_0_), channel_id=1, source_target_pairs={{0,4},{4,0},{8,12},{12,8},{16,20},{20,16},{24,28},{28,24},{1,5},{5... | collective-permute-start | bytes 12296 | tf_op jit(solution)/shard_map/ppermute | solution.py:615
  30.7 11.4 %all-to-all-start = ((f32[32,4,128]{2,1,0:T(4,128)}), f32[32,4,128]{2,1,0:T(4,128)S(1)}, u32[]{:S(2)}, u32[]{:S(2)}) async-start(f32[32,4,128]{2,1,0:T(4,128)} %get-tuple-element.41), calls=%async_computation | async-start | bytes 131072 | tf_op jit(solution)/shard_map/all_to_all | solution.py:638
  49.6 12.0 %all-to-all-start.2 = ((f32[32,4,128]{2,1,0:T(4,128)}), f32[32,4,128]{2,1,0:T(4,128)S(1)}, u32[]{:S(2)}, u32[]{:S(2)}) async-start(f32[32,4,128]{2,1,0:T(4,128)} %get-tuple-element.46), calls=%async_computation.2 | async-start | bytes 131072 | tf_op jit(solution)/shard_map/all_to_all | solution.py:641
